TPU v7x, 256 devices: a whole 4x4x8 slice. The times are simulated.
256 devices in a mesh: heads: 4 (over x), pages: 64 (over z, y, core).
Axes of the slice: x: 4, y: 4, z: 8, core: 2. Of those that a mesh axis runs over, the one named last changes fastest.
Arguments:
- queries: bfloat16 [4608, 16, 128], P('pages', 'heads'), may hold values from -60 to 60
- keys: bfloat16 [4608, 16, 128], P('pages', 'heads'), may hold values from -6 to 6
- values: bfloat16 [4608, 16, 128], P('pages', 'heads'), may hold values from -6 to 6
- key_cache: bfloat16 [768, 128, 16, 128], P('pages', None, 'heads'), may hold values from -6 to 6
- value_cache: bfloat16 [768, 128, 16, 128], P('pages', None, 'heads'), may hold values from -6 to 6
- cache_len: int32 [6], replicated, may hold values from 0 to 15616, as said below
- page_table: int32 [6, 122], replicated, may hold values from 0 to 767, as said below
- append_slots: int32 [6, 6], replicated, may hold values from 0 to 767
- out_weight: bfloat16 [2048, 4096], P('heads', 'pages'), may hold values from -0.125 to 0.125
- out_bias: float32 [4096], P('heads'), may hold values from -3 to 3
Outputs:
- hidden: bfloat16 [4608, 4096], P('pages', 'heads')
- key_cache_out: bfloat16 [768, 128, 16, 128], P('pages', None, 'heads')
- value_cache_out: bfloat16 [768, 128, 16, 128], P('pages', None, 'heads')
Inputs may be any that keep to these rules, and one draw needn't show every extreme that they name: Every entry of page_table and append_slots together is a different slot. `cache_len`: A multiple of 128; some request has exactly 15616.
All inputs are finite; a program needn't handle non-finite values.
Results may differ from a plain program's by a relative error of at most 0.018.
Values may be sent and summed in bfloat16 or wider, within the bound.
A program may use at most 128 MiB of HBM per device.

v0:
```python
import math

import jax
import jax.numpy as jnp
from jax import lax
from jax.sharding import PartitionSpec as P

ROT = 32
PAGE = 128


low_score = -1e30


def rotate(vectors, positions):
    half_rot = ROT // 2
    inv_freq = 10000.0 ** (-2.0 * jnp.arange(half_rot, dtype=jnp.float32) / ROT)
    angles = positions[:, None] * inv_freq[None, :]
    cosine = jnp.cos(angles)[:, None, :]
    sine = jnp.sin(angles)[:, None, :]
    first_half = vectors[..., :half_rot]
    second_half = vectors[..., half_rot:ROT]
    return jnp.concatenate(
        [
            first_half * cosine - second_half * sine,
            second_half * cosine + first_half * sine,
            vectors[..., ROT:],
        ],
        axis=-1,
    )


def per_device(
    queries,
    keys,
    values,
    key_cache,
    value_cache,
    cache_len,
    page_table,
    append_slots,
    out_weight,
    out_bias,
):
    tok_dev, head_count, head_dim = queries.shape
    requests = cache_len.shape[0]
    max_pages = page_table.shape[1]
    new_pages = append_slots.shape[1]
    span_len = new_pages * PAGE
    slot_count = key_cache.shape[0]
    device_at = lax.axis_index("pages")
    token_ids = device_at * tok_dev + jnp.arange(tok_dev, dtype=jnp.int32)
    request_ids = token_ids // span_len
    request_grid = jnp.arange(requests, dtype=jnp.int32)
    starts = jnp.sum(
        jnp.where(request_ids[:, None] == request_grid[None, :], cache_len[None, :], 0), axis=1
    )
    positions = (starts + token_ids % span_len).astype(jnp.float32)
    rotated_q = rotate(queries.astype(jnp.float32), positions).astype(jnp.bfloat16)
    rotated_k = rotate(keys.astype(jnp.float32), positions).astype(jnp.bfloat16)
    all_q, all_k, all_v = (
        lax.all_gather(rotated_q, "pages", axis=0, tiled=True),
        lax.all_gather(rotated_k, "pages", axis=0, tiled=True),
        lax.all_gather(values, "pages", axis=0, tiled=True),
    )
    my_slots = device_at * slot_count + jnp.arange(slot_count, dtype=jnp.int32)
    cached_hit = page_table.reshape(-1)[None, :] == my_slots[:, None]
    fresh_hit = append_slots.reshape(-1)[None, :] == my_slots[:, None]
    is_cached = jnp.any(cached_hit, axis=1)
    is_fresh = jnp.any(fresh_hit, axis=1)
    cached_index = jnp.sum(
        jnp.where(cached_hit, jnp.arange(requests * max_pages, dtype=jnp.int32)[None, :], 0), axis=1
    )
    fresh_index = jnp.sum(
        jnp.where(fresh_hit, jnp.arange(requests * new_pages, dtype=jnp.int32)[None, :], 0), axis=1
    )
    slot_request = jnp.where(is_fresh, fresh_index // new_pages, cached_index // max_pages)
    slot_page = jnp.where(is_fresh, fresh_index % new_pages, cached_index % max_pages)
    slot_length = jnp.sum(
        jnp.where(slot_request[:, None] == request_grid[None, :], cache_len[None, :], 0), axis=1
    )
    page_shape = (requests * new_pages, PAGE, head_count, head_dim)
    key_out = jnp.where(
        is_fresh[:, None, None, None],
        jnp.take(all_k.reshape(page_shape), fresh_index, axis=0),
        key_cache,
    )
    value_out = jnp.where(
        is_fresh[:, None, None, None],
        jnp.take(all_v.reshape(page_shape), fresh_index, axis=0),
        value_cache,
    )
    query_blocks = all_q.reshape(requests, span_len, head_count, head_dim)
    score_scale = 1.0 / math.sqrt(head_dim)
    query_offsets = jnp.arange(span_len, dtype=jnp.int32)
    key_offsets = jnp.arange(PAGE, dtype=jnp.int32)

    def slot_scores(slot):
        request = slot_request[slot]
        query_block = lax.dynamic_index_in_dim(query_blocks, request, 0, keepdims=False)
        key_block = lax.dynamic_index_in_dim(key_out, slot, 0, keepdims=False)
        scores = (
            jnp.einsum("qhd,khd->hqk", query_block, key_block, preferred_element_type=jnp.float32)
            * score_scale
        )
        length = slot_length[slot]
        base_pos = slot_page[slot] * PAGE + key_offsets
        cached_ok = is_cached[slot] & (base_pos < length)
        fresh_ok = is_fresh[slot] & (base_pos[None, :] <= query_offsets[:, None])
        allowed = cached_ok[None, :] | fresh_ok
        return (jnp.where(allowed[None], scores, low_score), request, allowed)

    def over_slots(step, start):
        return lax.fori_loop(0, slot_count, step, start)

    def peak_step(slot, peaks):
        scores, request, allowed = slot_scores(slot)
        local_max = jnp.transpose(jnp.max(scores, axis=2))
        earlier = lax.dynamic_index_in_dim(peaks, request, 0, keepdims=False)
        return lax.dynamic_update_index_in_dim(peaks, jnp.maximum(earlier, local_max), request, 0)

    peaks = over_slots(
        peak_step, jnp.full((requests, span_len, head_count), low_score, jnp.float32)
    )
    peaks = lax.pmax(peaks.astype(jnp.bfloat16), "pages").astype(peaks.dtype)

    def weigh_step(slot, carry):
        weighted, totals = carry
        scores, request, allowed = slot_scores(slot)
        row_peak = jnp.transpose(lax.dynamic_index_in_dim(peaks, request, 0, keepdims=False))
        weights = jnp.exp(scores - row_peak[:, :, None])
        value_block = lax.dynamic_index_in_dim(value_out, slot, 0, keepdims=False)
        contrib = jnp.einsum(
            "hqk,khd->qhd",
            weights.astype(jnp.bfloat16),
            value_block,
            preferred_element_type=jnp.float32,
        )
        earlier = lax.dynamic_index_in_dim(weighted, request, 0, keepdims=False)
        weighted = lax.dynamic_update_index_in_dim(weighted, earlier + contrib, request, 0)
        row_sums = jnp.transpose(jnp.sum(weights, axis=2))
        earlier_sums = lax.dynamic_index_in_dim(totals, request, 0, keepdims=False)
        totals = lax.dynamic_update_index_in_dim(totals, earlier_sums + row_sums, request, 0)
        return (weighted, totals)

    start_sums = (
        jnp.zeros((requests, span_len, head_count, head_dim), jnp.float32),
        jnp.zeros((requests, span_len, head_count), jnp.float32),
    )
    weighted, totals = over_slots(weigh_step, start_sums)
    weighted, totals = (
        lax.psum_scatter(
            weighted.reshape(requests * span_len, head_count * head_dim),
            "pages",
            scatter_dimension=0,
            tiled=True,
        ),
        lax.psum_scatter(
            totals.reshape(requests * span_len, head_count),
            "pages",
            scatter_dimension=0,
            tiled=True,
        ),
    )
    attended = (
        (weighted.reshape(tok_dev, head_count, head_dim) / totals[:, :, None])
        .reshape(tok_dev, head_count * head_dim)
        .astype(jnp.bfloat16)
    )
    projected = jnp.dot(
        attended,
        lax.all_gather(out_weight, "pages", axis=1, tiled=True),
        preferred_element_type=jnp.float32,
    )
    summed = lax.psum_scatter(
        projected.astype(jnp.bfloat16), "heads", scatter_dimension=1, tiled=True
    ).astype(jnp.float32)
    hidden = (summed + out_bias[None, :]).astype(jnp.bfloat16)
    return (hidden, key_out, value_out)


def solution(mesh):
    placed = (
        P("pages", "heads", None),
        P("pages", "heads", None),
        P("pages", "heads", None),
        P("pages", None, "heads", None),
        P("pages", None, "heads", None),
        P(),
        P(),
        P(),
        P("heads", "pages"),
        P("heads"),
    )
    return jax.shard_map(
        per_device,
        mesh=mesh,
        in_specs=placed,
        out_specs=(
            P("pages", "heads"),
            P("pages", None, "heads", None),
            P("pages", None, "heads", None),
        ),
        check_vma=False,
    )
```

profile of v0, /device:TPU:4, one launch (start us, length us, event | category | flops | bytes accessed | tf_op | source)
XLA Modules:
  0.0 1255.7 jit_solution(8616648984599023867)
XLA Ops:
  14.0 79.9 %all-gather.9.cloned.1.call-done = bf16[4608,4,128]{2,0,1:T(8,128)(2,1)} async-done(((bf16[72,4,128]{2,0,1:T(8,128)(2,1)}), bf16[4608,4,128]{2,0,1:T(8,128)(2,1)}) %all-gather.9.cloned.1.call-update) | async-done | bytes 4718608 | tf_op jit(solution)/shard_map/all_gather | solution.py:63
  93.9 6.3 copy.77
  100.2 73.7 %all-gather.5.cloned.1.call-done = bf16[4608,4,128]{2,0,1:T(8,128)(2,1)} async-done(((bf16[72,4,128]{2,0,1:T(8,128)(2,1)}), bf16[4608,4,128]{2,0,1:T(8,128)(2,1)}) %all-gather.5.cloned.1.call-update) | async-done | bytes 4718608 | tf_op jit(solution)/shard_map/all_gather | solution.py:64
  174.0 6.4 copy.71
  180.4 3.2 gather_fusion.1
  183.6 3.2 gather_fusion
  186.8 67.2 %all-gather.7.cloned.1.call-done = bf16[4608,4,128]{2,0,1:T(8,128)(2,1)} async-done(((bf16[72,4,128]{2,0,1:T(8,128)(2,1)}), bf16[4608,4,128]{2,0,1:T(8,128)(2,1)}) %all-gather.7.cloned.1.call-update) | async-done | bytes 4718608 | tf_op jit(solution)/shard_map/all_gather | solution.py:62
  254.0 5.2 copy.81
  259.2 2.3 copy_select_fusion
  261.5 109.8 %while.30 = (s32[]{:T(128)}, bf16[6,768,4]{1,2,0:T(4,128)(2,1)S(1)}, s32[12]{0:T(128)S(1)}, pred[12]{0:T(512)(128)(4,1)S(1)}, s32[12]{0:T(128)S(1)}, /*index=5*/...) while((s32[]{:T(128)}, ...), condition=%wide.region_8.10_spmd.clone, body=%wide.region_6.9_spmd.clone.sunk | while | flops 102147592 | bytes 1153013 | solution.py:114
  269.0 1.6 select_reduce_fusion.4
  278.2 1.6 select_reduce_fusion.4
  287.3 1.6 select_reduce_fusion.4
  296.5 1.6 select_reduce_fusion.4
  305.7 1.6 select_reduce_fusion.4
  314.8 1.6 select_reduce_fusion.4
  324.0 1.6 select_reduce_fusion.4
  333.1 1.6 select_reduce_fusion.4
  342.3 1.6 select_reduce_fusion.4
  351.4 1.6 select_reduce_fusion.4
  360.6 1.6 select_reduce_fusion.4
  369.7 1.6 select_reduce_fusion.4
  371.4 248.4 %pmax.7 = bf16[6,768,4]{1,2,0:T(4,128)(2,1)S(1)} all-reduce(bf16[6,768,4]{1,2,0:T(4,128)(2,1)S(1)} %get-tuple-element.418), channel_id=1, replica_groups=mesh['heads'=4,'pages'=64] {'pages'}, use_global_device_ids=true, to_apply=%region_9.11 | all-reduce | flops 18432 | bytes 73728 | tf_op jit(solution)/shard_map/pmax | solution.py:125
  619.8 4.8 broadcast_in_dim.197.clone
  624.6 196.3 %while.31 = (s32[]{:T(128)}, f32[6,768,4,128]{3,2,1,0:T(4,128)}, f32[6,768,4]{1,2,0:T(4,128)S(1)}, s32[12]{0:T(128)S(1)}, bf16[12,128,4,128]{3,1,2,0:T(8,128)(2,...) while((s32[]{:T(128)}, f32[6,768,4,128]{3,2,1,0:T(4,128)}, ...), condition=%wide.region_12.14_spmd.clone, body=%wide.region_10.13_spmd.clone.sunk | while | flops 203981312 | bytes 18659864 | solution.py:114
  632.4 2.6 fusion.53
  635.0 1.5 constant_dynamic-slice_fusion.8
  637.3 1.6 fusion.54
  648.8 2.6 fusion.53
  651.4 1.5 constant_dynamic-slice_fusion.8
  653.7 1.6 fusion.54
  665.1 2.6 fusion.53
  667.8 1.5 constant_dynamic-slice_fusion.8
  670.0 1.6 fusion.54
  681.6 2.6 fusion.53
  684.2 1.5 constant_dynamic-slice_fusion.8
  686.4 1.6 fusion.54
  698.0 2.6 fusion.53
  700.6 1.5 constant_dynamic-slice_fusion.8
  702.8 1.6 fusion.54
  714.3 2.6 fusion.53
  719.1 1.6 fusion.54
  730.6 2.6 fusion.53
  735.4 1.6 fusion.54
  746.9 2.6 fusion.53
  751.8 1.6 fusion.54
  763.3 2.6 fusion.53
  768.1 1.6 fusion.54
  779.6 2.6 fusion.53
  784.5 1.6 fusion.54
  795.9 2.6 fusion.53
  798.6 1.5 constant_dynamic-slice_fusion.8
  800.8 1.6 fusion.54
  812.3 2.6 fusion.53
  817.1 1.6 fusion.54
  822.2 8.4 copy.105
  832.5 154.2 %all-reduce.4.cloned.1.call-done = f32[4608,4]{0,1:T(4,128)} async-done(((f32[4608,4]{0,1:T(4,128)}), f32[4608,4]{0,1:T(4,128)}) %all-reduce.4.cloned.1.call-update) | async-done | bytes 73744
  987.5 77.5 %all-gather.11.cloned.1.call-done = bf16[512,4096]{0,1:T(8,128)(2,1)} async-done(((bf16[512,64]{0,1:T(8,128)(2,1)}), bf16[512,4096]{0,1:T(8,128)(2,1)}) %all-gather.11.cloned.1.call-update) | async-done | bytes 4194320 | tf_op jit(solution)/shard_map/all_gather | solution.py:172
  1065.0 156.6 %reduce-scatter.8.cloned.1.call-done = f32[72,512]{1,0:T(8,128)} async-done(((f32[4608,512]{1,0:T(8,128)}), f32[72,512]{1,0:T(8,128)}) %reduce-scatter.8.cloned.1.call-update) | async-done | bytes 147472
  1221.7 4.5 convolution_convert_fusion
  1226.3 3.9 copy.85
  1230.2 2.4 copy.86
  1232.5 14.8 %reduce-scatter.6.cloned.1.call-done = bf16[72,1024]{1,0:T(8,128)(2,1)} async-done(((bf16[72,4096]{1,0:T(8,128)(2,1)}), bf16[72,1024]{1,0:T(8,128)(2,1)}) %reduce-scatter.6.cloned.1.call-update) | async-done | bytes 147472 | tf_op jit(solution)/shard_map/reduce_scatter | solution.py:175
  1247.3 1.6 add_convert_fusion
  (362 shorter events, 173.5 us)
Async XLA Ops:
  7.2 6.6 copy-start.9
  7.2 4.8 copy-start.4
  7.2 4.0 copy-start.5
  7.2 5.8 copy-start.7
  7.2 5.8 copy-start.8
  7.2 86.7 %all-gather.9.cloned.1.call-start = ((), (), s32[]{:S(2)}) async-start(), calls=%async_computation.4 | async-start | bytes 4792320 | tf_op jit(solution)/shard_map/all_gather | solution.py:63
  11.2 162.8 %all-gather.5.cloned.1.call-start = ((), (), s32[]{:S(2)}) async-start(), calls=%async_computation.2 | async-start | bytes 4792320 | tf_op jit(solution)/shard_map/all_gather | solution.py:64
  11.9 242.1 %all-gather.7.cloned.1.call-start = ((), (), s32[]{:S(2)}) async-start(), calls=%async_computation.3 | async-start | bytes 4792320 | tf_op jit(solution)/shard_map/all_gather | solution.py:62
  12.9 973.8 %all-reduce.4.cloned.1.call-start = ((), (), s32[]{:S(2)}) async-start(), calls=%async_computation.7 | async-start | bytes 147456
  254.0 5.2 copy-start.1
  254.0 5.2 copy-start.2
  820.9 0.6 copy-start.3
  821.5 243.4 %all-gather.11.cloned.1.call-start = ((), (), s32[]{:S(2)}) async-start(), calls=%async_computation.5 | async-start | bytes 4259840 | tf_op jit(solution)/shard_map/all_gather | solution.py:172
  822.1 399.5 %reduce-scatter.8.cloned.1.call-start = ((), (), s32[]{:S(2)}) async-start(), calls=%async_computation.8 | async-start | bytes 9584640
  830.6 0.7 copy-start.10
  830.6 416.7 %reduce-scatter.6.cloned.1.call-start = ((), (), s32[]{:S(2)}) async-start(), calls=%async_computation.6 | async-start | bytes 737280 | tf_op jit(solution)/shard_map/reduce_scatter | solution.py:175
  1226.2 3.9 copy-start
  1230.2 17.1 %copy-start.6 = (f32[1024]{0:T(1024)S(1)}, f32[1024]{0:T(1024)}, u32[]{:S(2)}) copy-start(f32[1024]{0:T(1024)} %param.25) | copy-start | bytes 12292
Sparse Core Ops, SparseCore 0:
  11.3 82.5 all-gather.8
  97.2 76.7 all-gather.4
  177.3 76.7 all-gather.6
  821.7 164.9 all-reduce.3
  989.3 75.6 all-gather.10
  1069.1 152.4 reduce-scatter.7
  1226.4 20.8 reduce-scatter.5
where the time goes:
time: 1260 us
  waiting for transfers between devices  625 us (50%)
  blocking collectives  248 us (20%)
  local copies, waits for them, and re-layouts  171 us (14%)
  matrix products  74.4 us (6%)
  loops' own time  63.8 us (5%)
  other arithmetic  58.4 us (5%)
  between operations  15 us (1%)
    unnamed x9, waiting for transfers between devices  311 us
    pmax x1, blocking collectives, per_device(): peaks = lax.pmax(peaks.astype(jnp.bfloat16), 'pages').astype(peaks.dtype)  248 us
    all_gather x1, waiting for transfers between devices, per_device(): lax.all_gather(rotated_k, 'pages', axis=0, tiled=True)  79.9 us
    all_gather x1, waiting for transfers between devices, per_device(): lax.all_gather(out_weight, 'pages', axis=1, tiled=True)  77.5 us
    all_gather x1, waiting for transfers between devices, per_device(): lax.all_gather(values, 'pages', axis=0, tiled=True)  73.7 us
    all_gather x1, waiting for transfers between devices, per_device(): lax.all_gather(rotated_q, 'pages', axis=0, tiled=True)  67.2 us
    another operation x2, loops' own time, over_slots(): return lax.fori_loop(0, slot_count, step, start)  63.8 us
    dot_general x24, matrix products, slot_scores(): jnp.einsum('qhd,khd->hqk', query_block, key_block, preferred_element_type...  50.4 us
  transfers between devices with their start and end apart: 7, of which 7 were waited for; matrix products, arithmetic and copies ran while one was open for 3% of the time, Pallas kernels for 0%

commit v1 on v0

v1 whole, which is shorter than its diff:
```python
import functools
import math

import jax
import jax.numpy as jnp
from jax import lax
from jax.experimental import pallas as pl
from jax.experimental.pallas import tpu as pltpu
from jax.sharding import PartitionSpec as P

ROT = 32
PAGE = 128


low_score = -1e30


def rotate(vectors, positions):
    half_rot = ROT // 2
    inv_freq = 10000.0 ** (-2.0 * jnp.arange(half_rot, dtype=jnp.float32) / ROT)
    angles = positions[:, None] * inv_freq[None, :]
    cosine = jnp.cos(angles)[:, None, :]
    sine = jnp.sin(angles)[:, None, :]
    first_half = vectors[..., :half_rot]
    second_half = vectors[..., half_rot:ROT]
    return jnp.concatenate(
        [
            first_half * cosine - second_half * sine,
            second_half * cosine + first_half * sine,
            vectors[..., ROT:],
        ],
        axis=-1,
    )


def attend_kernel(heads, head_dim, sreq_ref, skind_ref, slim_ref, q_ref, k_ref, v_ref, o_ref, ml_ref):
    step = pl.program_id(0)
    span = q_ref.shape[1]
    lanes = ml_ref.shape[2]

    @pl.when(step == 0)
    def _init():
        o_ref[...] = jnp.zeros_like(o_ref)
        lane = lax.broadcasted_iota(jnp.int32, ml_ref.shape, 2)
        ml_ref[...] = jnp.where(lane < heads, low_score, 0.0).astype(jnp.float32)

    request = sreq_ref[step]
    kind = skind_ref[step]
    limit = slim_ref[step]
    scale = 1.0 / math.sqrt(head_dim)

    @pl.when(kind != 0)
    def _work():
        rows = lax.broadcasted_iota(jnp.int32, (span, PAGE), 0)
        cols = lax.broadcasted_iota(jnp.int32, (span, PAGE), 1)
        allowed = rows - cols >= limit
        lane = lax.broadcasted_iota(jnp.int32, (span, lanes), 1)
        ml = ml_ref[request]
        for h in range(heads):
            cut = slice(h * head_dim, (h + 1) * head_dim)
            q_h = q_ref[request, :, cut]
            k_h = k_ref[0, :, cut]
            v_h = v_ref[0, :, cut]
            scores = lax.dot_general(
                q_h, k_h, (((1,), (1,)), ((), ())), preferred_element_type=jnp.float32
            ) * scale
            scores = jnp.where(allowed, scores, low_score)
            m_prev = ml[:, h : h + 1]
            l_prev = ml[:, heads + h : heads + h + 1]
            m_new = jnp.maximum(m_prev, jnp.max(scores, axis=1, keepdims=True))
            alpha = jnp.exp(m_prev - m_new)
            weights = jnp.where(allowed, jnp.exp(scores - m_new), 0.0)
            l_new = alpha * l_prev + jnp.sum(weights, axis=1, keepdims=True)
            contrib = jnp.dot(
                weights.astype(jnp.bfloat16), v_h, preferred_element_type=jnp.float32
            )
            o_ref[request, :, cut] = alpha * o_ref[request, :, cut] + contrib
            ml = jnp.where(lane == h, m_new, jnp.where(lane == heads + h, l_new, ml))
        ml_ref[request] = ml


def local_attention(slot_request, slot_kind, slot_limit, q_all, k_slots, v_slots, heads, head_dim):
    requests, span, width = q_all.shape
    slot_count = k_slots.shape[0]
    kernel = functools.partial(attend_kernel, heads, head_dim)
    flops = 4 * slot_count * span * PAGE * width
    return pl.pallas_call(
        kernel,
        out_shape=(
            jax.ShapeDtypeStruct((requests, span, width), jnp.float32),
            jax.ShapeDtypeStruct((requests, span, 128), jnp.float32),
        ),
        grid_spec=pltpu.PrefetchScalarGridSpec(
            num_scalar_prefetch=3,
            grid=(slot_count,),
            in_specs=[
                pl.BlockSpec((requests, span, width), lambda s, *_: (0, 0, 0)),
                pl.BlockSpec((1, PAGE, width), lambda s, *_: (s, 0, 0)),
                pl.BlockSpec((1, PAGE, width), lambda s, *_: (s, 0, 0)),
            ],
            out_specs=[
                pl.BlockSpec((requests, span, width), lambda s, *_: (0, 0, 0)),
                pl.BlockSpec((requests, span, 128), lambda s, *_: (0, 0, 0)),
            ],
        ),
        compiler_params=pltpu.CompilerParams(
            dimension_semantics=("arbitrary",), vmem_limit_bytes=60 * 1024 * 1024
        ),
        cost_estimate=pl.CostEstimate(
            flops=flops,
            transcendentals=slot_count * span * PAGE * heads,
            bytes_accessed=q_all.size * 2 + 2 * k_slots.size * 2 + requests * span * (width + 128) * 4,
        ),
    )(slot_request, slot_kind, slot_limit, q_all, k_slots, v_slots)


def per_device(
    queries,
    keys,
    values,
    key_cache,
    value_cache,
    cache_len,
    page_table,
    append_slots,
    out_weight,
    out_bias,
):
    tok_dev, head_count, head_dim = queries.shape
    width = head_count * head_dim
    requests = cache_len.shape[0]
    max_pages = page_table.shape[1]
    new_pages = append_slots.shape[1]
    span_len = new_pages * PAGE
    slot_count = key_cache.shape[0]
    page_devices = lax.axis_size("pages")
    device_at = lax.axis_index("pages")
    token_ids = device_at * tok_dev + jnp.arange(tok_dev, dtype=jnp.int32)
    request_ids = token_ids // span_len
    request_grid = jnp.arange(requests, dtype=jnp.int32)
    starts = jnp.sum(
        jnp.where(request_ids[:, None] == request_grid[None, :], cache_len[None, :], 0), axis=1
    )
    positions = (starts + token_ids % span_len).astype(jnp.float32)
    rotated_q = rotate(queries.astype(jnp.float32), positions).astype(jnp.bfloat16)
    rotated_k = rotate(keys.astype(jnp.float32), positions).astype(jnp.bfloat16)
    stacked = jnp.stack(
        [
            rotated_q.reshape(tok_dev, width),
            rotated_k.reshape(tok_dev, width),
            values.reshape(tok_dev, width),
        ]
    )
    gathered = lax.all_gather(stacked, "pages", axis=1, tiled=True)
    all_q = gathered[0].reshape(requests, span_len, width)
    page_shape = (requests * new_pages, PAGE, head_count, head_dim)
    all_k = gathered[1].reshape(page_shape)
    all_v = gathered[2].reshape(page_shape)
    my_slots = device_at * slot_count + jnp.arange(slot_count, dtype=jnp.int32)
    cached_hit = page_table.reshape(-1)[None, :] == my_slots[:, None]
    fresh_hit = append_slots.reshape(-1)[None, :] == my_slots[:, None]
    is_cached = jnp.any(cached_hit, axis=1)
    is_fresh = jnp.any(fresh_hit, axis=1)
    cached_index = jnp.sum(
        jnp.where(cached_hit, jnp.arange(requests * max_pages, dtype=jnp.int32)[None, :], 0), axis=1
    )
    fresh_index = jnp.sum(
        jnp.where(fresh_hit, jnp.arange(requests * new_pages, dtype=jnp.int32)[None, :], 0), axis=1
    )
    slot_request = jnp.where(is_fresh, fresh_index // new_pages, cached_index // max_pages)
    slot_page = jnp.where(is_fresh, fresh_index % new_pages, cached_index % max_pages)
    slot_length = jnp.sum(
        jnp.where(slot_request[:, None] == request_grid[None, :], cache_len[None, :], 0), axis=1
    )
    visible = is_fresh | (is_cached & (slot_page * PAGE < slot_length))
    slot_kind = visible.astype(jnp.int32)
    slot_limit = jnp.where(is_fresh, slot_page * PAGE, -4 * span_len)
    key_out = jnp.where(
        is_fresh[:, None, None, None],
        jnp.take(all_k, fresh_index, axis=0),
        key_cache,
    )
    value_out = jnp.where(
        is_fresh[:, None, None, None],
        jnp.take(all_v, fresh_index, axis=0),
        value_cache,
    )
    o_loc, ml = local_attention(
        slot_request,
        slot_kind,
        slot_limit,
        all_q,
        key_out.reshape(slot_count, PAGE, width),
        value_out.reshape(slot_count, PAGE, width),
        head_count,
        head_dim,
    )
    m_loc = ml[:, :, :head_count]
    l_loc = ml[:, :, head_count : 2 * head_count]
    m_all = lax.all_gather(m_loc.astype(jnp.bfloat16), "pages", axis=0, tiled=False)
    peak = jnp.max(m_all, axis=0).astype(jnp.float32)
    factor = jnp.exp(m_loc - peak)
    o_scaled = o_loc.reshape(requests, span_len, head_count, head_dim) * factor[..., None]
    l_scaled = l_loc * factor
    extra = 8
    l_rows = jnp.pad(
        l_scaled.reshape(page_devices, tok_dev * head_count),
        ((0, 0), (0, extra * width - tok_dev * head_count)),
    ).reshape(page_devices, extra, width)
    packed = jnp.concatenate(
        [o_scaled.reshape(page_devices, tok_dev, width), l_rows], axis=1
    ).reshape(page_devices * (tok_dev + extra), width)
    mine = lax.psum_scatter(packed, "pages", scatter_dimension=0, tiled=True)
    weighted = mine[:tok_dev].reshape(tok_dev, head_count, head_dim)
    totals = mine[tok_dev:].reshape(-1)[: tok_dev * head_count].reshape(tok_dev, head_count)
    attended = (weighted / totals[:, :, None]).reshape(tok_dev, width).astype(jnp.bfloat16)
    projected = jnp.dot(
        attended,
        lax.all_gather(out_weight, "pages", axis=1, tiled=True),
        preferred_element_type=jnp.float32,
    )
    summed = lax.psum_scatter(
        projected.astype(jnp.bfloat16), "heads", scatter_dimension=1, tiled=True
    ).astype(jnp.float32)
    hidden = (summed + out_bias[None, :]).astype(jnp.bfloat16)
    return (hidden, key_out, value_out)


def solution(mesh):
    placed = (
        P("pages", "heads", None),
        P("pages", "heads", None),
        P("pages", "heads", None),
        P("pages", None, "heads", None),
        P("pages", None, "heads", None),
        P(),
        P(),
        P(),
        P("heads", "pages"),
        P("heads"),
    )
    return jax.shard_map(
        per_device,
        mesh=mesh,
        in_specs=placed,
        out_specs=(
            P("pages", "heads"),
            P("pages", None, "heads", None),
            P("pages", None, "heads", None),
        ),
        check_vma=False,
    )
```

time: 1260 us -> 602 us (0.48)
  blocking collectives: 248 us -> 0 us
  waiting for transfers between devices: 625 us -> 421 us
  local copies, waits for them, and re-layouts: 171 us -> 80.6 us
  matrix products: 74.4 us -> 4.59 us
  loops' own time: 63.8 us -> 0 us
  Pallas kernels: 0 us -> 39.5 us
  other arithmetic: 58.4 us -> 38.5 us
    unnamed x9 -> x5, waiting for transfers between devices: 311 us -> 0.59 us
    pmax x1 -> x0, blocking collectives: 248 us -> none  [per_device(): peaks = lax.pmax(peaks.astype(jnp.bfloat16), 'pages').astype(peaks.dtype)]
    reduce_scatter x0 -> x1, waiting for transfers between devices: none -> 153 us  [per_device(): mine = lax.psum_scatter(packed, 'pages', scatter_dimension=0, tiled=True)]
    dynamic_slice x168 -> x0, local copies, waits for them, and re-layouts: 97.7 us -> none  [the longest x24 26.4 us: weigh_step(): earlier = lax.dynamic_index_in_dim(weighted, request, 0, keepdims=False)]
    dot_general x36 -> x0, matrix products: 69.9 us -> none  [the longest x24 50.4 us: slot_scores(): jnp.einsum('qhd,khd->hqk', query_block, key_block, preferred_element_type...]
    another operation x2 -> x0, loops' own time: 63.8 us -> none  [over_slots(): return lax.fori_loop(0, slot_count, step, start)]
    all_gather x3 -> x2, waiting for transfers between devices: 221 us -> 173 us  [the longest x1 94.2 us: per_device(): gathered = lax.all_gather(stacked, 'pages', axis=1, tiled=True)]
    pallas_call x0 -> x1, Pallas kernels: none -> 39.5 us  [local_attention(): pl.pallas_call(kernel, out_shape=(jax.ShapeDtypeStruct((requests, span, w...]
  transfers between devices with their start and end apart: 7 -> 5, of which waited for: 7 -> 5; matrix products, arithmetic and copies ran while one was open for 3% -> 1% of each run, Pallas kernels for 0% -> 0%
where the time goes in v1:
time: 602 us; the launch traced here: 599 us
  waiting for transfers between devices  421 us (70%)
  local copies, waits for them, and re-layouts  80.6 us (13%)
  Pallas kernels  39.5 us (7%)
  other arithmetic  38.5 us (6%)
  between operations  14 us (2%)
    reduce_scatter x1, waiting for transfers between devices, per_device(): mine = lax.psum_scatter(packed, 'pages', scatter_dimension=0, tiled=True)  153 us
    all_gather x1, waiting for transfers between devices, per_device(): gathered = lax.all_gather(stacked, 'pages', axis=1, tiled=True)  94.2 us
    all_gather x1, waiting for transfers between devices, per_device(): lax.all_gather(out_weight, 'pages', axis=1, tiled=True)  79 us
    all_gather x1, waiting for transfers between devices, per_device(): lax.all_gather(m_loc.astype(jnp.bfloat16), 'pages', axis=0, tiled=False)  78.8 us
    pallas_call x1, Pallas kernels, local_attention(): pl.pallas_call(kernel, out_shape=(jax.ShapeDtypeStruct((requests, span, w...  39.5 us
    mul x2, local copies, waits for them, and re-layouts, per_device(): o_loc.reshape(requests, span_len, head_count, head_dim) * factor[..., None]  19 us
    reduce_scatter x1, waiting for transfers between devices, per_device(): lax.psum_scatter(projected.astype(jnp.bfloat16), 'heads', scatter_dimensi...  15.4 us
    another operation x2, local copies, waits for them, and re-layouts, per_device(): all_v = gathered[2].reshape(page_shape)  13.6 us
  transfers between devices with their start and end apart: 5, of which 5 were waited for; matrix products, arithmetic and copies ran while one was open for 1% of the time, Pallas kernels for 0%

profile of v1, /device:TPU:4, one launch (start us, length us, event | category | flops | bytes accessed | tf_op | source)
XLA Modules:
  0.0 598.9 jit_solution(13993528027276793035)
XLA Ops:
  7.2 0.0 copy-start.11
  7.2 0.0 all-gather.5.cloned.1.call-start
  7.3 0.9 convert_element_type.59
  8.2 1.0 slice.49
  9.2 0.9 convert_element_type.62
  10.1 1.0 slice.52
  11.1 0.7 select_reduce_fusion
  11.9 0.2 multiply_cosine_fusion
  12.1 0.3 subtract_convert_fusion.1
  12.4 0.3 pad_maximum_fusion.2
  12.9 0.7 pad_maximum_fusion.1
  13.6 0.0 all-gather.5.cloned.1.call-update
  13.6 0.0 all-gather.9.cloned.1.call-start
  13.7 0.1 eq.61
  13.7 0.1 eq.65
  13.8 0.2 compare_reduce_fusion.1
  14.0 0.2 fusion.3
  14.2 0.2 fusion.2
  14.4 0.5 broadcast_select_fusion
  14.9 0.1 select_reduce_fusion.1
  15.0 0.2 compare_reduce_fusion
  15.2 0.6 or_convert_fusion.skind_ref
  15.8 94.2 %all-gather.5.cloned.1.call-done = bf16[3,4608,512]{2,1,0:T(8,128)(2,1)} async-done(((bf16[3,72,512]{2,1,0:T(8,128)(2,1)}), bf16[3,4608,512]{2,1,0:T(8,128)(2,1)}) %all-gather.5.cloned.1.call-update) | async-done | bytes 14155792 | tf_op jit(solution)/shard_map/all_gather | solution.py:154
  110.0 10.7 %fusion.11 = (bf16[1,4608,512]{2,1,0:T(8,128)(2,1)}, bf16[1,4608,512]{2,1,0:T(8,128)(2,1)}, bf16[1,4608,512]{2,1,0:T(8,128)(2,1)}) fusion(bf16[3,4608,512]{2,1,0:T(8,128)(2,1)} %all-gather.5.cloned.1.call-done), kind=kLoop, calls=%fused_computation.53 | loop fusion | bytes 28311552 | tf_op jit(solution)/shard_map/slice | solution.py:158
  120.8 7.7 %reshape_squeeze.10 = bf16[36,128,4,128]{3,2,1,0:T(4,128)(2,1)} reshape(bf16[1,4608,512]{2,1,0:T(8,128)(2,1)} %get-tuple-element.28) | data formatting | bytes 9437184 | tf_op jit(solution)/shard_map/reshape;squeeze | solution.py:157
  128.5 5.8 copy.46
  134.3 7.7 %reshape_squeeze.11 = bf16[36,128,4,128]{3,2,1,0:T(4,128)(2,1)} reshape(bf16[1,4608,512]{2,1,0:T(8,128)(2,1)} %get-tuple-element.27) | data formatting | bytes 9437184 | tf_op jit(solution)/shard_map/reshape;squeeze | solution.py:158
  142.0 5.9 copy.49
  147.9 3.2 gather_fusion
  151.1 3.2 gather_fusion.1
  154.3 2.5 copy_select_fusion
  156.8 1.6 copy_bitcast_fusion.v_ref
  158.3 1.4 copy_bitcast_fusion.1.k_ref
  159.7 39.5 %shard_map.121 = (f32[6,768,512]{2,1,0:T(8,128)}, f32[6,768,128]{2,1,0:T(8,128)}) custom-call(s32[12]{0:T(128)} %copy-done.10, s32[12]{0:T(128)} %or_convert_fusion.skind_ref, s32[12]{0:T(128)} %get-tuple-element.25.slim_ref, bf16[6,768,512]{2,1,0:T(8,128)(2,1)} %bitcast.27, bf16[12,128,512]{2,1,0:T(8,128)(2,1)} %copy_bitcast_fusion.1.k_ref, ...), custom_call_target="tpu_custom_call" | custom-call | flops 2415919104 | bytes 19660800 | tf_op jit(solution)/shard_map/pallas_call | solution.py:87
  199.1 1.8 slice.56
  201.0 1.0 copy.52
  202.0 0.0 all-gather.9.cloned.1.call-update
  202.0 0.2 reduce-scatter.3.cloned.1.call-start
  202.3 78.8 %all-gather.9.cloned.1.call-done = bf16[384,768,4]{1,2,0:T(4,128)(2,1)} async-done(((bf16[6,768,4]{1,2,0:T(4,128)(2,1)}), bf16[384,768,4]{1,2,0:T(4,128)(2,1)}) %all-gather.9.cloned.1.call-update) | async-done | bytes 2359312 | tf_op jit(solution)/shard_map/all_gather | solution.py:200
  281.1 2.8 reduce_max.9
  283.9 1.9 copy.53
  285.7 3.8 slice_multiply_fusion
  289.5 6.6 %mul.122 = f32[6,768,4,128]{3,2,1,0:T(4,128)} broadcast(f32[6,768,4]{2,1,0:T(8,128)S(1)} %get-tuple-element.24), dimensions={0,1,2} | broadcast | bytes 9510912 | tf_op jit(solution)/shard_map/mul | solution.py:203
  296.1 12.4 %mul.123 = f32[64,72,512]{2,1,0:T(8,128)} reshape(f32[6,768,4,128]{3,2,1,0:T(4,128)} %mul.122) | data formatting | bytes 18874368 | tf_op jit(solution)/shard_map/mul | solution.py:203
  308.5 0.7 reshape.170
  309.2 0.1 pad.4
  309.3 0.6 copy.58
  309.9 12.3 %mul.124 = f32[64,72,512]{2,1,0:T(8,128)} multiply(f32[64,72,512]{2,1,0:T(8,128)} %bitcast.26, f32[64,72,512]{2,1,0:T(8,128)} %mul.123) | non-fusion elementwise | flops 2359296 | bytes 28311552 | tf_op jit(solution)/shard_map/mul | solution.py:203
  322.2 9.5 %pad_maximum_fusion = f32[64,80,512]{2,1,0:T(8,128)} fusion(f32[64,8,512]{2,1,0:T(8,128)S(1)} %bitcast.28, f32[64,72,512]{2,1,0:T(8,128)} %mul.124), kind=kLoop, calls=%fused_computation.2 | loop fusion | flops 2621440 | bytes 20971520 | tf_op jit(solution)/shard_map/concatenate | solution.py:210
  331.7 0.0 reduce-scatter.3.cloned.1.call-update
  331.7 0.0 all-gather.7.cloned.1.call-start
  331.8 0.5 all-gather.7.cloned.1.call-update
  332.3 0.3 reduce-scatter.5.cloned.1.call-start
  332.6 153.0 %reduce-scatter.3.cloned.1.call-done = f32[80,512]{1,0:T(8,128)} async-done(((f32[5120,512]{1,0:T(8,128)}), f32[80,512]{1,0:T(8,128)}) %reduce-scatter.3.cloned.1.call-update) | async-done | bytes 163856 | tf_op jit(solution)/shard_map/reduce_scatter | solution.py:213
  485.6 0.7 slice.74
  486.3 0.5 slice.60
  486.9 79.0 %all-gather.7.cloned.1.call-done = bf16[512,4096]{0,1:T(8,128)(2,1)} async-done(((bf16[512,64]{0,1:T(8,128)(2,1)}), bf16[512,4096]{0,1:T(8,128)(2,1)}) %all-gather.7.cloned.1.call-update) | async-done | bytes 4194320 | tf_op jit(solution)/shard_map/all_gather | solution.py:219
  565.9 0.1 div.53
  566.0 4.6 convolution_convert_fusion
  570.6 0.0 reduce-scatter.5.cloned.1.call-update
  570.6 2.4 copy.48
  573.0 2.4 copy.51
  575.4 15.4 %reduce-scatter.5.cloned.1.call-done = bf16[72,1024]{1,0:T(8,128)(2,1)} async-done(((bf16[72,4096]{1,0:T(8,128)(2,1)}), bf16[72,1024]{1,0:T(8,128)(2,1)}) %reduce-scatter.5.cloned.1.call-update) | async-done | bytes 147472 | tf_op jit(solution)/shard_map/reduce_scatter | solution.py:222
  590.7 1.6 add_convert_fusion
  (33 shorter events, 0.2 us)
Async XLA Ops:
  7.2 7.8 %copy-start.11 = (s32[6]{0:T(128)S(1)}, s32[6]{0:T(128)}, u32[]{:S(2)}) copy-start(s32[6]{0:T(128)} %param.17) | copy-start | bytes 76
  7.2 5.6 copy-start.6
  7.2 6.5 %copy-start.8 = (s32[6,6]{1,0:T(8,128)S(1)}, s32[6,6]{1,0:T(8,128)}, u32[]{:S(2)}) copy-start(s32[6,6]{1,0:T(8,128)} %param.19) | copy-start | bytes 436
  7.2 6.5 %copy-start.9 = (s32[6,122]{1,0:T(8,128)S(1)}, s32[6,122]{1,0:T(8,128)}, u32[]{:S(2)}) copy-start(s32[6,122]{1,0:T(8,128)} %param.18) | copy-start | bytes 8788
  7.2 102.8 %all-gather.5.cloned.1.call-start = ((), (), s32[]{:S(2)}) async-start(), calls=%async_computation.2 | async-start | bytes 14376960 | tf_op jit(solution)/shard_map/all_gather | solution.py:154
  13.6 267.5 %all-gather.9.cloned.1.call-start = ((), (), s32[]{:S(2)}) async-start(), calls=%async_computation.6 | async-start | bytes 2396160 | tf_op jit(solution)/shard_map/all_gather | solution.py:200
  14.9 105.8 %copy-start.10 = (s32[12]{0:T(128)}, s32[12]{0:T(128)S(1)}, u32[]{:S(2)}) copy-start(s32[12]{0:T(128)S(1)} %get-tuple-element.36.sreq_ref) | copy-start | bytes 148
  156.7 2.9 copy-start.1
  156.7 2.9 copy-start.3
  202.0 283.6 %reduce-scatter.3.cloned.1.call-start = ((), (), s32[]{:S(2)}) async-start(), calls=%async_computation.3 | async-start | bytes 10649600 | tf_op jit(solution)/shard_map/reduce_scatter | solution.py:213
  281.1 4.7 copy-start
  296.1 12.4 %copy-start.5 = (f32[6,768,4]{2,1,0:T(8,128)S(1)}, f32[6,768,4]{2,1,0:T(8,128)}, u32[]{:S(2)}) copy-start(f32[6,768,4]{2,1,0:T(8,128)} %get-tuple-element.23) | copy-start | bytes 221188
  331.7 234.1 %all-gather.7.cloned.1.call-start = ((), (), s32[]{:S(2)}) async-start(), calls=%async_computation.4 | async-start | bytes 4259840 | tf_op jit(solution)/shard_map/all_gather | solution.py:219
  332.3 258.4 %reduce-scatter.5.cloned.1.call-start = ((), (), s32[]{:S(2)}) async-start(), calls=%async_computation.5 | async-start | bytes 737280 | tf_op jit(solution)/shard_map/reduce_scatter | solution.py:222
  566.0 4.6 copy-start.4
  570.6 2.4 copy-start.2
  573.0 17.7 %copy-start.7 = (f32[1024]{0:T(1024)S(1)}, f32[1024]{0:T(1024)}, u32[]{:S(2)}) copy-start(f32[1024]{0:T(1024)} %param.21) | copy-start | bytes 12292
Sparse Core Ops, SparseCore 0:
  13.7 96.2 all-gather.4
  202.1 78.8 all-gather.8
  331.8 153.7 reduce-scatter.2
  488.6 77.2 all-gather.6
  570.7 19.9 reduce-scatter.4

commit v2 on v1

v2 whole, which is shorter than its diff:
```python
import functools
import math

import jax
import jax.numpy as jnp
from jax import lax
from jax.experimental import pallas as pl
from jax.experimental.pallas import tpu as pltpu
from jax.sharding import PartitionSpec as P

ROT = 32
PAGE = 128


low_score = -1e30
mask_score = -(2.0 ** 100)


def rotate(vectors, positions):
    half_rot = ROT // 2
    inv_freq = 10000.0 ** (-2.0 * jnp.arange(half_rot, dtype=jnp.float32) / ROT)
    angles = positions[:, None] * inv_freq[None, :]
    cosine = jnp.cos(angles)[:, None, :]
    sine = jnp.sin(angles)[:, None, :]
    first_half = vectors[..., :half_rot]
    second_half = vectors[..., half_rot:ROT]
    return jnp.concatenate(
        [
            first_half * cosine - second_half * sine,
            second_half * cosine + first_half * sine,
            vectors[..., ROT:],
        ],
        axis=-1,
    )


def attend_kernel(
    heads, head_dim, requests, span,
    sreq_ref, skind_ref, slim_ref, sfresh_ref,
    q_ref, kf_ref, vf_ref, kc_ref, vc_ref,
    out_ref, acc_ref, ml_ref,
):
    step = pl.program_id(0)
    lanes = ml_ref.shape[1]
    width = heads * head_dim

    @pl.when(step == 0)
    def _init():
        acc_ref[...] = jnp.zeros_like(acc_ref)
        lane = lax.broadcasted_iota(jnp.int32, ml_ref.shape, 1)
        ml_ref[...] = jnp.where(lane < heads, mask_score, 0.0).astype(jnp.float32)

    request = sreq_ref[step]
    kind = skind_ref[step]
    limit = slim_ref[step]
    scale = 1.0 / math.sqrt(head_dim)

    def attend(k_ref, v_ref):
        base = pl.multiple_of(request * span, span)
        rows = lax.broadcasted_iota(jnp.int32, (span, PAGE), 0)
        cols = lax.broadcasted_iota(jnp.int32, (span, PAGE), 1)
        allowed = rows - cols >= limit
        lane = lax.broadcasted_iota(jnp.int32, (span, lanes), 1)
        ml = ml_ref[pl.ds(base, span), :]
        for h in range(heads):
            cut = slice(h * head_dim, (h + 1) * head_dim)
            q_h = q_ref[0, pl.ds(base, span), cut]
            k_h = k_ref[0, :, cut]
            v_h = v_ref[0, :, cut]
            scores = lax.dot_general(
                q_h, k_h, (((1,), (1,)), ((), ())), preferred_element_type=jnp.float32
            ) * scale
            scores = jnp.where(allowed, scores, mask_score)
            m_prev = ml[:, h : h + 1]
            l_prev = ml[:, heads + h : heads + h + 1]
            m_new = jnp.maximum(m_prev, jnp.max(scores, axis=1, keepdims=True))
            m_new = m_new.astype(jnp.bfloat16).astype(jnp.float32)
            alpha = jnp.exp(m_prev - m_new)
            weights = jnp.where(allowed, jnp.exp(scores - m_new), 0.0)
            l_new = alpha * l_prev + jnp.sum(weights, axis=1, keepdims=True)
            contrib = jnp.dot(
                weights.astype(jnp.bfloat16), v_h, preferred_element_type=jnp.float32
            )
            acc_ref[pl.ds(base, span), cut] = alpha * acc_ref[pl.ds(base, span), cut] + contrib
            ml = jnp.where(
                lane == h,
                m_new,
                jnp.where((lane == heads + h) | (lane == 2 * heads + h), l_new, ml),
            )
        ml_ref[pl.ds(base, span), :] = ml

    @pl.when(kind == 1)
    def _cached():
        attend(kc_ref, vc_ref)

    @pl.when(kind == 2)
    def _fresh():
        attend(kf_ref, vf_ref)

    @pl.when(step == pl.num_programs(0) - 1)
    def _emit():
        chunks, rows_per, _ = out_ref.shape
        lane = lax.broadcasted_iota(jnp.int32, (rows_per, lanes), 1)
        for d in range(chunks):
            rows = pl.ds(d * rows_per, rows_per)
            out_ref[d, :, :width] = acc_ref[rows, :].astype(jnp.bfloat16)
            ml = ml_ref[rows, :]
            rounded = ml.astype(jnp.bfloat16).astype(jnp.float32)
            packed = jnp.where(
                lane < 2 * heads,
                rounded,
                jnp.where(lane < 3 * heads, ml - rounded, 0.0),
            )
            out_ref[d, :, width:] = packed.astype(jnp.bfloat16)


def local_attention(slot_request, slot_kind, slot_limit, slot_fresh, gathered, kc, vc,
                    heads, head_dim, requests, span, chunks):
    _, tokens, width = gathered.shape
    slot_count = kc.shape[0]
    rows_per = tokens // chunks
    kernel = functools.partial(attend_kernel, heads, head_dim, requests, span)
    flops = 4 * slot_count * span * PAGE * width
    return pl.pallas_call(
        kernel,
        out_shape=jax.ShapeDtypeStruct((chunks, rows_per, width + 128), jnp.bfloat16),
        grid_spec=pltpu.PrefetchScalarGridSpec(
            num_scalar_prefetch=4,
            grid=(slot_count,),
            in_specs=[
                pl.BlockSpec((1, tokens, width), lambda s, *_: (0, 0, 0),
                             pipeline_mode=pl.Buffered(1)),
                pl.BlockSpec((1, PAGE, width), lambda s, rq, kd, lm, fr: (1, fr[s], 0)),
                pl.BlockSpec((1, PAGE, width), lambda s, rq, kd, lm, fr: (2, fr[s], 0)),
                pl.BlockSpec((1, PAGE, width), lambda s, *_: (s, 0, 0)),
                pl.BlockSpec((1, PAGE, width), lambda s, *_: (s, 0, 0)),
            ],
            out_specs=pl.BlockSpec((chunks, rows_per, width + 128), lambda s, *_: (0, 0, 0)),
            scratch_shapes=[
                pltpu.VMEM((tokens, width), jnp.float32),
                pltpu.VMEM((tokens, 128), jnp.float32),
            ],
        ),
        compiler_params=pltpu.CompilerParams(
            dimension_semantics=("arbitrary",), vmem_limit_bytes=60 * 1024 * 1024
        ),
        cost_estimate=pl.CostEstimate(
            flops=flops,
            transcendentals=slot_count * span * PAGE * heads,
            bytes_accessed=tokens * width * 2 + 4 * kc.size * 2 + tokens * (width + 128) * 2,
        ),
    )(slot_request, slot_kind, slot_limit, slot_fresh, gathered, gathered, gathered, kc, vc)


def per_device(
    queries,
    keys,
    values,
    key_cache,
    value_cache,
    cache_len,
    page_table,
    append_slots,
    out_weight,
    out_bias,
):
    tok_dev, head_count, head_dim = queries.shape
    width = head_count * head_dim
    requests = cache_len.shape[0]
    max_pages = page_table.shape[1]
    new_pages = append_slots.shape[1]
    span_len = new_pages * PAGE
    slot_count = key_cache.shape[0]
    page_devices = lax.axis_size("pages")
    device_at = lax.axis_index("pages")
    token_ids = device_at * tok_dev + jnp.arange(tok_dev, dtype=jnp.int32)
    request_ids = token_ids // span_len
    request_grid = jnp.arange(requests, dtype=jnp.int32)
    starts = jnp.sum(
        jnp.where(request_ids[:, None] == request_grid[None, :], cache_len[None, :], 0), axis=1
    )
    positions = (starts + token_ids % span_len).astype(jnp.float32)
    rotated_q = rotate(queries.astype(jnp.float32), positions).astype(jnp.bfloat16)
    rotated_k = rotate(keys.astype(jnp.float32), positions).astype(jnp.bfloat16)
    w_cols = out_weight.shape[1]
    w_plane = jnp.pad(out_weight.T, ((0, tok_dev - w_cols), (0, 0)))
    stacked = jnp.stack(
        [
            rotated_q.reshape(tok_dev, width),
            rotated_k.reshape(tok_dev, width),
            values.reshape(tok_dev, width),
            w_plane,
        ]
    )
    gathered = lax.all_gather(stacked, "pages", axis=1, tiled=True)
    my_slots = device_at * slot_count + jnp.arange(slot_count, dtype=jnp.int32)
    cached_hit = page_table.reshape(-1)[None, :] == my_slots[:, None]
    fresh_hit = append_slots.reshape(-1)[None, :] == my_slots[:, None]
    is_cached = jnp.any(cached_hit, axis=1)
    is_fresh = jnp.any(fresh_hit, axis=1)
    cached_index = jnp.sum(
        jnp.where(cached_hit, jnp.arange(requests * max_pages, dtype=jnp.int32)[None, :], 0), axis=1
    )
    fresh_index = jnp.sum(
        jnp.where(fresh_hit, jnp.arange(requests * new_pages, dtype=jnp.int32)[None, :], 0), axis=1
    )
    slot_request = jnp.where(is_fresh, fresh_index // new_pages, cached_index // max_pages)
    slot_page = jnp.where(is_fresh, fresh_index % new_pages, cached_index % max_pages)
    slot_length = jnp.sum(
        jnp.where(slot_request[:, None] == request_grid[None, :], cache_len[None, :], 0), axis=1
    )
    visible = is_cached & (slot_page * PAGE < slot_length)
    slot_kind = jnp.where(is_fresh, 2, jnp.where(visible, 1, 0)).astype(jnp.int32)
    slot_limit = jnp.where(is_fresh, slot_page * PAGE, -4 * span_len)
    page_pool = (requests * new_pages, PAGE, width)
    fresh_k = jnp.take(gathered[1].reshape(page_pool), fresh_index, axis=0)
    fresh_v = jnp.take(gathered[2].reshape(page_pool), fresh_index, axis=0)
    cache_shape = key_cache.shape
    key_out = jnp.where(is_fresh[:, None, None, None], fresh_k.reshape(cache_shape), key_cache)
    value_out = jnp.where(is_fresh[:, None, None, None], fresh_v.reshape(cache_shape), value_cache)
    packed = local_attention(
        slot_request,
        slot_kind,
        slot_limit,
        fresh_index,
        gathered,
        key_cache.reshape(slot_count, PAGE, width),
        value_cache.reshape(slot_count, PAGE, width),
        head_count,
        head_dim,
        requests,
        span_len,
        page_devices,
    )
    received = lax.all_to_all(packed, "pages", 0, 0, tiled=True).astype(jnp.float32)
    part_o = received[:, :, :width].reshape(page_devices, tok_dev, head_count, head_dim)
    part_m = received[:, :, width : width + head_count]
    part_l = (
        received[:, :, width + head_count : width + 2 * head_count]
        + received[:, :, width + 2 * head_count : width + 3 * head_count]
    )
    peak = jnp.max(part_m, axis=0)
    factor = jnp.exp(part_m - peak[None])
    weighted = jnp.sum(part_o * factor[..., None], axis=0)
    totals = jnp.sum(part_l * factor, axis=0)
    attended = (weighted / totals[:, :, None]).reshape(tok_dev, width).astype(jnp.bfloat16)
    projected = lax.dot_general(
        attended, gathered[3], (((1,), (1,)), ((), ())), preferred_element_type=jnp.float32
    )
    projected = projected.reshape(tok_dev, page_devices, tok_dev)[:, :, :w_cols].reshape(
        tok_dev, page_devices * w_cols
    )
    summed = lax.psum_scatter(
        projected.astype(jnp.bfloat16), "heads", scatter_dimension=1, tiled=True
    ).astype(jnp.float32)
    hidden = (summed + out_bias[None, :]).astype(jnp.bfloat16)
    return (hidden, key_out, value_out)


def solution(mesh):
    placed = (
        P("pages", "heads", None),
        P("pages", "heads", None),
        P("pages", "heads", None),
        P("pages", None, "heads", None),
        P("pages", None, "heads", None),
        P(),
        P(),
        P(),
        P("heads", "pages"),
        P("heads"),
    )
    return jax.shard_map(
        per_device,
        mesh=mesh,
        in_specs=placed,
        out_specs=(
            P("pages", "heads"),
            P("pages", None, "heads", None),
            P("pages", None, "heads", None),
        ),
        check_vma=False,
    )
```

time: 602 us -> 377 us (0.63)
  waiting for transfers between devices: 421 us -> 224 us
  local copies, waits for them, and re-layouts: 80.6 us -> 57.6 us
  other arithmetic: 38.5 us -> 30.5 us
    all_gather x2 -> x0, waiting for transfers between devices: 158 us -> none  [the longest x1 79 us: per_device(): lax.all_gather(out_weight, 'pages', axis=1, tiled=True)]
    reduce_scatter x1 -> x0, waiting for transfers between devices: 153 us -> none  [per_device(): mine = lax.psum_scatter(packed, 'pages', scatter_dimension=0, tiled=True)]
    all_to_all x0 -> x1, waiting for transfers between devices: none -> 122 us  [per_device(): lax.all_to_all(packed, 'pages', 0, 0, tiled=True).astype(jnp.float32)]
    another operation x4 -> x0, local copies, waits for them, and re-layouts: 27.1 us -> none  [the longest x2 13.6 us: per_device(): all_v = gathered[2].reshape(page_shape)]
    mul x2 -> x0, other arithmetic: 16.1 us -> none  [the longest x1 12.3 us: per_device(): o_loc.reshape(requests, span_len, head_count, head_dim) * factor[..., None]]
    reduce_scatter x1, waiting for transfers between devices: 15.4 us -> 0.01 us  [per_device(): lax.psum_scatter(projected.astype(jnp.bfloat16), 'heads', scatter_dimensi...]
    reduce_sum x0 -> x2, other arithmetic: none -> 9.73 us  [the longest x1 8.44 us: per_device(): weighted = jnp.sum(part_o * factor[..., None], axis=0)]
    concatenate x1 -> x0, other arithmetic: 9.46 us -> none  [per_device(): jnp.concatenate([o_scaled.reshape(page_devices, tok_dev, width), l_rows],...]
  transfers between devices with their start and end apart: 5 -> 3, of which waited for: 5 -> 2; matrix products, arithmetic and copies ran while one was open for 1% -> 11% of each run, Pallas kernels for 0% -> 0%
where the time goes in v2:
time: 377 us; the launch traced here: 376 us
  waiting for transfers between devices  224 us (59%)
  local copies, waits for them, and re-layouts  57.6 us (15%)
  Pallas kernels  39.9 us (11%)
  other arithmetic  30.5 us (8%)
  between operations  14.3 us (4%)
  starting transfers between devices  5.96 us (2%)
    all_to_all x1, waiting for transfers between devices, per_device(): lax.all_to_all(packed, 'pages', 0, 0, tiled=True).astype(jnp.float32)  122 us
    all_gather x1, waiting for transfers between devices, per_device(): gathered = lax.all_gather(stacked, 'pages', axis=1, tiled=True)  102 us
    pallas_call x1, Pallas kernels, local_attention(): pl.pallas_call(kernel, out_shape=jax.ShapeDtypeStruct((chunks, rows_per,...  39.9 us
    mul x2, local copies, waits for them, and re-layouts, per_device(): weighted = jnp.sum(part_o * factor[..., None], axis=0)  18.7 us
    slice x1, local copies, waits for them, and re-layouts, per_device(): fresh_v = jnp.take(gathered[2].reshape(page_pool), fresh_index, axis=0)  10.9 us
    reduce_sum x1, other arithmetic, per_device(): weighted = jnp.sum(part_o * factor[..., None], axis=0)  8.44 us
  transfers between devices with their start and end apart: 3, of which 2 were waited for; matrix products, arithmetic and copies ran while one was open for 11% of the time, Pallas kernels for 0%

profile of v2, /device:TPU:4, one launch (start us, length us, event | category | flops | bytes accessed | tf_op | source)
XLA Modules:
  0.0 375.6 jit_solution(4785316611983052784)
XLA Ops:
  7.2 0.0 copy-start.4
  7.2 0.0 copy-start.3
  7.2 0.0 copy-start.6
  7.2 0.0 copy-start.7
  7.2 0.0 copy-start.1
  7.2 0.0 all-gather.2.cloned.1.call-start
  7.3 1.0 convert_element_type.62
  8.3 1.0 slice.47
  9.3 0.9 convert_element_type.65
  10.2 1.0 slice.50
  11.2 0.7 select_reduce_fusion
  12.0 0.2 multiply_cosine_fusion
  12.2 0.3 subtract_convert_fusion.1
  12.5 0.3 pad_maximum_fusion.1
  12.8 0.0 copy-start.2
  12.9 0.0 copy-done.4
  13.0 0.0 copy-done.3
  13.0 0.8 pad_maximum_fusion
  13.8 0.0 all-gather.2.cloned.1.call-update
  13.8 0.0 copy-done.6
  13.8 0.1 eq.61
  13.9 0.0 copy-done.7
  13.9 0.1 eq.65
  14.0 0.0 copy-done.1
  14.0 2.0 reshape.175.kc_ref
  16.0 0.0 copy-done.2
  16.0 2.0 reshape.176.vc_ref
  18.0 0.2 compare_reduce_fusion.1
  18.2 0.2 fusion.4.sfresh_ref
  18.4 0.2 fusion.3
  18.5 0.5 broadcast_select_fusion.4
  19.1 0.0 copy-done.11
  19.1 0.1 select_reduce_fusion.1
  19.2 0.2 compare_reduce_fusion
  19.3 0.5 fusion.8.skind_ref
  19.8 102.1 %all-gather.2.cloned.1.call-done.q_ref.kf_ref.vf_ref = bf16[4,4608,512]{2,1,0:T(8,128)(2,1)} async-done(((bf16[4,72,512]{2,1,0:T(8,128)(2,1)}), bf16[4,4608,512]{2,1,0:T(8,128)(2,1)}) %all-gather.2.cloned.1.call-update) | async-done | bytes 18874384 | tf_op jit(solution)/shard_map/all_gather | solution.py:195
  121.9 0.0 copy-done.8
  121.9 0.0 copy-done.10
  121.9 39.9 %shard_map.121 = bf16[64,72,640]{2,1,0:T(8,128)(2,1)} custom-call(s32[12]{0:T(128)} %copy-done.10, s32[12]{0:T(128)} %fusion.8.skind_ref, s32[12]{0:T(128)} %get-tuple-element.6.slim_ref, s32[12]{0:T(128)} %copy-done.8, bf16[4,4608,512]{2,1,0:T(8,128)(2,1)} %all-gather.2.cloned.1.call-done.q_ref.kf_ref.vf_ref, ...), custom_call_target="tpu_custom_call" | custom-call | flops 2415919104 | bytes 16908288 | tf_op jit(solution)/shard_map/pallas_call | solution.py:124
  161.8 5.7 %all-to-all-start = ((bf16[64,72,640]{2,1,0:T(8,128)(2,1)}), bf16[64,72,640]{2,1,0:T(8,128)(2,1)}, u32[]{:S(2)}, u32[]{:S(2)}) async-start(bf16[64,72,640]{2,1,0:T(8,128)(2,1)} %shard_map.121), calls=%async_computation | async-start | bytes 11796480 | tf_op jit(solution)/shard_map/all_to_all | solution.py:235
  167.5 0.2 reduce-scatter.2.cloned.1.call-start
  167.8 10.9 %fusion.13 = (bf16[1,4608,512]{2,1,0:T(8,128)(2,1)}, bf16[1,4608,512]{2,1,0:T(8,128)(2,1)}, bf16[1,4608,512]{2,1,0:T(8,128)(2,1)}) fusion(bf16[4,4608,512]{2,1,0:T(8,128)(2,1)} %all-gather.2.cloned.1.call-done.q_ref.kf_ref.vf_ref), kind=kLoop, calls=%fused_computation.57 | loop fusion | bytes 28311552 | tf_op jit(solution)/shard_map/slice | solution.py:217
  178.7 121.6 %all-to-all-done = bf16[64,72,640]{2,1,0:T(8,128)(2,1)} async-done(((bf16[64,72,640]{2,1,0:T(8,128)(2,1)}), bf16[64,72,640]{2,1,0:T(8,128)(2,1)}, u32[]{:S(2)}, u32[]{:S(2)}) %all-to-all-start) | async-done | bytes 5898272 | tf_op jit(solution)/shard_map/all_to_all | solution.py:235
  300.3 3.4 convert_element_type.67
  303.7 0.2 slice_reduce_fusion
  303.9 1.3 fusion.2
  305.2 2.9 copy-done
  308.1 6.5 %mul.122 = f32[64,72,4,128]{3,2,1,0:T(4,128)} broadcast(f32[64,72,4]{2,1,0:T(8,128)S(1)} %get-tuple-element.5), dimensions={0,1,2} | broadcast | bytes 9510912 | tf_op jit(solution)/shard_map/mul | solution.py:244
  314.6 12.3 %mul.123 = f32[64,72,512]{2,1,0:T(8,128)} reshape(f32[64,72,4,128]{3,2,1,0:T(4,128)} %mul.122) | data formatting | bytes 18874368 | tf_op jit(solution)/shard_map/mul | solution.py:244
  326.9 8.4 %fusion = f32[72,512]{1,0:T(8,128)S(1)} fusion(f32[64,72,512]{2,1,0:T(8,128)} %mul.123, f32[64,72,640]{2,1,0:T(8,128)} %copy-done), kind=kLoop, calls=%fused_computation.3 | loop fusion | flops 4681728 | bytes 19021824 | tf_op jit(solution)/shard_map/reduce_sum | solution.py:244
  335.3 0.1 reduce_sum.61
  335.4 0.1 divide_convert_fusion
  335.6 3.7 fusion.14
  339.3 0.0 copy-start.9
  339.3 1.1 slice.95
  340.4 2.1 copy.14
  342.6 0.0 reduce-scatter.2.cloned.1.call-update
  342.6 4.2 %gather_fusion = bf16[12,128,512]{2,1,0:T(8,128)(2,1)} fusion(bf16[36,128,512]{2,1,0:T(8,128)(2,1)} %bitcast.11, s32[1024]{0:T(1024)S(1)} %pad_clamp_fusion), kind=kCustom, calls=%fused_computation.clone | custom fusion | bytes 3145776 | tf_op jit(solution)/shard_map/jit(_take)/gather | solution.py:216
  346.8 4.2 %gather_fusion.1 = bf16[12,128,512]{2,1,0:T(8,128)(2,1)} fusion(bf16[36,128,512]{2,1,0:T(8,128)(2,1)} %bitcast.10, s32[1024]{0:T(1024)S(1)} %pad_clamp_fusion), kind=kCustom, calls=%fused_computation.1.clone | custom fusion | bytes 3145776 | tf_op jit(solution)/shard_map/jit(_take)/gather | solution.py:217
  351.0 3.9 %broadcast_select_fusion.2 = (bf16[12,128,512]{2,1,0:T(8,128)(2,1)}, bf16[12,128,512]{2,1,0:T(8,128)(2,1)}) fusion(bf16[12,128,512]{2,1,0:T(8,128)(2,1)} %gather_fusion.1, pred[12]{0:T(512)(128)(4,1)S(1)} %compare_and_fusion, bf16[12,128,512]{2,1,0:T(8,128)(2,1)} %gather_fusion), kind=kLoop, calls=%fused_computation.12 | loop fusion | flops 1572864 | bytes 6291468 | tf_op jit(solution)/shard_map/jit(_take)/select_n | solution.py:217
  354.9 3.5 reshape.177
  358.4 3.5 reshape.178
  361.9 5.3 %broadcast_select_fusion = (bf16[12,128,4,128]{3,2,1,0:T(4,128)(2,1)}, bf16[12,128,4,128]{3,2,1,0:T(4,128)(2,1)}) fusion(bf16[12,128,4,128]{3,2,1,0:T(4,128)(2,1)} %reshape.178, bf16[12,128,4,128]{3,2,1,0:T(4,128)(2,1)S(1)} %copy-done.2, pred[12]{0:T(512)(128)(4,1)S(1)} %compare_reduce_fusion.1, bf16[12,128,4,128]{3,2,1,0:T(4,128)(2,1)} %reshape.177, ...), kind=kLoop, calls=%fused_computation.10 | loop fusion | flops 1572864 | bytes 9437196 | tf_op jit(solution)/shard_map/jit(_where)/select_n | solution.py:220
  367.2 1.6 add_convert_fusion
  (19 shorter events, 0.2 us)
Async XLA Ops:
  7.2 5.8 %copy-start.4 = (bf16[512,64]{0,1:T(8,128)(2,1)S(1)}, bf16[512,64]{0,1:T(8,128)(2,1)}, u32[]{:S(2)}) copy-start(bf16[512,64]{0,1:T(8,128)(2,1)} %param.20) | copy-start | bytes 196612
  7.2 5.8 %copy-start.3 = (bf16[72,4,128]{2,1,0:T(4,128)(2,1)S(1)}, bf16[72,4,128]{2,1,0:T(4,128)(2,1)}, u32[]{:S(2)}) copy-start(bf16[72,4,128]{2,1,0:T(4,128)(2,1)} %param.14) | copy-start | bytes 221188
  7.2 6.6 %copy-start.6 = (s32[6,6]{1,0:T(8,128)S(1)}, s32[6,6]{1,0:T(8,128)}, u32[]{:S(2)}) copy-start(s32[6,6]{1,0:T(8,128)} %param.19) | copy-start | bytes 436
  7.2 6.7 %copy-start.7 = (s32[6,122]{1,0:T(8,128)S(1)}, s32[6,122]{1,0:T(8,128)}, u32[]{:S(2)}) copy-start(s32[6,122]{1,0:T(8,128)} %param.18) | copy-start | bytes 8788
  7.2 6.8 %copy-start.1 = (bf16[12,128,4,128]{3,2,1,0:T(4,128)(2,1)S(1)}, bf16[12,128,4,128]{3,2,1,0:T(4,128)(2,1)}, u32[]{:S(2)}) copy-start(bf16[12,128,4,128]{3,2,1,0:T(4,128)(2,1)} %param.15) | copy-start | bytes 4718596
  7.2 114.7 %all-gather.2.cloned.1.call-start = ((), (), s32[]{:S(2)}) async-start(), calls=%async_computation.2 | async-start | bytes 19169280 | tf_op jit(solution)/shard_map/all_gather | solution.py:195
  12.8 3.1 copy-start.2
  16.0 3.1 copy-start.11
  18.3 103.6 %copy-start.8 = (s32[12]{0:T(128)}, s32[12]{0:T(128)S(1)}, u32[]{:S(2)}) copy-start(s32[12]{0:T(128)S(1)} %fusion.4.sfresh_ref) | copy-start | bytes 148
  19.1 102.8 %copy-start.10 = (s32[12]{0:T(128)}, s32[12]{0:T(128)S(1)}, u32[]{:S(2)}) copy-start(s32[12]{0:T(128)S(1)} %get-tuple-element.17.sreq_ref) | copy-start | bytes 148
  161.8 138.5 %all-to-all-start = ((bf16[64,72,640]{2,1,0:T(8,128)(2,1)}), bf16[64,72,640]{2,1,0:T(8,128)(2,1)}, u32[]{:S(2)}, u32[]{:S(2)}) async-start(bf16[64,72,640]{2,1,0:T(8,128)(2,1)} %shard_map.121), calls=%async_computation | async-start | bytes 11796480 | tf_op jit(solution)/shard_map/all_to_all | solution.py:235
  167.5 199.7 %reduce-scatter.2.cloned.1.call-start = ((), (), s32[]{:S(2)}) async-start(), calls=%async_computation.3 | async-start | bytes 737280 | tf_op jit(solution)/shard_map/reduce_scatter | solution.py:253
  303.7 4.4 %copy-start = (f32[64,72,640]{2,1,0:T(8,128)}, f32[64,72,640]{2,1,0:T(8,128)S(1)}, u32[]{:S(2)}) copy-start(f32[64,72,640]{2,1,0:T(8,128)S(1)} %convert_element_type.67) | copy-start | bytes 35389444
  339.3 3.3 copy-start.9
  361.9 5.3 %copy-start.5 = (f32[1024]{0:T(1024)S(1)}, f32[1024]{0:T(1024)}, u32[]{:S(2)}) copy-start(f32[1024]{0:T(1024)} %param.21) | copy-start | bytes 12292
Sparse Core Ops, SparseCore 0:
  13.9 107.9 all-gather.1
  342.7 19.0 reduce-scatter.1

commit v3 on v2

--- a/solution.py
+++ b/solution.py
@@ -38,7 +38,7 @@
     heads, head_dim, requests, span,
     sreq_ref, skind_ref, slim_ref, sfresh_ref,
     q_ref, kf_ref, vf_ref, kc_ref, vc_ref,
-    out_ref, acc_ref, ml_ref,
+    out_ref, ko_ref, vo_ref, acc_ref, ml_ref,
 ):
     step = pl.program_id(0)
     lanes = ml_ref.shape[1]
@@ -97,6 +97,16 @@
     def _fresh():
         attend(kf_ref, vf_ref)
 
+    @pl.when(kind == 2)
+    def _store_fresh():
+        ko_ref[...] = kf_ref[...]
+        vo_ref[...] = vf_ref[...]
+
+    @pl.when(kind != 2)
+    def _store_cached():
+        ko_ref[...] = kc_ref[...]
+        vo_ref[...] = vc_ref[...]
+
     @pl.when(step == pl.num_programs(0) - 1)
     def _emit():
         chunks, rows_per, _ = out_ref.shape
@@ -123,7 +133,11 @@
     flops = 4 * slot_count * span * PAGE * width
     return pl.pallas_call(
         kernel,
-        out_shape=jax.ShapeDtypeStruct((chunks, rows_per, width + 128), jnp.bfloat16),
+        out_shape=(
+            jax.ShapeDtypeStruct((chunks, rows_per, width + 128), jnp.bfloat16),
+            jax.ShapeDtypeStruct(kc.shape, kc.dtype),
+            jax.ShapeDtypeStruct(vc.shape, vc.dtype),
+        ),
         grid_spec=pltpu.PrefetchScalarGridSpec(
             num_scalar_prefetch=4,
             grid=(slot_count,),
@@ -135,7 +149,11 @@
                 pl.BlockSpec((1, PAGE, width), lambda s, *_: (s, 0, 0)),
                 pl.BlockSpec((1, PAGE, width), lambda s, *_: (s, 0, 0)),
             ],
-            out_specs=pl.BlockSpec((chunks, rows_per, width + 128), lambda s, *_: (0, 0, 0)),
+            out_specs=[
+                pl.BlockSpec((chunks, rows_per, width + 128), lambda s, *_: (0, 0, 0)),
+                pl.BlockSpec((1, PAGE, width), lambda s, *_: (s, 0, 0)),
+                pl.BlockSpec((1, PAGE, width), lambda s, *_: (s, 0, 0)),
+            ],
             scratch_shapes=[
                 pltpu.VMEM((tokens, width), jnp.float32),
                 pltpu.VMEM((tokens, 128), jnp.float32),
@@ -150,6 +168,68 @@
             bytes_accessed=tokens * width * 2 + 4 * kc.size * 2 + tokens * (width + 128) * 2,
         ),
     )(slot_request, slot_kind, slot_limit, slot_fresh, gathered, gathered, gathered, kc, vc)
+
+
+def combine_kernel(heads, head_dim, recv_ref, w_ref, out_ref, o_acc, l_acc):
+    chunks, rows_per, _ = recv_ref.shape
+    width = heads * head_dim
+    lanes = 128
+
+    def peak_step(d, peak):
+        return jnp.maximum(peak, recv_ref[d, :, width:].astype(jnp.float32))
+
+    peak = lax.fori_loop(
+        0, chunks, peak_step, jnp.full((rows_per, lanes), mask_score, jnp.float32)
+    )
+    o_acc[...] = jnp.zeros_like(o_acc)
+    l_acc[...] = jnp.zeros_like(l_acc)
+
+    def sum_step(d, carry):
+        mld = recv_ref[d, :, width:].astype(jnp.float32)
+        factor = jnp.exp(mld - peak)
+        for h in range(heads):
+            f_h = factor[:, h : h + 1]
+            l_h = mld[:, heads + h : heads + h + 1] + mld[:, 2 * heads + h : 2 * heads + h + 1]
+            l_acc[:, h : h + 1] += f_h * l_h
+            cut = slice(h * head_dim, (h + 1) * head_dim)
+            o_acc[:, cut] += f_h * recv_ref[d, :, cut].astype(jnp.float32)
+        return carry
+
+    lax.fori_loop(0, chunks, sum_step, 0)
+    parts = []
+    for h in range(heads):
+        cut = slice(h * head_dim, (h + 1) * head_dim)
+        parts.append((o_acc[:, cut] / l_acc[:, h : h + 1]).astype(jnp.bfloat16))
+    attended = jnp.concatenate(parts, axis=1)
+    out_ref[...] = lax.dot_general(
+        attended, w_ref[0], (((1,), (1,)), ((), ())), preferred_element_type=jnp.float32
+    ).astype(out_ref.dtype)
+
+
+def combine_project(received, gathered, heads, head_dim):
+    chunks, rows_per, _ = received.shape
+    _, tokens, width = gathered.shape
+    kernel = functools.partial(combine_kernel, heads, head_dim)
+    return pl.pallas_call(
+        kernel,
+        out_shape=jax.ShapeDtypeStruct((rows_per, tokens), jnp.bfloat16),
+        grid=(1,),
+        in_specs=[
+            pl.BlockSpec(received.shape, lambda i: (0, 0, 0)),
+            pl.BlockSpec((1, tokens, width), lambda i: (3, 0, 0)),
+        ],
+        out_specs=pl.BlockSpec((rows_per, tokens), lambda i: (0, 0)),
+        scratch_shapes=[
+            pltpu.VMEM((rows_per, width), jnp.float32),
+            pltpu.VMEM((rows_per, 128), jnp.float32),
+        ],
+        compiler_params=pltpu.CompilerParams(vmem_limit_bytes=48 * 1024 * 1024),
+        cost_estimate=pl.CostEstimate(
+            flops=2 * rows_per * tokens * width + 4 * received.size,
+            transcendentals=chunks * rows_per * 128,
+            bytes_accessed=received.size * 2 + tokens * width * 2 + rows_per * tokens * 2,
+        ),
+    )(received, gathered)
 
 
 def per_device(
@@ -212,13 +292,7 @@
     visible = is_cached & (slot_page * PAGE < slot_length)
     slot_kind = jnp.where(is_fresh, 2, jnp.where(visible, 1, 0)).astype(jnp.int32)
     slot_limit = jnp.where(is_fresh, slot_page * PAGE, -4 * span_len)
-    page_pool = (requests * new_pages, PAGE, width)
-    fresh_k = jnp.take(gathered[1].reshape(page_pool), fresh_index, axis=0)
-    fresh_v = jnp.take(gathered[2].reshape(page_pool), fresh_index, axis=0)
-    cache_shape = key_cache.shape
-    key_out = jnp.where(is_fresh[:, None, None, None], fresh_k.reshape(cache_shape), key_cache)
-    value_out = jnp.where(is_fresh[:, None, None, None], fresh_v.reshape(cache_shape), value_cache)
-    packed = local_attention(
+    packed, key_slots, value_slots = local_attention(
         slot_request,
         slot_kind,
         slot_limit,
@@ -232,27 +306,14 @@
         span_len,
         page_devices,
     )
-    received = lax.all_to_all(packed, "pages", 0, 0, tiled=True).astype(jnp.float32)
-    part_o = received[:, :, :width].reshape(page_devices, tok_dev, head_count, head_dim)
-    part_m = received[:, :, width : width + head_count]
-    part_l = (
-        received[:, :, width + head_count : width + 2 * head_count]
-        + received[:, :, width + 2 * head_count : width + 3 * head_count]
-    )
-    peak = jnp.max(part_m, axis=0)
-    factor = jnp.exp(part_m - peak[None])
-    weighted = jnp.sum(part_o * factor[..., None], axis=0)
-    totals = jnp.sum(part_l * factor, axis=0)
-    attended = (weighted / totals[:, :, None]).reshape(tok_dev, width).astype(jnp.bfloat16)
-    projected = lax.dot_general(
-        attended, gathered[3], (((1,), (1,)), ((), ())), preferred_element_type=jnp.float32
-    )
+    received = lax.all_to_all(packed, "pages", 0, 0, tiled=True)
+    projected = combine_project(received, gathered, head_count, head_dim)
     projected = projected.reshape(tok_dev, page_devices, tok_dev)[:, :, :w_cols].reshape(
         tok_dev, page_devices * w_cols
     )
-    summed = lax.psum_scatter(
-        projected.astype(jnp.bfloat16), "heads", scatter_dimension=1, tiled=True
-    ).astype(jnp.float32)
+    key_out = key_slots.reshape(key_cache.shape)
+    value_out = value_slots.reshape(value_cache.shape)
+    summed = lax.psum_scatter(projected, "heads", scatter_dimension=1, tiled=True).astype(jnp.float32)
     hidden = (summed + out_bias[None, :]).astype(jnp.bfloat16)
     return (hidden, key_out, value_out)
 

time: 377 us -> 359 us (0.952)
  blocking collectives: 0 us -> 144 us
  waiting for transfers between devices: 224 us -> 117 us
  local copies, waits for them, and re-layouts: 57.6 us -> 16 us
  other arithmetic: 30.5 us -> 7.87 us
  Pallas kernels: 39.9 us -> 57.1 us
  starting transfers between devices: 5.96 us -> 0.08 us
    all_to_all x0 -> x1, blocking collectives: none -> 144 us  [per_device(): received = lax.all_to_all(packed, 'pages', 0, 0, tiled=True)]
    all_to_all x1 -> x0, waiting for transfers between devices: 122 us -> none  [per_device(): lax.all_to_all(packed, 'pages', 0, 0, tiled=True).astype(jnp.float32)]
    mul x2 -> x0, local copies, waits for them, and re-layouts: 18.7 us -> none  [per_device(): weighted = jnp.sum(part_o * factor[..., None], axis=0)]
    pallas_call x1 -> x2, Pallas kernels: 39.9 us -> 57.1 us  [the longest x1 39.6 us: local_attention(): pl.pallas_call(kernel, out_shape=(jax.ShapeDtypeStruct((chunks, rows_per,...]
    reduce_scatter x1, waiting for transfers between devices: 0.01 us -> 15.3 us  [per_device(): lax.psum_scatter(projected, 'heads', scatter_dimension=1, tiled=True)]
    slice x2 -> x0, local copies, waits for them, and re-layouts: 12 us -> none  [the longest x1 10.9 us: per_device(): fresh_v = jnp.take(gathered[2].reshape(page_pool), fresh_index, axis=0)]
    reduce_sum x2 -> x0, other arithmetic: 9.73 us -> none  [the longest x1 8.44 us: per_device(): weighted = jnp.sum(part_o * factor[..., None], axis=0)]
    select_n x2 -> x0, other arithmetic: 9.17 us -> none  [the longest x1 5.28 us: per_device(): jnp.where(is_fresh[:, None, None, None], fresh_v.reshape(cache_shape), va...]
  transfers between devices with their start and end apart: 3 -> 2, of which waited for: 2 -> 2; matrix products, arithmetic and copies ran while one was open for 11% -> 3% of each run, Pallas kernels for 0% -> 0%
where the time goes in v3:
time: 359 us; the launch traced here: 357 us
  blocking collectives  144 us (40%)
  waiting for transfers between devices  117 us (33%)
  Pallas kernels  57.1 us (16%)
  local copies, waits for them, and re-layouts  16 us (4%)
  between operations  14.2 us (4%)
  other arithmetic  7.87 us (2%)
    all_to_all x1, blocking collectives, per_device(): received = lax.all_to_all(packed, 'pages', 0, 0, tiled=True)  144 us
    all_gather x1, waiting for transfers between devices, per_device(): gathered = lax.all_gather(stacked, 'pages', axis=1, tiled=True)  102 us
    pallas_call x1, Pallas kernels, local_attention(): pl.pallas_call(kernel, out_shape=(jax.ShapeDtypeStruct((chunks, rows_per,...  39.6 us
    pallas_call x1, Pallas kernels, combine_project(): pl.pallas_call(kernel, out_shape=jax.ShapeDtypeStruct((rows_per, tokens),...  17.4 us
    reduce_scatter x1, waiting for transfers between devices, per_device(): lax.psum_scatter(projected, 'heads', scatter_dimension=1, tiled=True)  15.3 us
  transfers between devices with their start and end apart: 2, of which 2 were waited for; matrix products, arithmetic and copies ran while one was open for 3% of the time, Pallas kernels for 0%

profile of v3, /device:TPU:4, one launch (start us, length us, event | category | flops | bytes accessed | tf_op | source)
XLA Modules:
  0.0 356.6 jit_solution(2127158452752319501)
XLA Ops:
  7.2 0.0 all-gather.2.cloned.1.call-start
  7.2 1.0 slice.25
  8.2 0.9 convert_element_type.43
  9.1 1.0 slice.28
  10.1 0.9 convert_element_type.46
  11.0 0.0 copy-start.5
  11.1 0.0 copy-start.6
  11.1 0.0 copy-start
  11.1 0.9 select_reduce_fusion
  12.0 0.9 stack_reshape.2
  12.9 0.8 pad_bitcast_fusion
  13.7 0.2 multiply_cosine_fusion
  14.0 0.3 subtract_convert_fusion.1
  14.3 0.3 pad_maximum_fusion.1
  14.7 0.8 pad_maximum_fusion
  15.5 0.0 all-gather.2.cloned.1.call-update
  15.5 0.0 reduce-scatter.2.cloned.1.call-start
  15.5 0.0 copy-done.5
  15.5 0.1 eq.61
  15.6 0.0 copy-done.6
  15.6 0.1 eq.65
  15.7 0.0 copy-done
  15.7 0.0 copy-start.1
  15.7 2.0 reshape.151.kc_ref
  17.7 0.0 copy-done.1
  17.7 0.0 copy-start.9
  17.7 2.0 reshape.152.vc_ref
  19.7 0.2 fusion.1.sfresh_ref
  19.9 0.0 copy-start.7
  19.9 0.2 compare_reduce_fusion.1
  20.1 0.2 fusion
  20.3 0.5 broadcast_select_fusion
  20.8 0.0 copy-start.8
  20.8 0.0 copy-done.9
  20.8 0.1 select_reduce_fusion.1
  20.9 0.2 compare_reduce_fusion
  21.1 0.6 fusion.5.skind_ref
  21.7 101.9 %all-gather.2.cloned.1.call-done.q_ref.kf_ref.vf_ref.w_ref = bf16[4,4608,512]{2,1,0:T(8,128)(2,1)} async-done(((bf16[4,72,512]{2,1,0:T(8,128)(2,1)}), bf16[4,4608,512]{2,1,0:T(8,128)(2,1)}) %all-gather.2.cloned.1.call-update) | async-done | bytes 18874384 | tf_op jit(solution)/shard_map/all_gather | solution.py:275
  123.6 0.0 copy-done.7
  123.6 0.0 copy-done.8
  123.6 39.6 %shard_map.121 = (bf16[64,72,640]{2,1,0:T(8,128)(2,1)}, bf16[12,128,512]{2,1,0:T(8,128)(2,1)}, bf16[12,128,512]{2,1,0:T(8,128)(2,1)}) custom-call(s32[12]{0:T(128)} %copy-done.8, s32[12]{0:T(128)} %fusion.5.skind_ref, s32[12]{0:T(128)} %get-tuple-element.9.slim_ref, s32[12]{0:T(128)} %copy-done.7, ...), custom_call_target="tpu_custom_call" | custom-call | flops 2415919104 | bytes 16908288 | tf_op jit(solution)/shard_map/pallas_call | solution.py:134
  163.2 144.1 %all_to_all.5.recv_ref = bf16[64,72,640]{2,1,0:T(8,128)(2,1)} all-to-all(bf16[64,72,640]{2,1,0:T(8,128)(2,1)} %get-tuple-element.6), channel_id=1, replica_groups=mesh['heads'=4,'pages'=64] {'pages'}, dimensions={0} | all-to-all | bytes 11796480 | tf_op jit(solution)/shard_map/all_to_all | solution.py:309
  307.3 17.4 %shard_map.122 = bf16[72,4608]{1,0:T(8,128)(2,1)S(1)} custom-call(bf16[64,72,640]{2,1,0:T(8,128)(2,1)} %all_to_all.5.recv_ref, bf16[4,4608,512]{2,1,0:T(8,128)(2,1)} %all-gather.2.cloned.1.call-done.q_ref.kf_ref.vf_ref.w_ref), custom_call_target="tpu_custom_call" | custom-call | flops 351535104 | bytes 11280384 | tf_op jit(solution)/shard_map/pallas_call | solution.py:213
  324.8 2.6 reshape.153
  327.4 0.0 copy-start.3
  327.4 1.7 reshape.154
  329.1 0.0 reduce-scatter.2.cloned.1.call-update
  329.2 0.0 copy-done.3
  329.2 0.0 copy-start.2
  329.2 1.9 reshape.155
  331.0 0.0 copy-done.2
  331.0 0.0 copy-start.4
  331.0 1.8 reshape.156
  332.9 15.3 %reduce-scatter.2.cloned.1.call-done = bf16[72,1024]{1,0:T(8,128)(2,1)} async-done(((bf16[72,4096]{1,0:T(8,128)(2,1)}), bf16[72,1024]{1,0:T(8,128)(2,1)}) %reduce-scatter.2.cloned.1.call-update) | async-done | bytes 147472 | tf_op jit(solution)/shard_map/reduce_scatter | solution.py:316
  348.2 0.0 copy-done.4
  348.2 1.6 add_convert_fusion
  (6 shorter events, 0.1 us)
Async XLA Ops:
  7.2 116.4 %all-gather.2.cloned.1.call-start = ((), (), s32[]{:S(2)}) async-start(), calls=%async_computation.2 | async-start | bytes 19169280 | tf_op jit(solution)/shard_map/all_gather | solution.py:275
  11.0 4.5 %copy-start.5 = (s32[6,6]{1,0:T(8,128)S(1)}, s32[6,6]{1,0:T(8,128)}, u32[]{:S(2)}) copy-start(s32[6,6]{1,0:T(8,128)} %param.17) | copy-start | bytes 436
  11.1 4.6 %copy-start.6 = (s32[6,122]{1,0:T(8,128)S(1)}, s32[6,122]{1,0:T(8,128)}, u32[]{:S(2)}) copy-start(s32[6,122]{1,0:T(8,128)} %param.16) | copy-start | bytes 8788
  11.1 4.6 %copy-start = (bf16[12,128,4,128]{3,2,1,0:T(4,128)(2,1)S(1)}, bf16[12,128,4,128]{3,2,1,0:T(4,128)(2,1)}, u32[]{:S(2)}) copy-start(bf16[12,128,4,128]{3,2,1,0:T(4,128)(2,1)} %param.13) | copy-start | bytes 4718596
  15.5 332.7 %reduce-scatter.2.cloned.1.call-start = ((), (), s32[]{:S(2)}) async-start(), calls=%async_computation.3 | async-start | bytes 737280 | tf_op jit(solution)/shard_map/reduce_scatter | solution.py:316
  15.7 2.0 copy-start.1
  17.7 3.1 copy-start.9
  19.9 103.7 %copy-start.7 = (s32[12]{0:T(128)}, s32[12]{0:T(128)S(1)}, u32[]{:S(2)}) copy-start(s32[12]{0:T(128)S(1)} %fusion.1.sfresh_ref) | copy-start | bytes 148
  20.8 102.8 %copy-start.8 = (s32[12]{0:T(128)}, s32[12]{0:T(128)S(1)}, u32[]{:S(2)}) copy-start(s32[12]{0:T(128)S(1)} %get-tuple-element.17.sreq_ref) | copy-start | bytes 148
  327.4 1.8 copy-start.3
  329.2 1.9 copy-start.2
  331.0 17.2 %copy-start.4 = (f32[1024]{0:T(1024)S(1)}, f32[1024]{0:T(1024)}, u32[]{:S(2)}) copy-start(f32[1024]{0:T(1024)} %param.19) | copy-start | bytes 12292
Sparse Core Ops, SparseCore 0:
  15.6 107.9 all-gather.1
  329.3 18.8 reduce-scatter.1

commit v4 on v3

--- a/solution.py
+++ b/solution.py
@@ -10,6 +10,7 @@
 
 ROT = 32
 PAGE = 128
+PAGES = ("chips", "core")
 
 
 low_score = -1e30
@@ -232,6 +233,95 @@
     )(received, gathered)
 
 
+def pair_merge_kernel(heads, head_dim, packed_hbm, out_ref, mine, theirs, local_sem, send_sem, recv_sem):
+    core = lax.axis_index("core")
+    partner = 1 - core
+    width = heads * head_dim
+    lanes = 128
+    chunks, rows_per, _ = out_ref.shape
+
+    barrier = pltpu.get_barrier_semaphore()
+    pl.semaphore_signal(barrier, inc=1, device_id={"core": partner}, device_id_type=pl.DeviceIdType.MESH)
+    pl.semaphore_wait(barrier, 1)
+
+    local = pltpu.make_async_copy(packed_hbm.at[:, core], mine, local_sem)
+    local.start()
+    remote = pltpu.make_async_remote_copy(
+        src_ref=packed_hbm.at[:, partner],
+        dst_ref=theirs,
+        send_sem=send_sem,
+        recv_sem=recv_sem,
+        device_id={"core": partner},
+        device_id_type=pl.DeviceIdType.MESH,
+    )
+    remote.start()
+    local.wait()
+    remote.wait()
+
+    lane = lax.broadcasted_iota(jnp.int32, (rows_per, lanes), 1)
+
+    def merge_step(c, carry):
+        ml_a = mine[c, :, width:].astype(jnp.float32)
+        ml_b = theirs[c, :, width:].astype(jnp.float32)
+        peak = jnp.maximum(ml_a, ml_b)
+        f_a = jnp.exp(ml_a - peak)
+        f_b = jnp.exp(ml_b - peak)
+        merged = jnp.zeros((rows_per, lanes), jnp.float32)
+        for h in range(heads):
+            cut = slice(h * head_dim, (h + 1) * head_dim)
+            fa_h = f_a[:, h : h + 1]
+            fb_h = f_b[:, h : h + 1]
+            out_ref[c, :, cut] = (
+                fa_h * mine[c, :, cut].astype(jnp.float32)
+                + fb_h * theirs[c, :, cut].astype(jnp.float32)
+            ).astype(out_ref.dtype)
+            l_a = ml_a[:, heads + h : heads + h + 1] + ml_a[:, 2 * heads + h : 2 * heads + h + 1]
+            l_b = ml_b[:, heads + h : heads + h + 1] + ml_b[:, 2 * heads + h : 2 * heads + h + 1]
+            l_h = fa_h * l_a + fb_h * l_b
+            l_hi = l_h.astype(jnp.bfloat16).astype(jnp.float32)
+            merged = jnp.where(
+                lane == h,
+                peak[:, h : h + 1],
+                jnp.where(
+                    lane == heads + h,
+                    l_hi,
+                    jnp.where(lane == 2 * heads + h, l_h - l_hi, merged),
+                ),
+            )
+        out_ref[c, :, width:] = merged.astype(out_ref.dtype)
+        return carry
+
+    lax.fori_loop(0, chunks, merge_step, 0)
+
+
+def pair_merge(packed, heads, head_dim):
+    devices, rows_per, lanes_all = packed.shape
+    chips = devices // 2
+    view = packed.reshape(chips, 2, rows_per, lanes_all)
+    kernel = functools.partial(pair_merge_kernel, heads, head_dim)
+    return pl.pallas_call(
+        kernel,
+        out_shape=jax.ShapeDtypeStruct((chips, rows_per, lanes_all), packed.dtype),
+        in_specs=[pl.BlockSpec(memory_space=pl.ANY)],
+        out_specs=pl.BlockSpec(memory_space=pltpu.VMEM),
+        scratch_shapes=[
+            pltpu.VMEM((chips, rows_per, lanes_all), packed.dtype),
+            pltpu.VMEM((chips, rows_per, lanes_all), packed.dtype),
+            pltpu.SemaphoreType.DMA(()),
+            pltpu.SemaphoreType.DMA(()),
+            pltpu.SemaphoreType.DMA(()),
+        ],
+        compiler_params=pltpu.CompilerParams(
+            collective_id=0, has_side_effects=True, vmem_limit_bytes=40 * 1024 * 1024
+        ),
+        cost_estimate=pl.CostEstimate(
+            flops=6 * chips * rows_per * lanes_all,
+            transcendentals=2 * chips * rows_per * 128,
+            bytes_accessed=3 * chips * rows_per * lanes_all * 2,
+        ),
+    )(view)
+
+
 def per_device(
     queries,
     keys,
@@ -251,8 +341,8 @@
     new_pages = append_slots.shape[1]
     span_len = new_pages * PAGE
     slot_count = key_cache.shape[0]
-    page_devices = lax.axis_size("pages")
-    device_at = lax.axis_index("pages")
+    page_devices = lax.axis_size(PAGES)
+    device_at = lax.axis_index(PAGES)
     token_ids = device_at * tok_dev + jnp.arange(tok_dev, dtype=jnp.int32)
     request_ids = token_ids // span_len
     request_grid = jnp.arange(requests, dtype=jnp.int32)
@@ -272,7 +362,7 @@
             w_plane,
         ]
     )
-    gathered = lax.all_gather(stacked, "pages", axis=1, tiled=True)
+    gathered = lax.all_gather(stacked, PAGES, axis=1, tiled=True)
     my_slots = device_at * slot_count + jnp.arange(slot_count, dtype=jnp.int32)
     cached_hit = page_table.reshape(-1)[None, :] == my_slots[:, None]
     fresh_hit = append_slots.reshape(-1)[None, :] == my_slots[:, None]
@@ -306,7 +396,8 @@
         span_len,
         page_devices,
     )
-    received = lax.all_to_all(packed, "pages", 0, 0, tiled=True)
+    paired = pair_merge(packed, head_count, head_dim)
+    received = lax.all_to_all(paired, "chips", 0, 0, tiled=True)
     projected = combine_project(received, gathered, head_count, head_dim)
     projected = projected.reshape(tok_dev, page_devices, tok_dev)[:, :, :w_cols].reshape(
         tok_dev, page_devices * w_cols
@@ -319,26 +410,30 @@
 
 
 def solution(mesh):
+    heads_n, pages_n = mesh.devices.shape
+    split = jax.sharding.Mesh(
+        mesh.devices.reshape(heads_n, pages_n // 2, 2), ("heads", "chips", "core")
+    )
     placed = (
-        P("pages", "heads", None),
-        P("pages", "heads", None),
-        P("pages", "heads", None),
-        P("pages", None, "heads", None),
-        P("pages", None, "heads", None),
+        P(PAGES, "heads", None),
+        P(PAGES, "heads", None),
+        P(PAGES, "heads", None),
+        P(PAGES, None, "heads", None),
+        P(PAGES, None, "heads", None),
         P(),
         P(),
         P(),
-        P("heads", "pages"),
+        P("heads", PAGES),
         P("heads"),
     )
     return jax.shard_map(
         per_device,
-        mesh=mesh,
+        mesh=split,
         in_specs=placed,
         out_specs=(
-            P("pages", "heads"),
-            P("pages", None, "heads", None),
-            P("pages", None, "heads", None),
+            P(PAGES, "heads"),
+            P(PAGES, None, "heads", None),
+            P(PAGES, None, "heads", None),
         ),
         check_vma=False,
     )

time: 359 us -> 295 us (0.82)
  blocking collectives: 144 us -> 73.6 us
    all_to_all x1, blocking collectives: 144 us -> 73.6 us  [per_device(): received = lax.all_to_all(paired, 'chips', 0, 0, tiled=True)]
    pallas_call x0 -> x1, Pallas kernels: none -> 19.9 us  [pair_merge(): pl.pallas_call(kernel, out_shape=jax.ShapeDtypeStruct((chips, rows_per, l...]
    pallas_call x1, Pallas kernels: 39.6 us -> 30.6 us  [local_attention(): pl.pallas_call(kernel, out_shape=(jax.ShapeDtypeStruct((chunks, rows_per,...]
    pallas_call x1, Pallas kernels: 17.4 us -> 9.8 us  [combine_project(): pl.pallas_call(kernel, out_shape=jax.ShapeDtypeStruct((rows_per, tokens),...]
where the time goes in v4:
time: 295 us; the launch traced here: 293 us
  waiting for transfers between devices  118 us (40%)
  blocking collectives  73.6 us (25%)
  Pallas kernels  60.3 us (20%)
  local copies, waits for them, and re-layouts  18.7 us (6%)
  between operations  14.2 us (5%)
  other arithmetic  7.81 us (3%)
    all_gather x1, waiting for transfers between devices, per_device(): gathered = lax.all_gather(stacked, PAGES, axis=1, tiled=True)  102 us
    all_to_all x1, blocking collectives, per_device(): received = lax.all_to_all(paired, 'chips', 0, 0, tiled=True)  73.6 us
    pallas_call x1, Pallas kernels, local_attention(): pl.pallas_call(kernel, out_shape=(jax.ShapeDtypeStruct((chunks, rows_per,...  30.6 us
    pallas_call x1, Pallas kernels, pair_merge(): pl.pallas_call(kernel, out_shape=jax.ShapeDtypeStruct((chips, rows_per, l...  19.9 us
    reduce_scatter x1, waiting for transfers between devices, per_device(): lax.psum_scatter(projected, 'heads', scatter_dimension=1, tiled=True)  16.1 us
    pallas_call x1, Pallas kernels, combine_project(): pl.pallas_call(kernel, out_shape=jax.ShapeDtypeStruct((rows_per, tokens),...  9.8 us
  transfers between devices with their start and end apart: 2, of which 2 were waited for; matrix products, arithmetic and copies ran while one was open for 3% of the time, Pallas kernels for 0%

profile of v4, /device:TPU:4, one launch (start us, length us, event | category | flops | bytes accessed | tf_op | source)
XLA Modules:
  0.0 292.8 jit_solution(12801821864136225118)
XLA Ops:
  7.2 0.0 all-gather.2.cloned.1.call-start
  7.2 1.0 slice.25
  8.2 0.9 convert_element_type.43
  9.1 1.0 slice.28
  10.1 0.9 convert_element_type.46
  11.0 0.0 copy-start.6
  11.1 0.0 copy-start.7
  11.1 0.0 copy-start.1
  11.1 0.9 select_reduce_fusion
  12.0 0.9 stack_reshape.2
  12.9 0.8 pad_bitcast_fusion
  13.7 0.2 multiply_cosine_fusion
  14.0 0.3 subtract_convert_fusion.1
  14.3 0.3 pad_maximum_fusion.1
  14.7 0.8 pad_maximum_fusion
  15.5 0.0 all-gather.2.cloned.1.call-update
  15.5 0.0 reduce-scatter.2.cloned.1.call-start
  15.5 0.0 copy-done.6
  15.5 0.1 eq.61
  15.6 0.0 copy-done.7
  15.6 0.1 eq.65
  15.7 0.0 copy-done.1
  15.7 0.0 copy-start.2
  15.7 2.0 reshape.154.kc_ref
  17.7 0.0 copy-done.2
  17.7 0.0 copy-start.10
  17.7 2.0 reshape.155.vc_ref
  19.7 0.2 fusion.1.sfresh_ref
  19.9 0.0 copy-start.8
  19.9 0.2 compare_reduce_fusion.1
  20.1 0.2 fusion
  20.3 0.5 broadcast_select_fusion
  20.8 0.0 copy-start.9
  20.8 0.0 copy-done.10
  20.8 0.1 select_reduce_fusion.1
  20.9 0.2 compare_reduce_fusion
  21.1 0.5 fusion.5.skind_ref
  21.6 102.0 %all-gather.2.cloned.1.call-done.q_ref.kf_ref.vf_ref.w_ref = bf16[4,4608,512]{2,1,0:T(8,128)(2,1)} async-done(((bf16[4,72,512]{2,1,0:T(8,128)(2,1)}), bf16[4,4608,512]{2,1,0:T(8,128)(2,1)}) %all-gather.2.cloned.1.call-update) | async-done | bytes 18874384 | tf_op jit(solution)/shard_map/all_gather | solution.py:365
  123.6 0.0 copy-done.8
  123.6 0.0 copy-done.9
  123.6 30.6 %shard_map.121 = (bf16[64,72,640]{2,1,0:T(8,128)(2,1)}, bf16[12,128,512]{2,1,0:T(8,128)(2,1)}, bf16[12,128,512]{2,1,0:T(8,128)(2,1)}) custom-call(s32[12]{0:T(128)} %copy-done.9, s32[12]{0:T(128)} %fusion.5.skind_ref, s32[12]{0:T(128)} %get-tuple-element.9.slim_ref, s32[12]{0:T(128)} %copy-done.8, ...), custom_call_target="tpu_custom_call" | custom-call | flops 2415919104 | bytes 16908288 | tf_op jit(solution)/shard_map/pallas_call | solution.py:135
  154.2 0.0 copy-start
  154.2 2.7 copy-done
  156.9 19.9 %shard_map.122 = bf16[32,72,640]{2,1,0:T(8,128)(2,1)S(1)} custom-call(bf16[32,2,72,640]{3,2,1,0:T(8,128)(2,1)S(1)} %bitcast.5), custom_call_target="tpu_custom_call" | custom-call | flops 8847360 | bytes 8847360 | tf_op jit(solution)/shard_map/pallas_call | solution.py:302
  176.8 73.6 %all_to_all.5.recv_ref = bf16[32,72,640]{2,1,0:T(8,128)(2,1)S(1)} all-to-all(bf16[32,72,640]{2,1,0:T(8,128)(2,1)S(1)} %shard_map.122), channel_id=1, replica_groups=mesh['heads'=4,'chips'=32,'core'=2] {'chips'}, dimensions={0} | all-to-all | bytes 5898240 | tf_op jit(solution)/shard_map/all_to_all | solution.py:400
  250.3 9.8 %shard_map.123 = bf16[72,4608]{1,0:T(8,128)(2,1)S(1)} custom-call(bf16[32,72,640]{2,1,0:T(8,128)(2,1)S(1)} %all_to_all.5.recv_ref, bf16[4,4608,512]{2,1,0:T(8,128)(2,1)} %all-gather.2.cloned.1.call-done.q_ref.kf_ref.vf_ref.w_ref), custom_call_target="tpu_custom_call" | custom-call | flops 345636864 | bytes 8331264 | tf_op jit(solution)/shard_map/pallas_call | solution.py:214
  260.1 2.6 reshape.157
  262.8 0.0 copy-start.4
  262.8 1.7 reshape.158
  264.5 0.0 reduce-scatter.2.cloned.1.call-update
  264.5 0.0 copy-done.4
  264.5 0.0 copy-start.3
  264.5 1.9 reshape.159
  266.4 0.0 copy-done.3
  266.4 0.0 copy-start.5
  266.4 1.8 reshape.160
  268.2 16.1 %reduce-scatter.2.cloned.1.call-done = bf16[72,1024]{1,0:T(8,128)(2,1)} async-done(((bf16[72,4096]{1,0:T(8,128)(2,1)}), bf16[72,1024]{1,0:T(8,128)(2,1)}) %reduce-scatter.2.cloned.1.call-update) | async-done | bytes 147472 | tf_op jit(solution)/shard_map/reduce_scatter | solution.py:407
  284.3 0.0 copy-done.5
  284.3 1.6 add_convert_fusion
  (6 shorter events, 0.1 us)
Async XLA Ops:
  7.2 116.4 %all-gather.2.cloned.1.call-start = ((), (), s32[]{:S(2)}) async-start(), calls=%async_computation.2 | async-start | bytes 19169280 | tf_op jit(solution)/shard_map/all_gather | solution.py:365
  11.0 4.5 %copy-start.6 = (s32[6,6]{1,0:T(8,128)S(1)}, s32[6,6]{1,0:T(8,128)}, u32[]{:S(2)}) copy-start(s32[6,6]{1,0:T(8,128)} %param.17) | copy-start | bytes 436
  11.1 4.6 %copy-start.7 = (s32[6,122]{1,0:T(8,128)S(1)}, s32[6,122]{1,0:T(8,128)}, u32[]{:S(2)}) copy-start(s32[6,122]{1,0:T(8,128)} %param.16) | copy-start | bytes 8788
  11.1 4.6 %copy-start.1 = (bf16[12,128,4,128]{3,2,1,0:T(4,128)(2,1)S(1)}, bf16[12,128,4,128]{3,2,1,0:T(4,128)(2,1)}, u32[]{:S(2)}) copy-start(bf16[12,128,4,128]{3,2,1,0:T(4,128)(2,1)} %param.13) | copy-start | bytes 4718596
  15.5 268.8 %reduce-scatter.2.cloned.1.call-start = ((), (), s32[]{:S(2)}) async-start(), calls=%async_computation.3 | async-start | bytes 737280 | tf_op jit(solution)/shard_map/reduce_scatter | solution.py:407
  15.7 2.0 copy-start.2
  17.7 3.1 %copy-start.10 = (s32[6]{0:T(128)S(1)}, s32[6]{0:T(128)}, u32[]{:S(2)}) copy-start(s32[6]{0:T(128)} %param.15) | copy-start | bytes 76
  19.9 103.7 %copy-start.8 = (s32[12]{0:T(128)}, s32[12]{0:T(128)S(1)}, u32[]{:S(2)}) copy-start(s32[12]{0:T(128)S(1)} %fusion.1.sfresh_ref) | copy-start | bytes 148
  20.8 102.8 %copy-start.9 = (s32[12]{0:T(128)}, s32[12]{0:T(128)S(1)}, u32[]{:S(2)}) copy-start(s32[12]{0:T(128)S(1)} %get-tuple-element.17.sreq_ref) | copy-start | bytes 148
  154.2 2.7 copy-start
  262.8 1.8 copy-start.4
  264.5 1.9 copy-start.3
  266.4 17.9 %copy-start.5 = (f32[1024]{0:T(1024)S(1)}, f32[1024]{0:T(1024)}, u32[]{:S(2)}) copy-start(f32[1024]{0:T(1024)} %param.19) | copy-start | bytes 12292
Sparse Core Ops, SparseCore 0:
  15.6 107.9 all-gather.1
  264.6 19.6 reduce-scatter.1

commit v5 on v4

--- a/solution.py
+++ b/solution.py
@@ -362,7 +362,13 @@
             w_plane,
         ]
     )
-    gathered = lax.all_gather(stacked, PAGES, axis=1, tiled=True)
+    planes = stacked.shape[0]
+    chip_rows = lax.all_gather(stacked, "core", axis=1, tiled=True)
+    my_planes = lax.dynamic_slice_in_dim(
+        chip_rows, lax.axis_index("core") * (planes // 2), planes // 2, axis=0
+    )
+    half = lax.all_gather(my_planes, "chips", axis=1, tiled=True)
+    gathered = lax.all_gather(half, "core", axis=0, tiled=True)
     my_slots = device_at * slot_count + jnp.arange(slot_count, dtype=jnp.int32)
     cached_hit = page_table.reshape(-1)[None, :] == my_slots[:, None]
     fresh_hit = append_slots.reshape(-1)[None, :] == my_slots[:, None]

time: 295 us -> 343 us (1.16)
  waiting for transfers between devices: 118 us -> 153 us
  blocking collectives: 73.6 us -> 85 us
    all_gather x1 -> x2, waiting for transfers between devices: 102 us -> 137 us  [the longest x1 107 us: per_device(): half = lax.all_gather(my_planes, 'chips', axis=1, tiled=True)]
    all_to_all x1, blocking collectives: 73.6 us -> 82.8 us  [per_device(): received = lax.all_to_all(paired, 'chips', 0, 0, tiled=True)]
    pallas_call x1, Pallas kernels: 19.9 us -> 28.5 us  [pair_merge(): pl.pallas_call(kernel, out_shape=jax.ShapeDtypeStruct((chips, rows_per, l...]
    pallas_call x1, Pallas kernels: 30.6 us -> 22.5 us  [local_attention(): pl.pallas_call(kernel, out_shape=(jax.ShapeDtypeStruct((chunks, rows_per,...]
  transfers between devices with their start and end apart: 2 -> 3, of which waited for: 2 -> 3; matrix products, arithmetic and copies ran while one was open for 3% -> 3% of each run, Pallas kernels for 0% -> 0%
where the time goes in v5:
time: 343 us; the launch traced here: 341 us
  waiting for transfers between devices  153 us (45%)
  blocking collectives  85 us (25%)
  Pallas kernels  60.8 us (18%)
  local copies, waits for them, and re-layouts  20.6 us (6%)
  between operations  13.9 us (4%)
  other arithmetic  6.98 us (2%)
    all_gather x1, waiting for transfers between devices, per_device(): half = lax.all_gather(my_planes, 'chips', axis=1, tiled=True)  107 us
    all_to_all x1, blocking collectives, per_device(): received = lax.all_to_all(paired, 'chips', 0, 0, tiled=True)  82.8 us
    all_gather x1, waiting for transfers between devices, per_device(): gathered = lax.all_gather(half, 'core', axis=0, tiled=True)  30.8 us
    pallas_call x1, Pallas kernels, pair_merge(): pl.pallas_call(kernel, out_shape=jax.ShapeDtypeStruct((chips, rows_per, l...  28.5 us
    pallas_call x1, Pallas kernels, local_attention(): pl.pallas_call(kernel, out_shape=(jax.ShapeDtypeStruct((chunks, rows_per,...  22.5 us
    reduce_scatter x1, waiting for transfers between devices, per_device(): lax.psum_scatter(projected, 'heads', scatter_dimension=1, tiled=True)  16.1 us
    pallas_call x1, Pallas kernels, combine_project(): pl.pallas_call(kernel, out_shape=jax.ShapeDtypeStruct((rows_per, tokens),...  9.79 us
  transfers between devices with their start and end apart: 3, of which 3 were waited for; matrix products, arithmetic and copies ran while one was open for 3% of the time, Pallas kernels for 0%

profile of v5, /device:TPU:4, one launch (start us, length us, event | category | flops | bytes accessed | tf_op | source)
XLA Modules:
  0.0 340.8 jit_solution(10538658709932569655)
XLA Ops:
  7.2 0.0 all-gather.3.cloned.1.call-start
  7.2 1.0 slice.25
  8.2 0.9 convert_element_type.43
  9.1 1.0 slice.28
  10.1 0.9 convert_element_type.46
  11.1 0.7 select_reduce_fusion
  11.8 0.9 stack_reshape.2
  12.7 0.8 pad_bitcast_fusion
  13.6 0.2 multiply_cosine_fusion
  13.8 0.3 subtract_convert_fusion.1
  14.1 0.3 pad_maximum_fusion.1
  14.6 2.2 all_gather.9
  16.8 0.7 constant_dynamic-slice_fusion
  17.5 0.0 all-gather.3.cloned.1.call-update
  17.6 0.0 all-gather.5.cloned.1.call-start
  17.6 106.6 %all-gather.3.cloned.1.call-done = bf16[2,4608,512]{2,1,0:T(8,128)(2,1)} async-done(((bf16[2,144,512]{2,1,0:T(8,128)(2,1)}), bf16[2,4608,512]{2,1,0:T(8,128)(2,1)}) %all-gather.3.cloned.1.call-update) | async-done | bytes 9437200 | tf_op jit(solution)/shard_map/all_gather | solution.py:370
  124.2 0.0 copy-start.6
  124.2 0.0 copy-start.7
  124.2 0.0 copy-start.1
  124.2 0.0 all-gather.5.cloned.1.call-update
  124.2 0.0 reduce-scatter.2.cloned.1.call-start
  124.3 0.6 copy-done.6
  124.9 0.1 eq.61
  125.0 0.0 copy-done.7
  125.0 0.1 eq.65
  125.0 0.6 copy-done.1
  125.6 0.0 copy-start.2
  125.6 2.0 reshape.154.kc_ref
  127.6 0.0 copy-done.2
  127.6 0.0 copy-start.10
  127.6 2.0 reshape.155.vc_ref
  129.6 0.2 fusion.1.sfresh_ref
  129.8 0.0 copy-start.8
  129.8 0.2 compare_reduce_fusion.1
  130.0 0.2 fusion
  130.2 0.5 broadcast_select_fusion
  130.7 0.0 copy-start.9
  130.7 0.0 copy-done.10
  130.7 0.1 select_reduce_fusion.1
  130.8 0.2 compare_reduce_fusion
  131.0 0.5 fusion.5.skind_ref
  131.5 30.8 %all-gather.5.cloned.1.call-done.q_ref.kf_ref.vf_ref.w_ref = bf16[4,4608,512]{2,1,0:T(8,128)(2,1)} async-done(((bf16[2,4608,512]{2,1,0:T(8,128)(2,1)}), bf16[4,4608,512]{2,1,0:T(8,128)(2,1)}) %all-gather.5.cloned.1.call-update) | async-done | bytes 18874384 | tf_op jit(solution)/shard_map/all_gather | solution.py:371
  162.3 0.0 copy-done.8
  162.3 0.0 copy-done.9
  162.3 22.5 %shard_map.121 = (bf16[64,72,640]{2,1,0:T(8,128)(2,1)}, bf16[12,128,512]{2,1,0:T(8,128)(2,1)}, bf16[12,128,512]{2,1,0:T(8,128)(2,1)}) custom-call(s32[12]{0:T(128)} %copy-done.9, s32[12]{0:T(128)} %fusion.5.skind_ref, s32[12]{0:T(128)} %get-tuple-element.9.slim_ref, s32[12]{0:T(128)} %copy-done.8, ...), custom_call_target="tpu_custom_call" | custom-call | flops 2415919104 | bytes 16908288 | tf_op jit(solution)/shard_map/pallas_call | solution.py:135
  184.8 0.0 copy-start
  184.8 2.7 copy-done
  187.4 28.5 %shard_map.122 = bf16[32,72,640]{2,1,0:T(8,128)(2,1)S(1)} custom-call(bf16[32,2,72,640]{3,2,1,0:T(8,128)(2,1)S(1)} %bitcast.5), custom_call_target="tpu_custom_call" | custom-call | flops 8847360 | bytes 8847360 | tf_op jit(solution)/shard_map/pallas_call | solution.py:302
  215.9 82.8 %all_to_all.5.recv_ref = bf16[32,72,640]{2,1,0:T(8,128)(2,1)S(1)} all-to-all(bf16[32,72,640]{2,1,0:T(8,128)(2,1)S(1)} %shard_map.122), channel_id=1, replica_groups=mesh['heads'=4,'chips'=32,'core'=2] {'chips'}, dimensions={0} | all-to-all | bytes 5898240 | tf_op jit(solution)/shard_map/all_to_all | solution.py:406
  298.7 9.8 %shard_map.123 = bf16[72,4608]{1,0:T(8,128)(2,1)S(1)} custom-call(bf16[32,72,640]{2,1,0:T(8,128)(2,1)S(1)} %all_to_all.5.recv_ref, bf16[4,4608,512]{2,1,0:T(8,128)(2,1)} %all-gather.5.cloned.1.call-done.q_ref.kf_ref.vf_ref.w_ref), custom_call_target="tpu_custom_call" | custom-call | flops 345636864 | bytes 8331264 | tf_op jit(solution)/shard_map/pallas_call | solution.py:214
  308.5 2.6 reshape.157
  311.1 0.0 copy-start.4
  311.1 1.7 reshape.158
  312.9 0.0 reduce-scatter.2.cloned.1.call-update
  312.9 0.0 copy-done.4
  312.9 0.0 copy-start.3
  312.9 1.9 reshape.159
  314.8 0.0 copy-done.3
  314.8 0.0 copy-start.5
  314.8 1.8 reshape.160
  316.6 16.1 %reduce-scatter.2.cloned.1.call-done = bf16[72,1024]{1,0:T(8,128)(2,1)} async-done(((bf16[72,4096]{1,0:T(8,128)(2,1)}), bf16[72,1024]{1,0:T(8,128)(2,1)}) %reduce-scatter.2.cloned.1.call-update) | async-done | bytes 147472 | tf_op jit(solution)/shard_map/reduce_scatter | solution.py:413
  332.7 0.0 copy-done.5
  332.7 1.6 add_convert_fusion
  (7 shorter events, 0.2 us)
Async XLA Ops:
  7.2 117.0 %all-gather.3.cloned.1.call-start = ((), (), s32[]{:S(2)}) async-start(), calls=%async_computation.2 | async-start | bytes 9732096 | tf_op jit(solution)/shard_map/all_gather | solution.py:370
  17.6 144.7 %all-gather.5.cloned.1.call-start = ((), (), s32[]{:S(2)}) async-start(), calls=%async_computation.3 | async-start | bytes 28311552 | tf_op jit(solution)/shard_map/all_gather | solution.py:371
  124.2 0.7 copy-start.6
  124.2 0.8 copy-start.7
  124.2 1.4 copy-start.1
  124.2 208.5 %reduce-scatter.2.cloned.1.call-start = ((), (), s32[]{:S(2)}) async-start(), calls=%async_computation.4 | async-start | bytes 737280 | tf_op jit(solution)/shard_map/reduce_scatter | solution.py:413
  125.6 2.0 copy-start.2
  127.6 3.1 copy-start.10
  129.8 32.5 %copy-start.8 = (s32[12]{0:T(128)}, s32[12]{0:T(128)S(1)}, u32[]{:S(2)}) copy-start(s32[12]{0:T(128)S(1)} %fusion.1.sfresh_ref) | copy-start | bytes 148
  130.7 31.6 %copy-start.9 = (s32[12]{0:T(128)}, s32[12]{0:T(128)S(1)}, u32[]{:S(2)}) copy-start(s32[12]{0:T(128)S(1)} %get-tuple-element.17.sreq_ref) | copy-start | bytes 148
  184.8 2.7 copy-start
  311.1 1.8 copy-start.4
  312.9 1.9 copy-start.3
  314.8 17.9 %copy-start.5 = (f32[1024]{0:T(1024)S(1)}, f32[1024]{0:T(1024)}, u32[]{:S(2)}) copy-start(f32[1024]{0:T(1024)} %param.19) | copy-start | bytes 12292
Sparse Core Ops, SparseCore 0:
  17.7 106.4 all-gather.2
  126.0 36.2 all-gather.4
  313.0 19.6 reduce-scatter.1

commit v6 on v4

--- a/solution.py
+++ b/solution.py
@@ -56,11 +56,12 @@
     limit = slim_ref[step]
     scale = 1.0 / math.sqrt(head_dim)
 
-    def attend(k_ref, v_ref):
+    def attend(k_ref, v_ref, masked):
         base = pl.multiple_of(request * span, span)
-        rows = lax.broadcasted_iota(jnp.int32, (span, PAGE), 0)
-        cols = lax.broadcasted_iota(jnp.int32, (span, PAGE), 1)
-        allowed = rows - cols >= limit
+        if masked:
+            rows = lax.broadcasted_iota(jnp.int32, (span, PAGE), 0)
+            cols = lax.broadcasted_iota(jnp.int32, (span, PAGE), 1)
+            allowed = rows - cols >= limit
         lane = lax.broadcasted_iota(jnp.int32, (span, lanes), 1)
         ml = ml_ref[pl.ds(base, span), :]
         for h in range(heads):
@@ -71,13 +72,16 @@
             scores = lax.dot_general(
                 q_h, k_h, (((1,), (1,)), ((), ())), preferred_element_type=jnp.float32
             ) * scale
-            scores = jnp.where(allowed, scores, mask_score)
+            if masked:
+                scores = jnp.where(allowed, scores, mask_score)
             m_prev = ml[:, h : h + 1]
             l_prev = ml[:, heads + h : heads + h + 1]
             m_new = jnp.maximum(m_prev, jnp.max(scores, axis=1, keepdims=True))
             m_new = m_new.astype(jnp.bfloat16).astype(jnp.float32)
             alpha = jnp.exp(m_prev - m_new)
-            weights = jnp.where(allowed, jnp.exp(scores - m_new), 0.0)
+            weights = jnp.exp(scores - m_new)
+            if masked:
+                weights = jnp.where(allowed, weights, 0.0)
             l_new = alpha * l_prev + jnp.sum(weights, axis=1, keepdims=True)
             contrib = jnp.dot(
                 weights.astype(jnp.bfloat16), v_h, preferred_element_type=jnp.float32
@@ -92,11 +96,11 @@
 
     @pl.when(kind == 1)
     def _cached():
-        attend(kc_ref, vc_ref)
+        attend(kc_ref, vc_ref, False)
 
     @pl.when(kind == 2)
     def _fresh():
-        attend(kf_ref, vf_ref)
+        attend(kf_ref, vf_ref, True)
 
     @pl.when(kind == 2)
     def _store_fresh():

time: 295 us -> 301 us (1.020)
  Pallas kernels: 60.3 us -> 64 us
    pallas_call x1, Pallas kernels: 30.6 us -> 38.2 us  [local_attention(): pl.pallas_call(kernel, out_shape=(jax.ShapeDtypeStruct((chunks, rows_per,...]
    pallas_call x1, Pallas kernels: 19.9 us -> 16 us  [pair_merge(): pl.pallas_call(kernel, out_shape=jax.ShapeDtypeStruct((chips, rows_per, l...]
where the time goes in v6:
time: 301 us; the launch traced here: 299 us
  waiting for transfers between devices  118 us (39%)
  blocking collectives  76.2 us (25%)
  Pallas kernels  64 us (21%)
  local copies, waits for them, and re-layouts  18.7 us (6%)
  between operations  14.2 us (5%)
  other arithmetic  7.81 us (3%)
    all_gather x1, waiting for transfers between devices, per_device(): gathered = lax.all_gather(stacked, PAGES, axis=1, tiled=True)  102 us
    all_to_all x1, blocking collectives, per_device(): received = lax.all_to_all(paired, 'chips', 0, 0, tiled=True)  76.2 us
    pallas_call x1, Pallas kernels, local_attention(): pl.pallas_call(kernel, out_shape=(jax.ShapeDtypeStruct((chunks, rows_per,...  38.2 us
    reduce_scatter x1, waiting for transfers between devices, per_device(): lax.psum_scatter(projected, 'heads', scatter_dimension=1, tiled=True)  16.1 us
    pallas_call x1, Pallas kernels, pair_merge(): pl.pallas_call(kernel, out_shape=jax.ShapeDtypeStruct((chips, rows_per, l...  16 us
    pallas_call x1, Pallas kernels, combine_project(): pl.pallas_call(kernel, out_shape=jax.ShapeDtypeStruct((rows_per, tokens),...  9.8 us
  transfers between devices with their start and end apart: 2, of which 2 were waited for; matrix products, arithmetic and copies ran while one was open for 3% of the time, Pallas kernels for 0%

profile of v6, /device:TPU:4, one launch (start us, length us, event | category | flops | bytes accessed | tf_op | source)
XLA Modules:
  0.0 299.1 jit_solution(4160148452153426439)
XLA Ops:
  7.2 0.0 all-gather.2.cloned.1.call-start
  7.2 1.0 slice.25
  8.2 0.9 convert_element_type.43
  9.1 1.0 slice.28
  10.1 0.9 convert_element_type.46
  11.0 0.0 copy-start.6
  11.1 0.0 copy-start.7
  11.1 0.0 copy-start.1
  11.1 0.9 select_reduce_fusion
  12.0 0.9 stack_reshape.2
  12.9 0.8 pad_bitcast_fusion
  13.7 0.2 multiply_cosine_fusion
  14.0 0.3 subtract_convert_fusion.1
  14.3 0.3 pad_maximum_fusion.1
  14.7 0.8 pad_maximum_fusion
  15.5 0.0 all-gather.2.cloned.1.call-update
  15.5 0.0 reduce-scatter.2.cloned.1.call-start
  15.5 0.0 copy-done.6
  15.5 0.1 eq.61
  15.6 0.0 copy-done.7
  15.6 0.1 eq.65
  15.7 0.0 copy-done.1
  15.7 0.0 copy-start.2
  15.7 2.0 reshape.154.kc_ref
  17.7 0.0 copy-done.2
  17.7 0.0 copy-start.10
  17.7 2.0 reshape.155.vc_ref
  19.7 0.2 fusion.1.sfresh_ref
  19.9 0.0 copy-start.8
  19.9 0.2 compare_reduce_fusion.1
  20.1 0.2 fusion
  20.3 0.5 broadcast_select_fusion
  20.8 0.0 copy-start.9
  20.8 0.0 copy-done.10
  20.8 0.1 select_reduce_fusion.1
  20.9 0.2 compare_reduce_fusion
  21.1 0.5 fusion.5.skind_ref
  21.6 102.0 %all-gather.2.cloned.1.call-done.q_ref.kf_ref.vf_ref.w_ref = bf16[4,4608,512]{2,1,0:T(8,128)(2,1)} async-done(((bf16[4,72,512]{2,1,0:T(8,128)(2,1)}), bf16[4,4608,512]{2,1,0:T(8,128)(2,1)}) %all-gather.2.cloned.1.call-update) | async-done | bytes 18874384 | tf_op jit(solution)/shard_map/all_gather | solution.py:369
  123.6 0.0 copy-done.8
  123.6 0.0 copy-done.9
  123.6 38.2 %shard_map.121 = (bf16[64,72,640]{2,1,0:T(8,128)(2,1)}, bf16[12,128,512]{2,1,0:T(8,128)(2,1)}, bf16[12,128,512]{2,1,0:T(8,128)(2,1)}) custom-call(s32[12]{0:T(128)} %copy-done.9, s32[12]{0:T(128)} %fusion.5.skind_ref, s32[12]{0:T(128)} %get-tuple-element.9.slim_ref, s32[12]{0:T(128)} %copy-done.8, ...), custom_call_target="tpu_custom_call" | custom-call | flops 2415919104 | bytes 16908288 | tf_op jit(solution)/shard_map/pallas_call | solution.py:139
  161.8 0.0 copy-start
  161.8 2.7 copy-done
  164.4 16.0 %shard_map.122 = bf16[32,72,640]{2,1,0:T(8,128)(2,1)S(1)} custom-call(bf16[32,2,72,640]{3,2,1,0:T(8,128)(2,1)S(1)} %bitcast.5), custom_call_target="tpu_custom_call" | custom-call | flops 8847360 | bytes 8847360 | tf_op jit(solution)/shard_map/pallas_call | solution.py:306
  180.4 76.2 %all_to_all.5.recv_ref = bf16[32,72,640]{2,1,0:T(8,128)(2,1)S(1)} all-to-all(bf16[32,72,640]{2,1,0:T(8,128)(2,1)S(1)} %shard_map.122), channel_id=1, replica_groups=mesh['heads'=4,'chips'=32,'core'=2] {'chips'}, dimensions={0} | all-to-all | bytes 5898240 | tf_op jit(solution)/shard_map/all_to_all | solution.py:404
  256.6 9.8 %shard_map.123 = bf16[72,4608]{1,0:T(8,128)(2,1)S(1)} custom-call(bf16[32,72,640]{2,1,0:T(8,128)(2,1)S(1)} %all_to_all.5.recv_ref, bf16[4,4608,512]{2,1,0:T(8,128)(2,1)} %all-gather.2.cloned.1.call-done.q_ref.kf_ref.vf_ref.w_ref), custom_call_target="tpu_custom_call" | custom-call | flops 345636864 | bytes 8331264 | tf_op jit(solution)/shard_map/pallas_call | solution.py:218
  266.4 2.6 reshape.157
  269.1 0.0 copy-start.4
  269.1 1.7 reshape.158
  270.8 0.0 reduce-scatter.2.cloned.1.call-update
  270.8 0.0 copy-done.4
  270.8 0.0 copy-start.3
  270.9 1.9 reshape.159
  272.7 0.0 copy-done.3
  272.7 0.0 copy-start.5
  272.7 1.8 reshape.160
  274.6 16.1 %reduce-scatter.2.cloned.1.call-done = bf16[72,1024]{1,0:T(8,128)(2,1)} async-done(((bf16[72,4096]{1,0:T(8,128)(2,1)}), bf16[72,1024]{1,0:T(8,128)(2,1)}) %reduce-scatter.2.cloned.1.call-update) | async-done | bytes 147472 | tf_op jit(solution)/shard_map/reduce_scatter | solution.py:411
  290.7 0.0 copy-done.5
  290.7 1.6 add_convert_fusion
  (6 shorter events, 0.1 us)
Async XLA Ops:
  7.2 116.4 %all-gather.2.cloned.1.call-start = ((), (), s32[]{:S(2)}) async-start(), calls=%async_computation.2 | async-start | bytes 19169280 | tf_op jit(solution)/shard_map/all_gather | solution.py:369
  11.0 4.5 %copy-start.6 = (s32[6,6]{1,0:T(8,128)S(1)}, s32[6,6]{1,0:T(8,128)}, u32[]{:S(2)}) copy-start(s32[6,6]{1,0:T(8,128)} %param.17) | copy-start | bytes 436
  11.1 4.6 %copy-start.7 = (s32[6,122]{1,0:T(8,128)S(1)}, s32[6,122]{1,0:T(8,128)}, u32[]{:S(2)}) copy-start(s32[6,122]{1,0:T(8,128)} %param.16) | copy-start | bytes 8788
  11.1 4.6 %copy-start.1 = (bf16[12,128,4,128]{3,2,1,0:T(4,128)(2,1)S(1)}, bf16[12,128,4,128]{3,2,1,0:T(4,128)(2,1)}, u32[]{:S(2)}) copy-start(bf16[12,128,4,128]{3,2,1,0:T(4,128)(2,1)} %param.13) | copy-start | bytes 4718596
  15.5 275.2 %reduce-scatter.2.cloned.1.call-start = ((), (), s32[]{:S(2)}) async-start(), calls=%async_computation.3 | async-start | bytes 737280 | tf_op jit(solution)/shard_map/reduce_scatter | solution.py:411
  15.7 2.0 copy-start.2
  17.7 3.1 %copy-start.10 = (s32[6]{0:T(128)S(1)}, s32[6]{0:T(128)}, u32[]{:S(2)}) copy-start(s32[6]{0:T(128)} %param.15) | copy-start | bytes 76
  19.9 103.7 %copy-start.8 = (s32[12]{0:T(128)}, s32[12]{0:T(128)S(1)}, u32[]{:S(2)}) copy-start(s32[12]{0:T(128)S(1)} %fusion.1.sfresh_ref) | copy-start | bytes 148
  20.8 102.8 %copy-start.9 = (s32[12]{0:T(128)}, s32[12]{0:T(128)S(1)}, u32[]{:S(2)}) copy-start(s32[12]{0:T(128)S(1)} %get-tuple-element.17.sreq_ref) | copy-start | bytes 148
  161.8 2.7 copy-start
  269.1 1.8 copy-start.4
  270.8 1.9 copy-start.3
  272.7 17.9 %copy-start.5 = (f32[1024]{0:T(1024)S(1)}, f32[1024]{0:T(1024)}, u32[]{:S(2)}) copy-start(f32[1024]{0:T(1024)} %param.19) | copy-start | bytes 12292
Sparse Core Ops, SparseCore 0:
  15.6 107.9 all-gather.1
  271.0 19.6 reduce-scatter.1

commit v7 on v6

--- a/solution.py
+++ b/solution.py
@@ -39,7 +39,7 @@
     heads, head_dim, requests, span,
     sreq_ref, skind_ref, slim_ref, sfresh_ref,
     q_ref, kf_ref, vf_ref, kc_ref, vc_ref,
-    out_ref, ko_ref, vo_ref, acc_ref, ml_ref,
+    out_ref, ko_ref, vo_ref, acc_t, stats, tok_ref, ml_ref,
 ):
     step = pl.program_id(0)
     lanes = ml_ref.shape[1]
@@ -47,9 +47,9 @@
 
     @pl.when(step == 0)
     def _init():
-        acc_ref[...] = jnp.zeros_like(acc_ref)
-        lane = lax.broadcasted_iota(jnp.int32, ml_ref.shape, 1)
-        ml_ref[...] = jnp.where(lane < heads, mask_score, 0.0).astype(jnp.float32)
+        acc_t[...] = jnp.zeros_like(acc_t)
+        row = lax.broadcasted_iota(jnp.int32, stats.shape, 1)
+        stats[...] = jnp.where(row < heads, mask_score, 0.0).astype(jnp.float32)
 
     request = sreq_ref[step]
     kind = skind_ref[step]
@@ -59,40 +59,36 @@
     def attend(k_ref, v_ref, masked):
         base = pl.multiple_of(request * span, span)
         if masked:
-            rows = lax.broadcasted_iota(jnp.int32, (span, PAGE), 0)
-            cols = lax.broadcasted_iota(jnp.int32, (span, PAGE), 1)
-            allowed = rows - cols >= limit
-        lane = lax.broadcasted_iota(jnp.int32, (span, lanes), 1)
-        ml = ml_ref[pl.ds(base, span), :]
+            keys_at = lax.broadcasted_iota(jnp.int32, (PAGE, span), 0)
+            queries_at = lax.broadcasted_iota(jnp.int32, (PAGE, span), 1)
+            allowed = queries_at - keys_at >= limit
+        v_t = v_ref[0].astype(jnp.float32).T.astype(jnp.bfloat16)
         for h in range(heads):
             cut = slice(h * head_dim, (h + 1) * head_dim)
             q_h = q_ref[0, pl.ds(base, span), cut]
             k_h = k_ref[0, :, cut]
-            v_h = v_ref[0, :, cut]
             scores = lax.dot_general(
-                q_h, k_h, (((1,), (1,)), ((), ())), preferred_element_type=jnp.float32
+                k_h, q_h, (((1,), (1,)), ((), ())), preferred_element_type=jnp.float32
             ) * scale
             if masked:
                 scores = jnp.where(allowed, scores, mask_score)
-            m_prev = ml[:, h : h + 1]
-            l_prev = ml[:, heads + h : heads + h + 1]
-            m_new = jnp.maximum(m_prev, jnp.max(scores, axis=1, keepdims=True))
+            m_prev = stats[request, h : h + 1, :]
+            l_prev = stats[request, heads + h : heads + h + 1, :]
+            m_new = jnp.maximum(m_prev, jnp.max(scores, axis=0, keepdims=True))
             m_new = m_new.astype(jnp.bfloat16).astype(jnp.float32)
             alpha = jnp.exp(m_prev - m_new)
             weights = jnp.exp(scores - m_new)
             if masked:
                 weights = jnp.where(allowed, weights, 0.0)
-            l_new = alpha * l_prev + jnp.sum(weights, axis=1, keepdims=True)
+            l_new = alpha * l_prev + jnp.sum(weights, axis=0, keepdims=True)
             contrib = jnp.dot(
-                weights.astype(jnp.bfloat16), v_h, preferred_element_type=jnp.float32
+                v_t[cut, :], weights.astype(jnp.bfloat16), preferred_element_type=jnp.float32
             )
-            acc_ref[pl.ds(base, span), cut] = alpha * acc_ref[pl.ds(base, span), cut] + contrib
-            ml = jnp.where(
-                lane == h,
-                m_new,
-                jnp.where((lane == heads + h) | (lane == 2 * heads + h), l_new, ml),
-            )
-        ml_ref[pl.ds(base, span), :] = ml
+            slot = request * heads + h
+            acc_t[slot] = alpha * acc_t[slot] + contrib
+            stats[request, h : h + 1, :] = m_new
+            stats[request, heads + h : heads + h + 1, :] = l_new
+            stats[request, 2 * heads + h : 2 * heads + h + 1, :] = l_new
 
     @pl.when(kind == 1)
     def _cached():
@@ -114,11 +110,20 @@
 
     @pl.when(step == pl.num_programs(0) - 1)
     def _emit():
+        stat_rows = stats.shape[1]
+        for r in range(requests):
+            rows = pl.ds(r * span, span)
+            for h in range(heads):
+                tok_ref[rows, h * head_dim : (h + 1) * head_dim] = acc_t[r * heads + h].T
+            block = jnp.concatenate(
+                [stats[r], jnp.zeros((lanes - stat_rows, span), jnp.float32)], axis=0
+            )
+            ml_ref[rows, :] = block.T
         chunks, rows_per, _ = out_ref.shape
         lane = lax.broadcasted_iota(jnp.int32, (rows_per, lanes), 1)
         for d in range(chunks):
             rows = pl.ds(d * rows_per, rows_per)
-            out_ref[d, :, :width] = acc_ref[rows, :].astype(jnp.bfloat16)
+            out_ref[d, :, :width] = tok_ref[rows, :].astype(jnp.bfloat16)
             ml = ml_ref[rows, :]
             rounded = ml.astype(jnp.bfloat16).astype(jnp.float32)
             packed = jnp.where(
@@ -160,12 +165,14 @@
                 pl.BlockSpec((1, PAGE, width), lambda s, *_: (s, 0, 0)),
             ],
             scratch_shapes=[
+                pltpu.VMEM((requests * heads, head_dim, span), jnp.float32),
+                pltpu.VMEM((requests, 16, span), jnp.float32),
                 pltpu.VMEM((tokens, width), jnp.float32),
                 pltpu.VMEM((tokens, 128), jnp.float32),
             ],
         ),
         compiler_params=pltpu.CompilerParams(
-            dimension_semantics=("arbitrary",), vmem_limit_bytes=60 * 1024 * 1024
+            dimension_semantics=("arbitrary",), vmem_limit_bytes=62 * 1024 * 1024
         ),
         cost_estimate=pl.CostEstimate(
             flops=flops,

time: 301 us -> 287 us (0.953)
  Pallas kernels: 64 us -> 50 us
    pallas_call x1, Pallas kernels: 38.2 us -> 24.3 us  [local_attention(): pl.pallas_call(kernel, out_shape=(jax.ShapeDtypeStruct((chunks, rows_per,...]
where the time goes in v7:
time: 287 us; the launch traced here: 284 us
  waiting for transfers between devices  118 us (41%)
  blocking collectives  75.5 us (26%)
  Pallas kernels  50 us (17%)
  local copies, waits for them, and re-layouts  18.7 us (7%)
  between operations  14.2 us (5%)
  other arithmetic  7.81 us (3%)
    all_gather x1, waiting for transfers between devices, per_device(): gathered = lax.all_gather(stacked, PAGES, axis=1, tiled=True)  102 us
    all_to_all x1, blocking collectives, per_device(): received = lax.all_to_all(paired, 'chips', 0, 0, tiled=True)  75.5 us
    pallas_call x1, Pallas kernels, local_attention(): pl.pallas_call(kernel, out_shape=(jax.ShapeDtypeStruct((chunks, rows_per,...  24.3 us
    reduce_scatter x1, waiting for transfers between devices, per_device(): lax.psum_scatter(projected, 'heads', scatter_dimension=1, tiled=True)  16.1 us
    pallas_call x1, Pallas kernels, pair_merge(): pl.pallas_call(kernel, out_shape=jax.ShapeDtypeStruct((chips, rows_per, l...  16 us
    pallas_call x1, Pallas kernels, combine_project(): pl.pallas_call(kernel, out_shape=jax.ShapeDtypeStruct((rows_per, tokens),...  9.8 us
  transfers between devices with their start and end apart: 2, of which 2 were waited for; matrix products, arithmetic and copies ran while one was open for 3% of the time, Pallas kernels for 0%

profile of v7, /device:TPU:4, one launch (start us, length us, event | category | flops | bytes accessed | tf_op | source)
XLA Modules:
  0.0 284.4 jit_solution(17359663857146297694)
XLA Ops:
  7.2 0.0 all-gather.2.cloned.1.call-start
  7.2 1.0 slice.25
  8.2 0.9 convert_element_type.43
  9.1 1.0 slice.28
  10.1 0.9 convert_element_type.46
  11.0 0.0 copy-start.6
  11.1 0.0 copy-start.7
  11.1 0.0 copy-start.1
  11.1 0.9 select_reduce_fusion
  12.0 0.9 stack_reshape.2
  12.9 0.8 pad_bitcast_fusion
  13.7 0.2 multiply_cosine_fusion
  14.0 0.3 subtract_convert_fusion.1
  14.3 0.3 pad_maximum_fusion.1
  14.7 0.8 pad_maximum_fusion
  15.5 0.0 all-gather.2.cloned.1.call-update
  15.5 0.0 reduce-scatter.2.cloned.1.call-start
  15.5 0.0 copy-done.6
  15.5 0.1 eq.61
  15.6 0.0 copy-done.7
  15.6 0.1 eq.65
  15.7 0.0 copy-done.1
  15.7 0.0 copy-start.2
  15.7 2.0 reshape.154.kc_ref
  17.7 0.0 copy-done.2
  17.7 0.0 copy-start.10
  17.7 2.0 reshape.155.vc_ref
  19.7 0.2 fusion.1.sfresh_ref
  19.9 0.0 copy-start.8
  19.9 0.2 compare_reduce_fusion.1
  20.1 0.2 fusion
  20.3 0.5 broadcast_select_fusion
  20.8 0.0 copy-start.9
  20.8 0.0 copy-done.10
  20.8 0.1 select_reduce_fusion.1
  20.9 0.2 compare_reduce_fusion
  21.1 0.5 fusion.5.skind_ref
  21.6 102.0 %all-gather.2.cloned.1.call-done.q_ref.kf_ref.vf_ref.w_ref = bf16[4,4608,512]{2,1,0:T(8,128)(2,1)} async-done(((bf16[4,72,512]{2,1,0:T(8,128)(2,1)}), bf16[4,4608,512]{2,1,0:T(8,128)(2,1)}) %all-gather.2.cloned.1.call-update) | async-done | bytes 18874384 | tf_op jit(solution)/shard_map/all_gather | solution.py:376
  123.6 0.0 copy-done.8
  123.6 0.0 copy-done.9
  123.6 24.3 %shard_map.121 = (bf16[64,72,640]{2,1,0:T(8,128)(2,1)}, bf16[12,128,512]{2,1,0:T(8,128)(2,1)}, bf16[12,128,512]{2,1,0:T(8,128)(2,1)}) custom-call(s32[12]{0:T(128)} %copy-done.9, s32[12]{0:T(128)} %fusion.5.skind_ref, s32[12]{0:T(128)} %get-tuple-element.9.slim_ref, s32[12]{0:T(128)} %copy-done.8, ...), custom_call_target="tpu_custom_call" | custom-call | flops 2415919104 | bytes 16908288 | tf_op jit(solution)/shard_map/pallas_call | solution.py:144
  147.8 0.0 copy-start
  147.8 2.7 copy-done
  150.5 16.0 %shard_map.122 = bf16[32,72,640]{2,1,0:T(8,128)(2,1)S(1)} custom-call(bf16[32,2,72,640]{3,2,1,0:T(8,128)(2,1)S(1)} %bitcast.5), custom_call_target="tpu_custom_call" | custom-call | flops 8847360 | bytes 8847360 | tf_op jit(solution)/shard_map/pallas_call | solution.py:313
  166.5 75.5 %all_to_all.5.recv_ref = bf16[32,72,640]{2,1,0:T(8,128)(2,1)S(1)} all-to-all(bf16[32,72,640]{2,1,0:T(8,128)(2,1)S(1)} %shard_map.122), channel_id=1, replica_groups=mesh['heads'=4,'chips'=32,'core'=2] {'chips'}, dimensions={0} | all-to-all | bytes 5898240 | tf_op jit(solution)/shard_map/all_to_all | solution.py:411
  242.0 9.8 %shard_map.123 = bf16[72,4608]{1,0:T(8,128)(2,1)S(1)} custom-call(bf16[32,72,640]{2,1,0:T(8,128)(2,1)S(1)} %all_to_all.5.recv_ref, bf16[4,4608,512]{2,1,0:T(8,128)(2,1)} %all-gather.2.cloned.1.call-done.q_ref.kf_ref.vf_ref.w_ref), custom_call_target="tpu_custom_call" | custom-call | flops 345636864 | bytes 8331264 | tf_op jit(solution)/shard_map/pallas_call | solution.py:225
  251.8 2.6 reshape.157
  254.4 0.0 copy-start.4
  254.5 1.7 reshape.158
  256.2 0.0 reduce-scatter.2.cloned.1.call-update
  256.2 0.0 copy-done.4
  256.2 0.0 copy-start.3
  256.2 1.9 reshape.159
  258.1 0.0 copy-done.3
  258.1 0.0 copy-start.5
  258.1 1.8 reshape.160
  259.9 16.1 %reduce-scatter.2.cloned.1.call-done = bf16[72,1024]{1,0:T(8,128)(2,1)} async-done(((bf16[72,4096]{1,0:T(8,128)(2,1)}), bf16[72,1024]{1,0:T(8,128)(2,1)}) %reduce-scatter.2.cloned.1.call-update) | async-done | bytes 147472 | tf_op jit(solution)/shard_map/reduce_scatter | solution.py:418
  276.0 0.0 copy-done.5
  276.0 1.6 add_convert_fusion
  (6 shorter events, 0.1 us)
Async XLA Ops:
  7.2 116.4 %all-gather.2.cloned.1.call-start = ((), (), s32[]{:S(2)}) async-start(), calls=%async_computation.2 | async-start | bytes 19169280 | tf_op jit(solution)/shard_map/all_gather | solution.py:376
  11.0 4.5 %copy-start.6 = (s32[6,6]{1,0:T(8,128)S(1)}, s32[6,6]{1,0:T(8,128)}, u32[]{:S(2)}) copy-start(s32[6,6]{1,0:T(8,128)} %param.17) | copy-start | bytes 436
  11.1 4.6 %copy-start.7 = (s32[6,122]{1,0:T(8,128)S(1)}, s32[6,122]{1,0:T(8,128)}, u32[]{:S(2)}) copy-start(s32[6,122]{1,0:T(8,128)} %param.16) | copy-start | bytes 8788
  11.1 4.6 %copy-start.1 = (bf16[12,128,4,128]{3,2,1,0:T(4,128)(2,1)S(1)}, bf16[12,128,4,128]{3,2,1,0:T(4,128)(2,1)}, u32[]{:S(2)}) copy-start(bf16[12,128,4,128]{3,2,1,0:T(4,128)(2,1)} %param.13) | copy-start | bytes 4718596
  15.5 260.5 %reduce-scatter.2.cloned.1.call-start = ((), (), s32[]{:S(2)}) async-start(), calls=%async_computation.3 | async-start | bytes 737280 | tf_op jit(solution)/shard_map/reduce_scatter | solution.py:418
  15.7 2.0 copy-start.2
  17.7 3.1 %copy-start.10 = (s32[6]{0:T(128)S(1)}, s32[6]{0:T(128)}, u32[]{:S(2)}) copy-start(s32[6]{0:T(128)} %param.15) | copy-start | bytes 76
  19.9 103.7 %copy-start.8 = (s32[12]{0:T(128)}, s32[12]{0:T(128)S(1)}, u32[]{:S(2)}) copy-start(s32[12]{0:T(128)S(1)} %fusion.1.sfresh_ref) | copy-start | bytes 148
  20.8 102.8 %copy-start.9 = (s32[12]{0:T(128)}, s32[12]{0:T(128)S(1)}, u32[]{:S(2)}) copy-start(s32[12]{0:T(128)S(1)} %get-tuple-element.17.sreq_ref) | copy-start | bytes 148
  147.8 2.7 copy-start
  254.4 1.8 copy-start.4
  256.2 1.9 copy-start.3
  258.1 17.9 %copy-start.5 = (f32[1024]{0:T(1024)S(1)}, f32[1024]{0:T(1024)}, u32[]{:S(2)}) copy-start(f32[1024]{0:T(1024)} %param.19) | copy-start | bytes 12292
Sparse Core Ops, SparseCore 0:
  15.6 107.9 all-gather.1
  256.3 19.6 reduce-scatter.1

commit v8 on v7

--- a/solution.py
+++ b/solution.py
@@ -333,6 +333,66 @@
     )(view)
 
 
+def heads_sum_kernel(groups, block, proj_hbm, out_ref, own, received, own_sem, send_sems, recv_sems):
+    group = lax.axis_index("heads")
+    barrier = pltpu.get_barrier_semaphore()
+    for k in range(1, groups):
+        pl.semaphore_signal(
+            barrier, inc=1, device_id={"heads": lax.rem(group + k, groups)},
+            device_id_type=pl.DeviceIdType.MESH,
+        )
+    pl.semaphore_wait(barrier, groups - 1)
+    local = pltpu.make_async_copy(
+        proj_hbm.at[:, pl.ds(pl.multiple_of(group * block, 128), block)], own, own_sem
+    )
+    local.start()
+    copies = []
+    for k in range(1, groups):
+        dest = lax.rem(group + k, groups)
+        copy = pltpu.make_async_remote_copy(
+            src_ref=proj_hbm.at[:, pl.ds(pl.multiple_of(dest * block, 128), block)],
+            dst_ref=received.at[k - 1],
+            send_sem=send_sems.at[k - 1],
+            recv_sem=recv_sems.at[k - 1],
+            device_id={"heads": dest},
+            device_id_type=pl.DeviceIdType.MESH,
+        )
+        copy.start()
+        copies.append(copy)
+    local.wait()
+    for copy in copies:
+        copy.wait()
+    total = own[...].astype(jnp.float32)
+    for k in range(groups - 1):
+        total = total + received[k].astype(jnp.float32)
+    out_ref[...] = total
+
+
+def heads_sum(projected, groups):
+    rows, cols = projected.shape
+    block = cols // groups
+    kernel = functools.partial(heads_sum_kernel, groups, block)
+    return pl.pallas_call(
+        kernel,
+        out_shape=jax.ShapeDtypeStruct((rows, block), jnp.float32),
+        in_specs=[pl.BlockSpec(memory_space=pl.ANY)],
+        out_specs=pl.BlockSpec(memory_space=pltpu.VMEM),
+        scratch_shapes=[
+            pltpu.VMEM((rows, block), projected.dtype),
+            pltpu.VMEM((groups - 1, rows, block), projected.dtype),
+            pltpu.SemaphoreType.DMA(()),
+            pltpu.SemaphoreType.DMA((groups - 1,)),
+            pltpu.SemaphoreType.DMA((groups - 1,)),
+        ],
+        compiler_params=pltpu.CompilerParams(collective_id=1, has_side_effects=True),
+        cost_estimate=pl.CostEstimate(
+            flops=groups * rows * block,
+            transcendentals=0,
+            bytes_accessed=groups * rows * block * 2 + rows * block * 4,
+        ),
+    )(projected)
+
+
 def per_device(
     queries,
     keys,
@@ -410,12 +470,13 @@
     paired = pair_merge(packed, head_count, head_dim)
     received = lax.all_to_all(paired, "chips", 0, 0, tiled=True)
     projected = combine_project(received, gathered, head_count, head_dim)
-    projected = projected.reshape(tok_dev, page_devices, tok_dev)[:, :, :w_cols].reshape(
-        tok_dev, page_devices * w_cols
+    head_groups = lax.axis_size("heads")
+    summed = heads_sum(projected, head_groups)
+    summed = summed.reshape(tok_dev, page_devices // head_groups, tok_dev)[:, :, :w_cols].reshape(
+        tok_dev, (page_devices // head_groups) * w_cols
     )
     key_out = key_slots.reshape(key_cache.shape)
     value_out = value_slots.reshape(value_cache.shape)
-    summed = lax.psum_scatter(projected, "heads", scatter_dimension=1, tiled=True).astype(jnp.float32)
     hidden = (summed + out_bias[None, :]).astype(jnp.bfloat16)
     return (hidden, key_out, value_out)
 

time: 287 us -> 280 us (0.976)
  blocking collectives: 75.5 us -> 0 us
  waiting for transfers between devices: 118 us -> 168 us
  Pallas kernels: 50 us -> 60.3 us
  starting transfers between devices: 0.08 us -> 4.1 us
  local copies, waits for them, and re-layouts: 18.7 us -> 21.7 us
    all_to_all x1 -> x0, blocking collectives: 75.5 us -> none  [per_device(): received = lax.all_to_all(paired, 'chips', 0, 0, tiled=True)]
    all_to_all x0 -> x1, waiting for transfers between devices: none -> 66.2 us  [per_device(): received = lax.all_to_all(paired, 'chips', 0, 0, tiled=True)]
    reduce_scatter x1 -> x0, waiting for transfers between devices: 16.1 us -> none  [per_device(): lax.psum_scatter(projected, 'heads', scatter_dimension=1, tiled=True)]
    pallas_call x0 -> x1, Pallas kernels: none -> 9.86 us  [heads_sum(): pl.pallas_call(kernel, out_shape=jax.ShapeDtypeStruct((rows, block), jnp....]
    all_to_all x0 -> x1, starting transfers between devices: none -> 4.06 us  [per_device(): received = lax.all_to_all(paired, 'chips', 0, 0, tiled=True)]
where the time goes in v8:
time: 280 us; the launch traced here: 275 us
  waiting for transfers between devices  168 us (60%)
  Pallas kernels  60.3 us (22%)
  local copies, waits for them, and re-layouts  21.7 us (8%)
  between operations  14.2 us (5%)
  other arithmetic  6.85 us (2%)
  starting transfers between devices  4.1 us (1%)
    all_gather x1, waiting for transfers between devices, per_device(): gathered = lax.all_gather(stacked, PAGES, axis=1, tiled=True)  102 us
    all_to_all x1, waiting for transfers between devices, per_device(): received = lax.all_to_all(paired, 'chips', 0, 0, tiled=True)  66.2 us
    pallas_call x1, Pallas kernels, local_attention(): pl.pallas_call(kernel, out_shape=(jax.ShapeDtypeStruct((chunks, rows_per,...  24.7 us
    pallas_call x1, Pallas kernels, pair_merge(): pl.pallas_call(kernel, out_shape=jax.ShapeDtypeStruct((chips, rows_per, l...  16 us
    pallas_call x1, Pallas kernels, heads_sum(): pl.pallas_call(kernel, out_shape=jax.ShapeDtypeStruct((rows, block), jnp....  9.86 us
    pallas_call x1, Pallas kernels, combine_project(): pl.pallas_call(kernel, out_shape=jax.ShapeDtypeStruct((rows_per, tokens),...  9.8 us
  transfers between devices with their start and end apart: 2, of which 2 were waited for; matrix products, arithmetic and copies ran while one was open for 3% of the time, Pallas kernels for 0%

profile of v8, /device:TPU:4, one launch (start us, length us, event | category | flops | bytes accessed | tf_op | source)
XLA Modules:
  0.0 275.5 jit_solution(14848441979587314427)
XLA Ops:
  7.2 0.0 all-gather.2.cloned.1.call-start
  7.2 1.0 slice.25
  8.2 0.9 convert_element_type.40
  9.1 1.0 slice.28
  10.1 0.9 convert_element_type.43
  11.0 0.0 copy-start.6
  11.1 0.0 copy-start.7
  11.1 0.0 copy-start.3
  11.1 0.9 select_reduce_fusion
  12.0 0.9 stack_reshape.2
  12.9 0.8 pad_bitcast_fusion
  13.7 0.2 multiply_cosine_fusion
  14.0 0.3 subtract_convert_fusion.1
  14.3 0.3 pad_maximum_fusion.1
  14.7 0.8 pad_maximum_fusion
  15.4 0.0 all-gather.2.cloned.1.call-update
  15.5 0.0 copy-done.6
  15.5 0.1 eq.61
  15.6 0.0 copy-done.7
  15.6 0.1 eq.65
  15.6 0.0 copy-done.3
  15.6 0.0 copy-start.4
  15.7 2.0 reshape.154.kc_ref
  17.7 0.0 copy-done.4
  17.7 0.0 copy-start.10
  17.7 2.0 reshape.155.vc_ref
  19.6 0.2 fusion.1.sfresh_ref
  19.8 0.0 copy-start.8
  19.8 0.2 compare_reduce_fusion.1
  20.0 0.2 fusion
  20.2 0.5 broadcast_select_fusion
  20.7 0.0 copy-start.9
  20.7 0.0 copy-done.10
  20.7 0.1 select_reduce_fusion.1
  20.8 0.2 compare_reduce_fusion
  21.0 0.5 fusion.5.skind_ref
  21.5 102.0 %all-gather.2.cloned.1.call-done.q_ref.kf_ref.vf_ref.w_ref = bf16[4,4608,512]{2,1,0:T(8,128)(2,1)} async-done(((bf16[4,72,512]{2,1,0:T(8,128)(2,1)}), bf16[4,4608,512]{2,1,0:T(8,128)(2,1)}) %all-gather.2.cloned.1.call-update) | async-done | bytes 18874384 | tf_op jit(solution)/shard_map/all_gather | solution.py:436
  123.6 0.0 copy-done.8
  123.6 0.0 copy-done.9
  123.6 24.7 %shard_map.121 = (bf16[64,72,640]{2,1,0:T(8,128)(2,1)}, bf16[12,128,512]{2,1,0:T(8,128)(2,1)}, bf16[12,128,512]{2,1,0:T(8,128)(2,1)}) custom-call(s32[12]{0:T(128)} %copy-done.9, s32[12]{0:T(128)} %fusion.5.skind_ref, s32[12]{0:T(128)} %get-tuple-element.9.slim_ref, s32[12]{0:T(128)} %copy-done.8, ...), custom_call_target="tpu_custom_call" | custom-call | flops 2415919104 | bytes 16908288 | tf_op jit(solution)/shard_map/pallas_call | solution.py:144
  148.2 0.0 copy-start.1
  148.2 2.7 copy-done.1
  150.9 16.0 %shard_map.122 = bf16[32,72,640]{2,1,0:T(8,128)(2,1)S(1)} custom-call(bf16[32,2,72,640]{3,2,1,0:T(8,128)(2,1)S(1)} %bitcast.5), custom_call_target="tpu_custom_call" | custom-call | flops 8847360 | bytes 8847360 | tf_op jit(solution)/shard_map/pallas_call | solution.py:313
  166.9 0.0 copy-start
  166.9 1.6 copy-done
  168.5 4.1 %all-to-all-start = ((bf16[32,72,640]{2,1,0:T(8,128)(2,1)}), bf16[32,72,640]{2,1,0:T(8,128)(2,1)S(1)}, u32[]{:S(2)}, u32[]{:S(2)}) async-start(bf16[32,72,640]{2,1,0:T(8,128)(2,1)} %copy-done), calls=%async_computation | async-start | bytes 5898240 | tf_op jit(solution)/shard_map/all_to_all | solution.py:471
  172.6 3.5 %reshape.159 = bf16[12,128,4,128]{3,2,1,0:T(4,128)(2,1)} reshape(bf16[12,128,512]{2,1,0:T(8,128)(2,1)} %get-tuple-element.7) | data formatting | bytes 3145728 | tf_op jit(solution)/shard_map/reshape | solution.py:478
  176.1 66.2 %all-to-all-done.recv_ref = bf16[32,72,640]{2,1,0:T(8,128)(2,1)S(1)} async-done(((bf16[32,72,640]{2,1,0:T(8,128)(2,1)}), bf16[32,72,640]{2,1,0:T(8,128)(2,1)S(1)}, u32[]{:S(2)}, u32[]{:S(2)}) %all-to-all-start) | async-done | bytes 2949152 | tf_op jit(solution)/shard_map/all_to_all | solution.py:471
  242.3 9.8 %shard_map.123.proj_hbm = bf16[72,4608]{1,0:T(8,128)(2,1)S(1)} custom-call(bf16[32,72,640]{2,1,0:T(8,128)(2,1)S(1)} %all-to-all-done.recv_ref, bf16[4,4608,512]{2,1,0:T(8,128)(2,1)} %all-gather.2.cloned.1.call-done.q_ref.kf_ref.vf_ref.w_ref), custom_call_target="tpu_custom_call" | custom-call | flops 345636864 | bytes 8331264 | tf_op jit(solution)/shard_map/pallas_call | solution.py:225
  252.1 0.0 copy-start.2
  252.1 0.8 copy-done.2
  252.9 3.5 %reshape.160 = bf16[12,128,4,128]{3,2,1,0:T(4,128)(2,1)} reshape(bf16[12,128,512]{2,1,0:T(8,128)(2,1)} %get-tuple-element.8) | data formatting | bytes 3145728 | tf_op jit(solution)/shard_map/reshape | solution.py:479
  256.4 0.0 copy-start.5
  256.4 9.9 %shard_map.124 = f32[72,1152]{1,0:T(8,128)} custom-call(bf16[72,4608]{1,0:T(8,128)(2,1)} %copy-done.2), custom_call_target="tpu_custom_call" | custom-call | flops 331776 | bytes 995328 | tf_op jit(solution)/shard_map/pallas_call | solution.py:375
  266.3 1.5 reshape.157
  267.8 0.2 reshape.158
  267.9 0.0 copy-done.5
  268.0 0.7 add_convert_fusion
  (6 shorter events, 0.1 us)
Async XLA Ops:
  7.2 116.4 %all-gather.2.cloned.1.call-start = ((), (), s32[]{:S(2)}) async-start(), calls=%async_computation.1 | async-start | bytes 19169280 | tf_op jit(solution)/shard_map/all_gather | solution.py:436
  11.0 4.4 %copy-start.6 = (s32[6,6]{1,0:T(8,128)S(1)}, s32[6,6]{1,0:T(8,128)}, u32[]{:S(2)}) copy-start(s32[6,6]{1,0:T(8,128)} %param.17) | copy-start | bytes 436
  11.1 4.5 %copy-start.7 = (s32[6,122]{1,0:T(8,128)S(1)}, s32[6,122]{1,0:T(8,128)}, u32[]{:S(2)}) copy-start(s32[6,122]{1,0:T(8,128)} %param.16) | copy-start | bytes 8788
  11.1 4.6 %copy-start.3 = (bf16[12,128,4,128]{3,2,1,0:T(4,128)(2,1)S(1)}, bf16[12,128,4,128]{3,2,1,0:T(4,128)(2,1)}, u32[]{:S(2)}) copy-start(bf16[12,128,4,128]{3,2,1,0:T(4,128)(2,1)} %param.13) | copy-start | bytes 4718596
  15.6 2.0 copy-start.4
  17.7 3.1 %copy-start.10 = (s32[6]{0:T(128)S(1)}, s32[6]{0:T(128)}, u32[]{:S(2)}) copy-start(s32[6]{0:T(128)} %param.15) | copy-start | bytes 76
  19.8 103.7 %copy-start.8 = (s32[12]{0:T(128)}, s32[12]{0:T(128)S(1)}, u32[]{:S(2)}) copy-start(s32[12]{0:T(128)S(1)} %fusion.1.sfresh_ref) | copy-start | bytes 148
  20.7 102.8 %copy-start.9 = (s32[12]{0:T(128)}, s32[12]{0:T(128)S(1)}, u32[]{:S(2)}) copy-start(s32[12]{0:T(128)S(1)} %get-tuple-element.17.sreq_ref) | copy-start | bytes 148
  148.2 2.7 copy-start.1
  166.9 1.6 copy-start
  168.5 73.8 %all-to-all-start = ((bf16[32,72,640]{2,1,0:T(8,128)(2,1)}), bf16[32,72,640]{2,1,0:T(8,128)(2,1)S(1)}, u32[]{:S(2)}, u32[]{:S(2)}) async-start(bf16[32,72,640]{2,1,0:T(8,128)(2,1)} %copy-done), calls=%async_computation | async-start | bytes 5898240 | tf_op jit(solution)/shard_map/all_to_all | solution.py:471
  252.1 0.8 copy-start.2
  256.4 11.5 %copy-start.5 = (f32[1024]{0:T(1024)S(1)}, f32[1024]{0:T(1024)}, u32[]{:S(2)}) copy-start(f32[1024]{0:T(1024)} %param.19) | copy-start | bytes 12292
Sparse Core Ops, SparseCore 0:
  15.6 107.9 all-gather.1

commit v9 on v8

--- a/solution.py
+++ b/solution.py
@@ -10,7 +10,7 @@
 
 ROT = 32
 PAGE = 128
-PAGES = ("chips", "core")
+PAGES = ("z", "y", "core")
 
 
 low_score = -1e30
@@ -393,6 +393,66 @@
     )(projected)
 
 
+def merge_parts_kernel(heads, head_dim, parts_ref, out_ref):
+    chunks, parts, rows_per, _ = parts_ref.shape
+    width = heads * head_dim
+    lanes = 128
+    lane = lax.broadcasted_iota(jnp.int32, (rows_per, lanes), 1)
+
+    def merge_step(c, carry):
+        stats = [parts_ref[c, j, :, width:].astype(jnp.float32) for j in range(parts)]
+        peak = stats[0]
+        for j in range(1, parts):
+            peak = jnp.maximum(peak, stats[j])
+        factors = [jnp.exp(st - peak) for st in stats]
+        merged = jnp.zeros((rows_per, lanes), jnp.float32)
+        for h in range(heads):
+            cut = slice(h * head_dim, (h + 1) * head_dim)
+            o_h = jnp.zeros((rows_per, head_dim), jnp.float32)
+            l_h = jnp.zeros((rows_per, 1), jnp.float32)
+            for j in range(parts):
+                f_h = factors[j][:, h : h + 1]
+                o_h = o_h + f_h * parts_ref[c, j, :, cut].astype(jnp.float32)
+                l_j = (
+                    stats[j][:, heads + h : heads + h + 1]
+                    + stats[j][:, 2 * heads + h : 2 * heads + h + 1]
+                )
+                l_h = l_h + f_h * l_j
+            out_ref[c, :, cut] = o_h.astype(out_ref.dtype)
+            l_hi = l_h.astype(jnp.bfloat16).astype(jnp.float32)
+            merged = jnp.where(
+                lane == h,
+                peak[:, h : h + 1],
+                jnp.where(
+                    lane == heads + h,
+                    l_hi,
+                    jnp.where(lane == 2 * heads + h, l_h - l_hi, merged),
+                ),
+            )
+        out_ref[c, :, width:] = merged.astype(out_ref.dtype)
+        return carry
+
+    lax.fori_loop(0, chunks, merge_step, 0)
+
+
+def merge_parts(parts_in, heads, head_dim):
+    chunks, parts, rows_per, lanes_all = parts_in.shape
+    kernel = functools.partial(merge_parts_kernel, heads, head_dim)
+    return pl.pallas_call(
+        kernel,
+        out_shape=jax.ShapeDtypeStruct((chunks, rows_per, lanes_all), parts_in.dtype),
+        grid=(1,),
+        in_specs=[pl.BlockSpec(parts_in.shape, lambda i: (0, 0, 0, 0))],
+        out_specs=pl.BlockSpec((chunks, rows_per, lanes_all), lambda i: (0, 0, 0)),
+        compiler_params=pltpu.CompilerParams(vmem_limit_bytes=32 * 1024 * 1024),
+        cost_estimate=pl.CostEstimate(
+            flops=4 * parts_in.size,
+            transcendentals=chunks * parts * rows_per * 128,
+            bytes_accessed=parts_in.size * 2 + chunks * rows_per * lanes_all * 2,
+        ),
+    )(parts_in)
+
+
 def per_device(
     queries,
     keys,
@@ -468,7 +528,12 @@
         page_devices,
     )
     paired = pair_merge(packed, head_count, head_dim)
-    received = lax.all_to_all(paired, "chips", 0, 0, tiled=True)
+    z_n = lax.axis_size("z")
+    y_n = lax.axis_size("y")
+    by_y = paired.reshape(z_n, y_n, tok_dev, paired.shape[-1])
+    from_y = lax.all_to_all(by_y, "y", 1, 1, tiled=True)
+    merged = merge_parts(from_y, head_count, head_dim)
+    received = lax.all_to_all(merged, "z", 0, 0, tiled=True)
     projected = combine_project(received, gathered, head_count, head_dim)
     head_groups = lax.axis_size("heads")
     summed = heads_sum(projected, head_groups)
@@ -483,8 +548,9 @@
 
 def solution(mesh):
     heads_n, pages_n = mesh.devices.shape
+    z_n = pages_n // 8
     split = jax.sharding.Mesh(
-        mesh.devices.reshape(heads_n, pages_n // 2, 2), ("heads", "chips", "core")
+        mesh.devices.reshape(heads_n, z_n, 4, 2), ("heads", "z", "y", "core")
     )
     placed = (
         P(PAGES, "heads", None),

time: 280 us -> 266 us (0.950); the launches traced: 275 us -> 265 us
  waiting for transfers between devices: 168 us -> 121 us
  blocking collectives: 0 us -> 38.7 us
  local copies, waits for them, and re-layouts: 21.7 us -> 17.4 us
    all_to_all x1, waiting for transfers between devices: 66.2 us -> 19.4 us  [per_device(): received = lax.all_to_all(merged, 'z', 0, 0, tiled=True)]
    all_to_all x0 -> x1, blocking collectives: none -> 38.7 us  [per_device(): from_y = lax.all_to_all(by_y, 'y', 1, 1, tiled=True)]
    pallas_call x0 -> x1, Pallas kernels: none -> 4.82 us  [merge_parts(): pl.pallas_call(kernel, out_shape=jax.ShapeDtypeStruct((chunks, rows_per,...]
    pallas_call x1, Pallas kernels: 9.8 us -> 5.37 us  [combine_project(): pl.pallas_call(kernel, out_shape=jax.ShapeDtypeStruct((rows_per, tokens),...]
where the time goes in v9:
time: 266 us; the launch traced here: 265 us
  waiting for transfers between devices  121 us (45%)
  Pallas kernels  59.9 us (23%)
  blocking collectives  38.7 us (15%)
  local copies, waits for them, and re-layouts  17.4 us (7%)
  between operations  14.2 us (5%)
  other arithmetic  6.92 us (3%)
  starting transfers between devices  6.67 us (3%)
    all_gather x1, waiting for transfers between devices, per_device(): gathered = lax.all_gather(stacked, PAGES, axis=1, tiled=True)  102 us
    all_to_all x1, blocking collectives, per_device(): from_y = lax.all_to_all(by_y, 'y', 1, 1, tiled=True)  38.7 us
    pallas_call x1, Pallas kernels, local_attention(): pl.pallas_call(kernel, out_shape=(jax.ShapeDtypeStruct((chunks, rows_per,...  22.8 us
    all_to_all x1, waiting for transfers between devices, per_device(): received = lax.all_to_all(merged, 'z', 0, 0, tiled=True)  19.4 us
    pallas_call x1, Pallas kernels, pair_merge(): pl.pallas_call(kernel, out_shape=jax.ShapeDtypeStruct((chips, rows_per, l...  16 us
    pallas_call x1, Pallas kernels, heads_sum(): pl.pallas_call(kernel, out_shape=jax.ShapeDtypeStruct((rows, block), jnp....  11 us
    all_to_all x1, starting transfers between devices, per_device(): received = lax.all_to_all(merged, 'z', 0, 0, tiled=True)  6.63 us
    pallas_call x1, Pallas kernels, combine_project(): pl.pallas_call(kernel, out_shape=jax.ShapeDtypeStruct((rows_per, tokens),...  5.37 us
  transfers between devices with their start and end apart: 2, of which 2 were waited for; matrix products, arithmetic and copies ran while one was open for 3% of the time, Pallas kernels for 0%

profile of v9, /device:TPU:4, one launch (start us, length us, event | category | flops | bytes accessed | tf_op | source)
XLA Modules:
  0.0 265.1 jit_solution(4085765395504238396)
XLA Ops:
  7.2 0.0 all-gather.2.cloned.1.call-start
  7.2 1.0 slice.25
  8.2 0.9 convert_element_type.40
  9.1 1.0 slice.28
  10.1 0.9 convert_element_type.43
  11.0 0.0 copy-start.7
  11.1 0.0 copy-start.8
  11.1 0.0 copy-start.2
  11.1 0.9 select_reduce_fusion
  12.0 0.9 stack_reshape.2
  12.9 0.8 pad_bitcast_fusion
  13.7 0.2 multiply_cosine_fusion
  14.0 0.3 subtract_convert_fusion.1
  14.3 0.3 pad_maximum_fusion.1
  14.7 0.8 pad_maximum_fusion
  15.4 0.0 all-gather.2.cloned.1.call-update
  15.5 0.0 copy-done.7
  15.5 0.1 eq.61
  15.5 0.0 copy-done.8
  15.5 0.1 eq.65
  15.6 0.0 copy-done.2
  15.6 0.0 copy-start.3
  15.6 2.0 reshape.157.kc_ref
  17.6 0.0 copy-done.3
  17.6 0.0 copy-start.11
  17.6 2.0 reshape.158.vc_ref
  19.6 0.2 fusion.1.sfresh_ref
  19.8 0.0 copy-start.9
  19.8 0.2 compare_reduce_fusion.1
  20.0 0.2 fusion
  20.2 0.5 broadcast_select_fusion
  20.7 0.0 copy-start.10
  20.7 0.0 copy-done.11
  20.7 0.1 select_reduce_fusion.1
  20.8 0.2 compare_reduce_fusion
  21.0 0.6 fusion.5.skind_ref
  21.6 102.0 %all-gather.2.cloned.1.call-done.q_ref.kf_ref.vf_ref.w_ref = bf16[4,4608,512]{2,1,0:T(8,128)(2,1)} async-done(((bf16[4,72,512]{2,1,0:T(8,128)(2,1)}), bf16[4,4608,512]{2,1,0:T(8,128)(2,1)}) %all-gather.2.cloned.1.call-update) | async-done | bytes 18874384 | tf_op jit(solution)/shard_map/all_gather | solution.py:496
  123.5 0.0 copy-done.9
  123.5 0.0 copy-done.10
  123.5 22.8 %shard_map.121 = (bf16[64,72,640]{2,1,0:T(8,128)(2,1)}, bf16[12,128,512]{2,1,0:T(8,128)(2,1)}, bf16[12,128,512]{2,1,0:T(8,128)(2,1)}) custom-call(s32[12]{0:T(128)} %copy-done.10, s32[12]{0:T(128)} %fusion.5.skind_ref, s32[12]{0:T(128)} %get-tuple-element.9.slim_ref, s32[12]{0:T(128)} %copy-done.9, ...), custom_call_target="tpu_custom_call" | custom-call | flops 2415919104 | bytes 16908288 | tf_op jit(solution)/shard_map/pallas_call | solution.py:144
  146.3 0.0 copy-start
  146.3 2.7 %copy-done = bf16[64,72,640]{2,1,0:T(8,128)(2,1)S(1)} copy-done((bf16[64,72,640]{2,1,0:T(8,128)(2,1)S(1)}, bf16[64,72,640]{2,1,0:T(8,128)(2,1)}, u32[]{:S(2)}) %copy-start) | copy-done | bytes 5898264
  149.0 16.0 %shard_map.122 = bf16[32,72,640]{2,1,0:T(8,128)(2,1)S(1)} custom-call(bf16[32,2,72,640]{3,2,1,0:T(8,128)(2,1)S(1)} %bitcast.7), custom_call_target="tpu_custom_call" | custom-call | flops 8847360 | bytes 8847360 | tf_op jit(solution)/shard_map/pallas_call | solution.py:313
  164.9 0.3 copy.15
  165.2 38.7 %all_to_all.10 = bf16[8,4,72,640]{3,2,0,1:T(8,128)(2,1)S(1)} all-to-all(bf16[8,4,72,640]{3,2,0,1:T(8,128)(2,1)S(1)} %copy.15), channel_id=1, replica_groups=mesh['heads'=4,'z'=8,'y'=4,'core'=2] {'y'}, dimensions={1} | all-to-all | bytes 5898240 | tf_op jit(solution)/shard_map/all_to_all | solution.py:534
  203.9 0.3 copy.16.parts_ref
  204.2 0.0 copy-start.5
  204.2 4.8 %shard_map.123 = bf16[8,72,640]{2,1,0:T(8,128)(2,1)} custom-call(bf16[8,4,72,640]{3,2,1,0:T(8,128)(2,1)S(1)} %copy.16.parts_ref), custom_call_target="tpu_custom_call" | custom-call | flops 5898240 | bytes 3686400 | tf_op jit(solution)/shard_map/pallas_call | solution.py:441
  209.0 6.6 %all-to-all-start.1 = ((bf16[8,72,640]{2,1,0:T(8,128)(2,1)}), bf16[8,72,640]{2,1,0:T(8,128)(2,1)S(1)}, u32[]{:S(2)}, u32[]{:S(2)}) async-start(bf16[8,72,640]{2,1,0:T(8,128)(2,1)} %shard_map.123), calls=%async_computation.1 | async-start | bytes 1474560 | tf_op jit(solution)/shard_map/all_to_all | solution.py:536
  215.6 0.0 copy-done.5
  215.6 1.9 reshape.163
  217.5 0.0 copy-start.4
  217.5 19.4 %all-to-all-done.1.recv_ref = bf16[8,72,640]{2,1,0:T(8,128)(2,1)S(1)} async-done(((bf16[8,72,640]{2,1,0:T(8,128)(2,1)}), bf16[8,72,640]{2,1,0:T(8,128)(2,1)S(1)}, u32[]{:S(2)}, u32[]{:S(2)}) %all-to-all-start.1) | async-done | bytes 737312 | tf_op jit(solution)/shard_map/all_to_all | solution.py:536
  236.8 5.4 %shard_map.124.proj_hbm = bf16[72,4608]{1,0:T(8,128)(2,1)S(1)} custom-call(bf16[8,72,640]{2,1,0:T(8,128)(2,1)S(1)} %all-to-all-done.1.recv_ref, bf16[4,4608,512]{2,1,0:T(8,128)(2,1)} %all-gather.2.cloned.1.call-done.q_ref.kf_ref.vf_ref.w_ref), custom_call_target="tpu_custom_call" | custom-call | flops 341213184 | bytes 6119424 | tf_op jit(solution)/shard_map/pallas_call | solution.py:225
  242.2 0.0 copy-start.1
  242.2 0.8 copy-done.1
  243.1 0.0 copy-done.4
  243.1 1.8 reshape.164
  244.9 0.0 copy-start.6
  244.9 11.0 %shard_map.125 = f32[72,1152]{1,0:T(8,128)} custom-call(bf16[72,4608]{1,0:T(8,128)(2,1)} %copy-done.1), custom_call_target="tpu_custom_call" | custom-call | flops 331776 | bytes 995328 | tf_op jit(solution)/shard_map/pallas_call | solution.py:375
  255.9 1.5 reshape.161
  257.4 0.2 reshape.162
  257.6 0.0 copy-done.6
  257.6 0.7 add_convert_fusion
  (6 shorter events, 0.1 us)
Async XLA Ops:
  7.2 116.4 %all-gather.2.cloned.1.call-start = ((), (), s32[]{:S(2)}) async-start(), calls=%async_computation.2 | async-start | bytes 19169280 | tf_op jit(solution)/shard_map/all_gather | solution.py:496
  11.0 4.4 %copy-start.7 = (s32[6,6]{1,0:T(8,128)S(1)}, s32[6,6]{1,0:T(8,128)}, u32[]{:S(2)}) copy-start(s32[6,6]{1,0:T(8,128)} %param.17) | copy-start | bytes 436
  11.1 4.5 %copy-start.8 = (s32[6,122]{1,0:T(8,128)S(1)}, s32[6,122]{1,0:T(8,128)}, u32[]{:S(2)}) copy-start(s32[6,122]{1,0:T(8,128)} %param.16) | copy-start | bytes 8788
  11.1 4.6 %copy-start.2 = (bf16[12,128,4,128]{3,2,1,0:T(4,128)(2,1)S(1)}, bf16[12,128,4,128]{3,2,1,0:T(4,128)(2,1)}, u32[]{:S(2)}) copy-start(bf16[12,128,4,128]{3,2,1,0:T(4,128)(2,1)} %param.13) | copy-start | bytes 4718596
  15.6 2.0 copy-start.3
  17.6 3.1 %copy-start.11 = (s32[6]{0:T(128)S(1)}, s32[6]{0:T(128)}, u32[]{:S(2)}) copy-start(s32[6]{0:T(128)} %param.15) | copy-start | bytes 76
  19.8 103.7 %copy-start.9 = (s32[12]{0:T(128)}, s32[12]{0:T(128)S(1)}, u32[]{:S(2)}) copy-start(s32[12]{0:T(128)S(1)} %fusion.1.sfresh_ref) | copy-start | bytes 148
  20.7 102.8 %copy-start.10 = (s32[12]{0:T(128)}, s32[12]{0:T(128)S(1)}, u32[]{:S(2)}) copy-start(s32[12]{0:T(128)S(1)} %get-tuple-element.17.sreq_ref) | copy-start | bytes 148
  146.3 2.7 %copy-start = (bf16[64,72,640]{2,1,0:T(8,128)(2,1)S(1)}, bf16[64,72,640]{2,1,0:T(8,128)(2,1)}, u32[]{:S(2)}) copy-start(bf16[64,72,640]{2,1,0:T(8,128)(2,1)} %get-tuple-element.6) | copy-start | bytes 17694724
  204.2 11.5 %copy-start.5 = (bf16[12,128,512]{2,1,0:T(8,128)(2,1)S(1)}, bf16[12,128,512]{2,1,0:T(8,128)(2,1)}, u32[]{:S(2)}) copy-start(bf16[12,128,512]{2,1,0:T(8,128)(2,1)} %get-tuple-element.7) | copy-start | bytes 4718596
  209.0 27.8 %all-to-all-start.1 = ((bf16[8,72,640]{2,1,0:T(8,128)(2,1)}), bf16[8,72,640]{2,1,0:T(8,128)(2,1)S(1)}, u32[]{:S(2)}, u32[]{:S(2)}) async-start(bf16[8,72,640]{2,1,0:T(8,128)(2,1)} %shard_map.123), calls=%async_computation.1 | async-start | bytes 1474560 | tf_op jit(solution)/shard_map/all_to_all | solution.py:536
  217.5 25.6 %copy-start.4 = (bf16[12,128,512]{2,1,0:T(8,128)(2,1)S(1)}, bf16[12,128,512]{2,1,0:T(8,128)(2,1)}, u32[]{:S(2)}) copy-start(bf16[12,128,512]{2,1,0:T(8,128)(2,1)} %get-tuple-element.8) | copy-start | bytes 4718596
  242.2 0.9 copy-start.1
  244.9 12.7 %copy-start.6 = (f32[1024]{0:T(1024)S(1)}, f32[1024]{0:T(1024)}, u32[]{:S(2)}) copy-start(f32[1024]{0:T(1024)} %param.19) | copy-start | bytes 12292
Sparse Core Ops, SparseCore 0:
  15.6 107.9 all-gather.1

commit v10 on v9

--- a/solution.py
+++ b/solution.py
@@ -228,7 +228,7 @@
         grid=(1,),
         in_specs=[
             pl.BlockSpec(received.shape, lambda i: (0, 0, 0)),
-            pl.BlockSpec((1, tokens, width), lambda i: (3, 0, 0)),
+            pl.BlockSpec((1, tokens, width), lambda i: (0, 0, 0)),
         ],
         out_specs=pl.BlockSpec((rows_per, tokens), lambda i: (0, 0)),
         scratch_shapes=[
@@ -490,9 +490,9 @@
             rotated_q.reshape(tok_dev, width),
             rotated_k.reshape(tok_dev, width),
             values.reshape(tok_dev, width),
-            w_plane,
         ]
     )
+    w_all = lax.all_gather(w_plane[None], PAGES, axis=1, tiled=True)
     gathered = lax.all_gather(stacked, PAGES, axis=1, tiled=True)
     my_slots = device_at * slot_count + jnp.arange(slot_count, dtype=jnp.int32)
     cached_hit = page_table.reshape(-1)[None, :] == my_slots[:, None]
@@ -534,7 +534,7 @@
     from_y = lax.all_to_all(by_y, "y", 1, 1, tiled=True)
     merged = merge_parts(from_y, head_count, head_dim)
     received = lax.all_to_all(merged, "z", 0, 0, tiled=True)
-    projected = combine_project(received, gathered, head_count, head_dim)
+    projected = combine_project(received, w_all, head_count, head_dim)
     head_groups = lax.axis_size("heads")
     summed = heads_sum(projected, head_groups)
     summed = summed.reshape(tok_dev, page_devices // head_groups, tok_dev)[:, :, :w_cols].reshape(

time: 266 us -> 263 us (0.989)
  waiting for transfers between devices: 121 us -> 109 us
  blocking collectives: 38.7 us -> 49 us
  Pallas kernels: 59.9 us -> 56.8 us
    all_gather x1, waiting for transfers between devices: 102 us -> 89.6 us  [per_device(): gathered = lax.all_gather(stacked, PAGES, axis=1, tiled=True)]
    all_to_all x1, blocking collectives: 38.7 us -> 49 us  [per_device(): from_y = lax.all_to_all(by_y, 'y', 1, 1, tiled=True)]
    unnamed x24 -> x30, local copies, waits for them, and re-layouts: 3.56 us -> 5.93 us
  transfers between devices with their start and end apart: 2 -> 3, of which waited for: 2 -> 2; matrix products, arithmetic and copies ran while one was open for 3% -> 3% of each run, Pallas kernels for 0% -> 16%
where the time goes in v10:
time: 263 us; the launch traced here: 262 us
  waiting for transfers between devices  109 us (41%)
  Pallas kernels  56.8 us (22%)
  blocking collectives  49 us (19%)
  local copies, waits for them, and re-layouts  18.7 us (7%)
  between operations  14.3 us (5%)
  starting transfers between devices  7.26 us (3%)
  other arithmetic  6.8 us (3%)
    all_gather x1, waiting for transfers between devices, per_device(): gathered = lax.all_gather(stacked, PAGES, axis=1, tiled=True)  89.6 us
    all_to_all x1, blocking collectives, per_device(): from_y = lax.all_to_all(by_y, 'y', 1, 1, tiled=True)  49 us
    pallas_call x1, Pallas kernels, local_attention(): pl.pallas_call(kernel, out_shape=(jax.ShapeDtypeStruct((chunks, rows_per,...  22 us
    all_to_all x1, waiting for transfers between devices, per_device(): received = lax.all_to_all(merged, 'z', 0, 0, tiled=True)  19.4 us
    pallas_call x1, Pallas kernels, pair_merge(): pl.pallas_call(kernel, out_shape=jax.ShapeDtypeStruct((chips, rows_per, l...  16 us
    pallas_call x1, Pallas kernels, heads_sum(): pl.pallas_call(kernel, out_shape=jax.ShapeDtypeStruct((rows, block), jnp....  11 us
    all_to_all x1, starting transfers between devices, per_device(): received = lax.all_to_all(merged, 'z', 0, 0, tiled=True)  7.18 us
    unnamed x30, local copies, waits for them, and re-layouts  5.93 us
  transfers between devices with their start and end apart: 3, of which 2 were waited for; matrix products, arithmetic and copies ran while one was open for 3% of the time, Pallas kernels for 16%

profile of v10, /device:TPU:4, one launch (start us, length us, event | category | flops | bytes accessed | tf_op | source)
XLA Modules:
  0.0 261.9 jit_solution(14843789371192785412)
XLA Ops:
  7.2 0.0 copy-start.7
  7.2 0.0 all-gather.4.cloned.1.call-start
  7.2 0.9 convert_element_type.40
  8.1 1.0 slice.25
  9.1 0.0 copy-start.8
  9.2 0.9 convert_element_type.43
  10.1 0.0 copy-start.10
  10.1 0.0 copy-start.11
  10.1 0.0 copy-start.3
  10.1 1.1 slice.28
  11.3 0.7 select_reduce_fusion
  12.0 0.2 multiply_cosine_fusion
  12.2 0.3 subtract_convert_fusion.1
  12.6 0.3 pad_maximum_fusion.1
  13.0 0.0 copy-done.7
  13.0 0.7 pad_maximum_fusion
  13.7 0.0 all-gather.4.cloned.1.call-update
  13.8 0.0 all-gather.6.cloned.1.call-start
  13.8 0.0 copy-done.8
  13.8 0.6 pad.4
  14.5 0.0 all-gather.6.cloned.1.call-update
  14.5 0.0 copy-done.10
  14.5 0.1 eq.61
  14.6 0.0 copy-done.11
  14.6 0.1 eq.65
  14.7 0.0 copy-done.3
  14.7 0.0 copy-start.4
  14.7 2.0 reshape.157.kc_ref
  16.7 0.0 copy-done.4
  16.7 0.0 copy-start.14
  16.7 2.0 reshape.158.vc_ref
  18.7 0.2 fusion.1.sfresh_ref
  18.9 0.2 compare_reduce_fusion.1
  19.0 0.2 fusion
  19.2 0.5 broadcast_select_fusion
  19.8 0.0 copy-done.14
  19.8 0.1 select_reduce_fusion.1
  19.9 0.2 compare_reduce_fusion
  20.1 0.6 fusion.5.skind_ref
  20.6 89.6 %all-gather.4.cloned.1.call-done.q_ref.kf_ref.vf_ref = bf16[3,4608,512]{2,1,0:T(8,128)(2,1)} async-done(((bf16[3,72,512]{2,1,0:T(8,128)(2,1)}), bf16[3,4608,512]{2,1,0:T(8,128)(2,1)}) %all-gather.4.cloned.1.call-update) | async-done | bytes 14155792 | tf_op jit(solution)/shard_map/all_gather | solution.py:496
  110.2 0.0 copy-done.12
  110.2 0.0 copy-done.13
  110.2 22.0 %shard_map.121 = (bf16[64,72,640]{2,1,0:T(8,128)(2,1)}, bf16[12,128,512]{2,1,0:T(8,128)(2,1)}, bf16[12,128,512]{2,1,0:T(8,128)(2,1)}) custom-call(s32[12]{0:T(128)} %copy-done.13, s32[12]{0:T(128)} %fusion.5.skind_ref, s32[12]{0:T(128)} %get-tuple-element.9.slim_ref, s32[12]{0:T(128)} %copy-done.12, ...), custom_call_target="tpu_custom_call" | custom-call | flops 2415919104 | bytes 16908288 | tf_op jit(solution)/shard_map/pallas_call | solution.py:144
  132.2 2.7 %copy-done = bf16[64,72,640]{2,1,0:T(8,128)(2,1)S(1)} copy-done((bf16[64,72,640]{2,1,0:T(8,128)(2,1)S(1)}, bf16[64,72,640]{2,1,0:T(8,128)(2,1)}, u32[]{:S(2)}) %copy-start) | copy-done | bytes 5898264
  134.9 16.0 %shard_map.122 = bf16[32,72,640]{2,1,0:T(8,128)(2,1)S(1)} custom-call(bf16[32,2,72,640]{3,2,1,0:T(8,128)(2,1)S(1)} %bitcast.6), custom_call_target="tpu_custom_call" | custom-call | flops 8847360 | bytes 8847360 | tf_op jit(solution)/shard_map/pallas_call | solution.py:313
  150.9 0.3 copy.15
  151.1 49.0 %all_to_all.10 = bf16[8,4,72,640]{3,2,0,1:T(8,128)(2,1)S(1)} all-to-all(bf16[8,4,72,640]{3,2,0,1:T(8,128)(2,1)S(1)} %copy.15), channel_id=1, replica_groups=mesh['heads'=4,'z'=8,'y'=4,'core'=2] {'y'}, dimensions={1} | all-to-all | bytes 5898240 | tf_op jit(solution)/shard_map/all_to_all | solution.py:534
  200.2 0.3 copy.16.parts_ref
  200.4 0.0 copy-start.6
  200.4 4.8 %shard_map.123 = bf16[8,72,640]{2,1,0:T(8,128)(2,1)} custom-call(bf16[8,4,72,640]{3,2,1,0:T(8,128)(2,1)S(1)} %copy.16.parts_ref), custom_call_target="tpu_custom_call" | custom-call | flops 5898240 | bytes 3686400 | tf_op jit(solution)/shard_map/pallas_call | solution.py:441
  205.3 7.2 %all-to-all-start.1 = ((bf16[8,72,640]{2,1,0:T(8,128)(2,1)}), bf16[8,72,640]{2,1,0:T(8,128)(2,1)S(1)}, u32[]{:S(2)}, u32[]{:S(2)}) async-start(bf16[8,72,640]{2,1,0:T(8,128)(2,1)} %shard_map.123), calls=%async_computation.1 | async-start | bytes 1474560 | tf_op jit(solution)/shard_map/all_to_all | solution.py:536
  212.4 0.0 copy-done.6
  212.4 1.9 reshape.163
  214.3 19.4 %all-to-all-done.1.recv_ref = bf16[8,72,640]{2,1,0:T(8,128)(2,1)S(1)} async-done(((bf16[8,72,640]{2,1,0:T(8,128)(2,1)}), bf16[8,72,640]{2,1,0:T(8,128)(2,1)S(1)}, u32[]{:S(2)}, u32[]{:S(2)}) %all-to-all-start.1) | async-done | bytes 737312 | tf_op jit(solution)/shard_map/all_to_all | solution.py:536
  233.7 2.3 copy-done.1
  236.0 3.0 %shard_map.124.proj_hbm = bf16[72,4608]{1,0:T(8,128)(2,1)S(1)} custom-call(bf16[8,72,640]{2,1,0:T(8,128)(2,1)S(1)} %all-to-all-done.1.recv_ref, bf16[1,4608,512]{2,1,0:T(8,128)(2,1)S(1)} %bitcast.7), custom_call_target="tpu_custom_call" | custom-call | flops 341213184 | bytes 6119424 | tf_op jit(solution)/shard_map/pallas_call | solution.py:225
  239.0 0.8 copy-done.2
  239.9 0.0 copy-done.5
  239.9 1.8 reshape.164
  241.7 11.0 %shard_map.125 = f32[72,1152]{1,0:T(8,128)} custom-call(bf16[72,4608]{1,0:T(8,128)(2,1)} %copy-done.2), custom_call_target="tpu_custom_call" | custom-call | flops 331776 | bytes 995328 | tf_op jit(solution)/shard_map/pallas_call | solution.py:375
  252.7 1.5 reshape.161
  254.2 0.2 reshape.162
  254.4 0.0 copy-done.9
  254.4 0.7 add_convert_fusion
  (15 shorter events, 0.2 us)
Async XLA Ops:
  7.2 5.8 %copy-start.7 = (bf16[72,4,128]{2,1,0:T(4,128)(2,1)S(1)}, bf16[72,4,128]{2,1,0:T(4,128)(2,1)}, u32[]{:S(2)}) copy-start(bf16[72,4,128]{2,1,0:T(4,128)(2,1)} %param.12) | copy-start | bytes 221188
  7.2 103.0 %all-gather.4.cloned.1.call-start = ((), (), s32[]{:S(2)}) async-start(), calls=%async_computation.2 | async-start | bytes 14376960 | tf_op jit(solution)/shard_map/all_gather | solution.py:496
  9.1 4.7 %copy-start.8 = (bf16[512,64]{0,1:T(8,128)(2,1)S(1)}, bf16[512,64]{0,1:T(8,128)(2,1)}, u32[]{:S(2)}) copy-start(bf16[512,64]{0,1:T(8,128)(2,1)} %param.18) | copy-start | bytes 196612
  10.1 4.4 %copy-start.10 = (s32[6,6]{1,0:T(8,128)S(1)}, s32[6,6]{1,0:T(8,128)}, u32[]{:S(2)}) copy-start(s32[6,6]{1,0:T(8,128)} %param.17) | copy-start | bytes 436
  10.1 4.5 %copy-start.11 = (s32[6,122]{1,0:T(8,128)S(1)}, s32[6,122]{1,0:T(8,128)}, u32[]{:S(2)}) copy-start(s32[6,122]{1,0:T(8,128)} %param.16) | copy-start | bytes 8788
  10.1 4.6 %copy-start.3 = (bf16[12,128,4,128]{3,2,1,0:T(4,128)(2,1)S(1)}, bf16[12,128,4,128]{3,2,1,0:T(4,128)(2,1)}, u32[]{:S(2)}) copy-start(bf16[12,128,4,128]{3,2,1,0:T(4,128)(2,1)} %param.13) | copy-start | bytes 4718596
  13.8 200.5 %all-gather.6.cloned.1.call-start = ((), (), s32[]{:S(2)}) async-start(), calls=%async_computation.3 | async-start | bytes 4792320 | tf_op jit(solution)/shard_map/all_gather | solution.py:495
  14.7 2.0 copy-start.4
  16.7 3.1 %copy-start.14 = (s32[6]{0:T(128)S(1)}, s32[6]{0:T(128)}, u32[]{:S(2)}) copy-start(s32[6]{0:T(128)} %param.15) | copy-start | bytes 76
  18.9 91.3 %copy-start.12 = (s32[12]{0:T(128)}, s32[12]{0:T(128)S(1)}, u32[]{:S(2)}) copy-start(s32[12]{0:T(128)S(1)} %fusion.1.sfresh_ref) | copy-start | bytes 148
  19.8 90.4 %copy-start.13 = (s32[12]{0:T(128)}, s32[12]{0:T(128)S(1)}, u32[]{:S(2)}) copy-start(s32[12]{0:T(128)S(1)} %get-tuple-element.17.sreq_ref) | copy-start | bytes 148
  132.2 2.7 %copy-start = (bf16[64,72,640]{2,1,0:T(8,128)(2,1)S(1)}, bf16[64,72,640]{2,1,0:T(8,128)(2,1)}, u32[]{:S(2)}) copy-start(bf16[64,72,640]{2,1,0:T(8,128)(2,1)} %get-tuple-element.6) | copy-start | bytes 17694724
  200.4 12.0 %copy-start.6 = (bf16[12,128,512]{2,1,0:T(8,128)(2,1)S(1)}, bf16[12,128,512]{2,1,0:T(8,128)(2,1)}, u32[]{:S(2)}) copy-start(bf16[12,128,512]{2,1,0:T(8,128)(2,1)} %get-tuple-element.7) | copy-start | bytes 4718596
  205.3 28.4 %all-to-all-start.1 = ((bf16[8,72,640]{2,1,0:T(8,128)(2,1)}), bf16[8,72,640]{2,1,0:T(8,128)(2,1)S(1)}, u32[]{:S(2)}, u32[]{:S(2)}) async-start(bf16[8,72,640]{2,1,0:T(8,128)(2,1)} %shard_map.123), calls=%async_computation.1 | async-start | bytes 1474560 | tf_op jit(solution)/shard_map/all_to_all | solution.py:536
  233.7 2.3 copy-start.1
  236.0 3.9 %copy-start.5 = (bf16[12,128,512]{2,1,0:T(8,128)(2,1)S(1)}, bf16[12,128,512]{2,1,0:T(8,128)(2,1)}, u32[]{:S(2)}) copy-start(bf16[12,128,512]{2,1,0:T(8,128)(2,1)} %get-tuple-element.8) | copy-start | bytes 4718596
  239.0 0.9 copy-start.2
  241.7 12.7 %copy-start.9 = (f32[1024]{0:T(1024)S(1)}, f32[1024]{0:T(1024)}, u32[]{:S(2)}) copy-start(f32[1024]{0:T(1024)} %param.19) | copy-start | bytes 12292
Sparse Core Ops, SparseCore 0:
  13.9 96.2 all-gather.3
  113.5 86.3 all-gather.5

commit v11 on v8

--- a/solution.py
+++ b/solution.py
@@ -10,7 +10,7 @@
 
 ROT = 32
 PAGE = 128
-PAGES = ("chips", "core")
+PAGES = ("z", "y", "core")
 
 
 low_score = -1e30
@@ -228,7 +228,7 @@
         grid=(1,),
         in_specs=[
             pl.BlockSpec(received.shape, lambda i: (0, 0, 0)),
-            pl.BlockSpec((1, tokens, width), lambda i: (3, 0, 0)),
+            pl.BlockSpec((1, tokens, width), lambda i: (0, 0, 0)),
         ],
         out_specs=pl.BlockSpec((rows_per, tokens), lambda i: (0, 0)),
         scratch_shapes=[
@@ -393,6 +393,107 @@
     )(projected)
 
 
+def merge_chunk(heads, head_dim, parts, get_part, out_ref, c):
+    rows_per = out_ref.shape[1]
+    width = heads * head_dim
+    lanes = 128
+    lane = lax.broadcasted_iota(jnp.int32, (rows_per, lanes), 1)
+    stats = [get_part(j, c, slice(width, width + lanes)).astype(jnp.float32) for j in range(parts)]
+    peak = stats[0]
+    for j in range(1, parts):
+        peak = jnp.maximum(peak, stats[j])
+    factors = [jnp.exp(st - peak) for st in stats]
+    merged = jnp.zeros((rows_per, lanes), jnp.float32)
+    for h in range(heads):
+        cut = slice(h * head_dim, (h + 1) * head_dim)
+        o_h = jnp.zeros((rows_per, head_dim), jnp.float32)
+        l_h = jnp.zeros((rows_per, 1), jnp.float32)
+        for j in range(parts):
+            f_h = factors[j][:, h : h + 1]
+            o_h = o_h + f_h * get_part(j, c, cut).astype(jnp.float32)
+            l_j = (
+                stats[j][:, heads + h : heads + h + 1]
+                + stats[j][:, 2 * heads + h : 2 * heads + h + 1]
+            )
+            l_h = l_h + f_h * l_j
+        out_ref[c, :, cut] = o_h.astype(out_ref.dtype)
+        l_hi = l_h.astype(jnp.bfloat16).astype(jnp.float32)
+        merged = jnp.where(
+            lane == h,
+            peak[:, h : h + 1],
+            jnp.where(
+                lane == heads + h,
+                l_hi,
+                jnp.where(lane == 2 * heads + h, l_h - l_hi, merged),
+            ),
+        )
+    out_ref[c, :, width:] = merged.astype(out_ref.dtype)
+
+
+def y_exchange_kernel(heads, head_dim, groups, src_hbm, out_ref, parts, own_sem, send_sems, recv_sems):
+    me = lax.axis_index("y")
+    chunks = out_ref.shape[0]
+    barrier = pltpu.get_barrier_semaphore()
+    for k in range(1, groups):
+        pl.semaphore_signal(
+            barrier, inc=1, device_id={"y": lax.rem(me + k, groups)},
+            device_id_type=pl.DeviceIdType.MESH,
+        )
+    pl.semaphore_wait(barrier, groups - 1)
+    local = pltpu.make_async_copy(src_hbm.at[:, me], parts.at[0], own_sem)
+    local.start()
+    copies = []
+    for k in range(1, groups):
+        dest = lax.rem(me + k, groups)
+        copy = pltpu.make_async_remote_copy(
+            src_ref=src_hbm.at[:, dest],
+            dst_ref=parts.at[k],
+            send_sem=send_sems.at[k - 1],
+            recv_sem=recv_sems.at[k - 1],
+            device_id={"y": dest},
+            device_id_type=pl.DeviceIdType.MESH,
+        )
+        copy.start()
+        copies.append(copy)
+    local.wait()
+    for copy in copies:
+        copy.wait()
+
+    def get_part(j, c, cut):
+        return parts[j, c, :, cut]
+
+    def step(c, carry):
+        merge_chunk(heads, head_dim, groups, get_part, out_ref, c)
+        return carry
+
+    lax.fori_loop(0, chunks, step, 0)
+
+
+def y_exchange(by_y, heads, head_dim):
+    chunks, groups, rows_per, lanes_all = by_y.shape
+    kernel = functools.partial(y_exchange_kernel, heads, head_dim, groups)
+    return pl.pallas_call(
+        kernel,
+        out_shape=jax.ShapeDtypeStruct((chunks, rows_per, lanes_all), by_y.dtype),
+        in_specs=[pl.BlockSpec(memory_space=pl.ANY)],
+        out_specs=pl.BlockSpec(memory_space=pltpu.VMEM),
+        scratch_shapes=[
+            pltpu.VMEM((groups, chunks, rows_per, lanes_all), by_y.dtype),
+            pltpu.SemaphoreType.DMA(()),
+            pltpu.SemaphoreType.DMA((groups - 1,)),
+            pltpu.SemaphoreType.DMA((groups - 1,)),
+        ],
+        compiler_params=pltpu.CompilerParams(
+            collective_id=2, has_side_effects=True, vmem_limit_bytes=32 * 1024 * 1024
+        ),
+        cost_estimate=pl.CostEstimate(
+            flops=4 * by_y.size,
+            transcendentals=chunks * groups * rows_per * 128,
+            bytes_accessed=2 * by_y.size * 2,
+        ),
+    )(by_y)
+
+
 def per_device(
     queries,
     keys,
@@ -430,9 +531,9 @@
             rotated_q.reshape(tok_dev, width),
             rotated_k.reshape(tok_dev, width),
             values.reshape(tok_dev, width),
-            w_plane,
         ]
     )
+    w_all = lax.all_gather(w_plane[None], PAGES, axis=1, tiled=True)
     gathered = lax.all_gather(stacked, PAGES, axis=1, tiled=True)
     my_slots = device_at * slot_count + jnp.arange(slot_count, dtype=jnp.int32)
     cached_hit = page_table.reshape(-1)[None, :] == my_slots[:, None]
@@ -468,8 +569,12 @@
         page_devices,
     )
     paired = pair_merge(packed, head_count, head_dim)
-    received = lax.all_to_all(paired, "chips", 0, 0, tiled=True)
-    projected = combine_project(received, gathered, head_count, head_dim)
+    z_n = lax.axis_size("z")
+    y_n = lax.axis_size("y")
+    by_y = paired.reshape(z_n, y_n, tok_dev, paired.shape[-1])
+    merged = y_exchange(by_y, head_count, head_dim)
+    received = lax.all_to_all(merged, "z", 0, 0, tiled=True)
+    projected = combine_project(received, w_all, head_count, head_dim)
     head_groups = lax.axis_size("heads")
     summed = heads_sum(projected, head_groups)
     summed = summed.reshape(tok_dev, page_devices // head_groups, tok_dev)[:, :, :w_cols].reshape(
@@ -483,8 +588,9 @@
 
 def solution(mesh):
     heads_n, pages_n = mesh.devices.shape
+    z_n = pages_n // 8
     split = jax.sharding.Mesh(
-        mesh.devices.reshape(heads_n, pages_n // 2, 2), ("heads", "chips", "core")
+        mesh.devices.reshape(heads_n, z_n, 4, 2), ("heads", "z", "y", "core")
     )
     placed = (
         P(PAGES, "heads", None),

time: 280 us -> 261 us (0.932); the launches traced: 275 us -> 260 us
  waiting for transfers between devices: 168 us -> 109 us
  Pallas kernels: 60.3 us -> 108 us
  local copies, waits for them, and re-layouts: 21.7 us -> 18.2 us
    pallas_call x0 -> x1, Pallas kernels: none -> 50.5 us  [y_exchange(): pl.pallas_call(kernel, out_shape=jax.ShapeDtypeStruct((chunks, rows_per,...]
    all_to_all x1, waiting for transfers between devices: 66.2 us -> 19.4 us  [per_device(): received = lax.all_to_all(merged, 'z', 0, 0, tiled=True)]
    all_gather x1, waiting for transfers between devices: 102 us -> 89.6 us  [per_device(): gathered = lax.all_gather(stacked, PAGES, axis=1, tiled=True)]
    pallas_call x1, Pallas kernels: 9.8 us -> 3.04 us  [combine_project(): pl.pallas_call(kernel, out_shape=jax.ShapeDtypeStruct((rows_per, tokens),...]
    unnamed x22 -> x30, local copies, waits for them, and re-layouts: 5.15 us -> 5.93 us
  transfers between devices with their start and end apart: 2 -> 3, of which waited for: 2 -> 3; matrix products, arithmetic and copies ran while one was open for 3% -> 3% of each run, Pallas kernels for 0% -> 36%
where the time goes in v11:
time: 261 us; the launch traced here: 260 us
  waiting for transfers between devices  109 us (42%)
  Pallas kernels  108 us (41%)
  local copies, waits for them, and re-layouts  18.2 us (7%)
  between operations  14.3 us (5%)
  other arithmetic  6.8 us (3%)
  starting transfers between devices  3.64 us (1%)
    all_gather x1, waiting for transfers between devices, per_device(): gathered = lax.all_gather(stacked, PAGES, axis=1, tiled=True)  89.6 us
    pallas_call x1, Pallas kernels, y_exchange(): pl.pallas_call(kernel, out_shape=jax.ShapeDtypeStruct((chunks, rows_per,...  50.5 us
    pallas_call x1, Pallas kernels, local_attention(): pl.pallas_call(kernel, out_shape=(jax.ShapeDtypeStruct((chunks, rows_per,...  25.8 us
    all_to_all x1, waiting for transfers between devices, per_device(): received = lax.all_to_all(merged, 'z', 0, 0, tiled=True)  19.4 us
    pallas_call x1, Pallas kernels, pair_merge(): pl.pallas_call(kernel, out_shape=jax.ShapeDtypeStruct((chips, rows_per, l...  16 us
    pallas_call x1, Pallas kernels, heads_sum(): pl.pallas_call(kernel, out_shape=jax.ShapeDtypeStruct((rows, block), jnp....  12.3 us
    unnamed x30, local copies, waits for them, and re-layouts  5.93 us
  transfers between devices with their start and end apart: 3, of which 3 were waited for; matrix products, arithmetic and copies ran while one was open for 3% of the time, Pallas kernels for 36%

profile of v11, /device:TPU:4, one launch (start us, length us, event | category | flops | bytes accessed | tf_op | source)
XLA Modules:
  0.0 260.0 jit_solution(10140849573485421711)
XLA Ops:
  7.2 0.0 copy-start.7
  7.2 0.0 all-gather.4.cloned.1.call-start
  7.2 0.9 convert_element_type.40
  8.1 1.0 slice.25
  9.1 0.0 copy-start.8
  9.2 0.9 convert_element_type.43
  10.1 0.0 copy-start.10
  10.1 0.0 copy-start.11
  10.1 0.0 copy-start.3
  10.1 1.1 slice.28
  11.3 0.7 select_reduce_fusion
  12.0 0.2 multiply_cosine_fusion
  12.2 0.3 subtract_convert_fusion.1
  12.6 0.3 pad_maximum_fusion.1
  13.0 0.0 copy-done.7
  13.0 0.7 pad_maximum_fusion
  13.7 0.0 all-gather.4.cloned.1.call-update
  13.8 0.0 all-gather.6.cloned.1.call-start
  13.8 0.0 copy-done.8
  13.8 0.6 pad.4
  14.5 0.0 all-gather.6.cloned.1.call-update
  14.5 0.0 copy-done.10
  14.5 0.1 eq.61
  14.6 0.0 copy-done.11
  14.6 0.1 eq.65
  14.7 0.0 copy-done.3
  14.7 0.0 copy-start.4
  14.7 2.0 reshape.157.kc_ref
  16.7 0.0 copy-done.4
  16.7 0.0 copy-start.14
  16.7 2.0 reshape.158.vc_ref
  18.7 0.2 fusion.1.sfresh_ref
  18.9 0.0 copy-start.12
  18.9 0.2 compare_reduce_fusion.1
  19.0 0.2 fusion
  19.2 0.5 broadcast_select_fusion
  19.8 0.0 copy-done.14
  19.8 0.1 select_reduce_fusion.1
  19.9 0.2 compare_reduce_fusion
  20.1 0.6 fusion.5.skind_ref
  20.6 89.6 %all-gather.4.cloned.1.call-done.q_ref.kf_ref.vf_ref = bf16[3,4608,512]{2,1,0:T(8,128)(2,1)} async-done(((bf16[3,72,512]{2,1,0:T(8,128)(2,1)}), bf16[3,4608,512]{2,1,0:T(8,128)(2,1)}) %all-gather.4.cloned.1.call-update) | async-done | bytes 14155792 | tf_op jit(solution)/shard_map/all_gather | solution.py:537
  110.2 0.0 copy-done.12
  110.2 0.0 copy-done.13
  110.2 25.8 %shard_map.121 = (bf16[64,72,640]{2,1,0:T(8,128)(2,1)}, bf16[12,128,512]{2,1,0:T(8,128)(2,1)}, bf16[12,128,512]{2,1,0:T(8,128)(2,1)}) custom-call(s32[12]{0:T(128)} %copy-done.13, s32[12]{0:T(128)} %fusion.5.skind_ref, s32[12]{0:T(128)} %get-tuple-element.9.slim_ref, s32[12]{0:T(128)} %copy-done.12, ...), custom_call_target="tpu_custom_call" | custom-call | flops 2415919104 | bytes 16908288 | tf_op jit(solution)/shard_map/pallas_call | solution.py:144
  136.0 0.0 copy-start
  136.0 2.7 %copy-done = bf16[64,72,640]{2,1,0:T(8,128)(2,1)S(1)} copy-done((bf16[64,72,640]{2,1,0:T(8,128)(2,1)S(1)}, bf16[64,72,640]{2,1,0:T(8,128)(2,1)}, u32[]{:S(2)}) %copy-start) | copy-done | bytes 5898264
  138.7 16.0 %shard_map.122 = bf16[32,72,640]{2,1,0:T(8,128)(2,1)S(1)} custom-call(bf16[32,2,72,640]{3,2,1,0:T(8,128)(2,1)S(1)} %bitcast.6), custom_call_target="tpu_custom_call" | custom-call | flops 8847360 | bytes 8847360 | tf_op jit(solution)/shard_map/pallas_call | solution.py:313
  154.7 0.0 copy-start.6
  154.7 50.5 %shard_map.123 = bf16[8,72,640]{2,1,0:T(8,128)(2,1)} custom-call(bf16[8,4,72,640]{3,2,1,0:T(8,128)(2,1)S(1)} %bitcast.5), custom_call_target="tpu_custom_call" | custom-call | flops 5898240 | bytes 5898240 | tf_op jit(solution)/shard_map/pallas_call | solution.py:475
  205.2 3.6 %all-to-all-start = ((bf16[8,72,640]{2,1,0:T(8,128)(2,1)}), bf16[8,72,640]{2,1,0:T(8,128)(2,1)S(1)}, u32[]{:S(2)}, u32[]{:S(2)}) async-start(bf16[8,72,640]{2,1,0:T(8,128)(2,1)} %shard_map.123), calls=%async_computation | async-start | bytes 1474560 | tf_op jit(solution)/shard_map/all_to_all | solution.py:576
  208.8 0.0 copy-done.6
  208.8 1.9 reshape.163
  210.7 0.5 all-gather.6.cloned.1.call-done
  211.1 19.4 %all-to-all-done.recv_ref = bf16[8,72,640]{2,1,0:T(8,128)(2,1)S(1)} async-done(((bf16[8,72,640]{2,1,0:T(8,128)(2,1)}), bf16[8,72,640]{2,1,0:T(8,128)(2,1)S(1)}, u32[]{:S(2)}, u32[]{:S(2)}) %all-to-all-start) | async-done | bytes 737312 | tf_op jit(solution)/shard_map/all_to_all | solution.py:576
  230.5 2.3 copy-done.1
  232.8 3.0 %shard_map.124.proj_hbm = bf16[72,4608]{1,0:T(8,128)(2,1)S(1)} custom-call(bf16[8,72,640]{2,1,0:T(8,128)(2,1)S(1)} %all-to-all-done.recv_ref, bf16[1,4608,512]{2,1,0:T(8,128)(2,1)S(1)} %bitcast.7), custom_call_target="tpu_custom_call" | custom-call | flops 341213184 | bytes 6119424 | tf_op jit(solution)/shard_map/pallas_call | solution.py:225
  235.9 0.8 copy-done.2
  236.7 0.0 copy-done.5
  236.7 1.8 reshape.164
  238.5 12.3 %shard_map.125 = f32[72,1152]{1,0:T(8,128)} custom-call(bf16[72,4608]{1,0:T(8,128)(2,1)} %copy-done.2), custom_call_target="tpu_custom_call" | custom-call | flops 331776 | bytes 995328 | tf_op jit(solution)/shard_map/pallas_call | solution.py:375
  250.8 1.5 reshape.161
  252.3 0.2 reshape.162
  252.5 0.0 copy-done.9
  252.5 0.7 add_convert_fusion
  (12 shorter events, 0.2 us)
Async XLA Ops:
  7.2 5.8 %copy-start.7 = (bf16[72,4,128]{2,1,0:T(4,128)(2,1)S(1)}, bf16[72,4,128]{2,1,0:T(4,128)(2,1)}, u32[]{:S(2)}) copy-start(bf16[72,4,128]{2,1,0:T(4,128)(2,1)} %param.12) | copy-start | bytes 221188
  7.2 103.0 %all-gather.4.cloned.1.call-start = ((), (), s32[]{:S(2)}) async-start(), calls=%async_computation.1 | async-start | bytes 14376960 | tf_op jit(solution)/shard_map/all_gather | solution.py:537
  9.1 4.7 %copy-start.8 = (bf16[512,64]{0,1:T(8,128)(2,1)S(1)}, bf16[512,64]{0,1:T(8,128)(2,1)}, u32[]{:S(2)}) copy-start(bf16[512,64]{0,1:T(8,128)(2,1)} %param.18) | copy-start | bytes 196612
  10.1 4.4 %copy-start.10 = (s32[6,6]{1,0:T(8,128)S(1)}, s32[6,6]{1,0:T(8,128)}, u32[]{:S(2)}) copy-start(s32[6,6]{1,0:T(8,128)} %param.17) | copy-start | bytes 436
  10.1 4.5 %copy-start.11 = (s32[6,122]{1,0:T(8,128)S(1)}, s32[6,122]{1,0:T(8,128)}, u32[]{:S(2)}) copy-start(s32[6,122]{1,0:T(8,128)} %param.16) | copy-start | bytes 8788
  10.1 4.6 %copy-start.3 = (bf16[12,128,4,128]{3,2,1,0:T(4,128)(2,1)S(1)}, bf16[12,128,4,128]{3,2,1,0:T(4,128)(2,1)}, u32[]{:S(2)}) copy-start(bf16[12,128,4,128]{3,2,1,0:T(4,128)(2,1)} %param.13) | copy-start | bytes 4718596
  13.8 197.4 %all-gather.6.cloned.1.call-start = ((), (), s32[]{:S(2)}) async-start(), calls=%async_computation.2 | async-start | bytes 4792320 | tf_op jit(solution)/shard_map/all_gather | solution.py:536
  14.7 2.0 copy-start.4
  16.7 3.1 %copy-start.14 = (s32[6]{0:T(128)S(1)}, s32[6]{0:T(128)}, u32[]{:S(2)}) copy-start(s32[6]{0:T(128)} %param.15) | copy-start | bytes 76
  18.9 91.3 %copy-start.12 = (s32[12]{0:T(128)}, s32[12]{0:T(128)S(1)}, u32[]{:S(2)}) copy-start(s32[12]{0:T(128)S(1)} %fusion.1.sfresh_ref) | copy-start | bytes 148
  19.8 90.4 %copy-start.13 = (s32[12]{0:T(128)}, s32[12]{0:T(128)S(1)}, u32[]{:S(2)}) copy-start(s32[12]{0:T(128)S(1)} %get-tuple-element.17.sreq_ref) | copy-start | bytes 148
  136.0 2.7 %copy-start = (bf16[64,72,640]{2,1,0:T(8,128)(2,1)S(1)}, bf16[64,72,640]{2,1,0:T(8,128)(2,1)}, u32[]{:S(2)}) copy-start(bf16[64,72,640]{2,1,0:T(8,128)(2,1)} %get-tuple-element.6) | copy-start | bytes 17694724
  154.7 54.1 %copy-start.6 = (bf16[12,128,512]{2,1,0:T(8,128)(2,1)S(1)}, bf16[12,128,512]{2,1,0:T(8,128)(2,1)}, u32[]{:S(2)}) copy-start(bf16[12,128,512]{2,1,0:T(8,128)(2,1)} %get-tuple-element.7) | copy-start | bytes 4718596
  205.2 25.2 %all-to-all-start = ((bf16[8,72,640]{2,1,0:T(8,128)(2,1)}), bf16[8,72,640]{2,1,0:T(8,128)(2,1)S(1)}, u32[]{:S(2)}, u32[]{:S(2)}) async-start(bf16[8,72,640]{2,1,0:T(8,128)(2,1)} %shard_map.123), calls=%async_computation | async-start | bytes 1474560 | tf_op jit(solution)/shard_map/all_to_all | solution.py:576
  230.5 2.3 copy-start.1
  232.8 3.9 %copy-start.5 = (bf16[12,128,512]{2,1,0:T(8,128)(2,1)S(1)}, bf16[12,128,512]{2,1,0:T(8,128)(2,1)}, u32[]{:S(2)}) copy-start(bf16[12,128,512]{2,1,0:T(8,128)(2,1)} %get-tuple-element.8) | copy-start | bytes 4718596
  235.9 0.9 copy-start.2
  238.5 14.0 %copy-start.9 = (f32[1024]{0:T(1024)S(1)}, f32[1024]{0:T(1024)}, u32[]{:S(2)}) copy-start(f32[1024]{0:T(1024)} %param.19) | copy-start | bytes 12292
Sparse Core Ops, SparseCore 0:
  13.9 96.2 all-gather.3
  113.5 97.5 all-gather.5

commit v12 on v11

--- a/solution.py
+++ b/solution.py
@@ -494,6 +494,68 @@
     )(by_y)
 
 
+def z_combine_kernel(heads, head_dim, groups, src_hbm, w_ref, out_ref, parts, o_acc, l_acc,
+                     own_sem, send_sems, recv_sems):
+    me = lax.axis_index("z")
+    barrier = pltpu.get_barrier_semaphore()
+    for k in range(1, groups):
+        pl.semaphore_signal(
+            barrier, inc=1, device_id={"z": lax.rem(me + k, groups)},
+            device_id_type=pl.DeviceIdType.MESH,
+        )
+    pl.semaphore_wait(barrier, groups - 1)
+    local = pltpu.make_async_copy(src_hbm.at[me], parts.at[0], own_sem)
+    local.start()
+    copies = []
+    for k in range(1, groups):
+        dest = lax.rem(me + k, groups)
+        copy = pltpu.make_async_remote_copy(
+            src_ref=src_hbm.at[dest],
+            dst_ref=parts.at[k],
+            send_sem=send_sems.at[k - 1],
+            recv_sem=recv_sems.at[k - 1],
+            device_id={"z": dest},
+            device_id_type=pl.DeviceIdType.MESH,
+        )
+        copy.start()
+        copies.append(copy)
+    local.wait()
+    for copy in copies:
+        copy.wait()
+    combine_kernel(heads, head_dim, parts, w_ref, out_ref, o_acc, l_acc)
+
+
+def z_combine(merged, w_all, heads, head_dim):
+    groups, rows_per, lanes_all = merged.shape
+    _, tokens, width = w_all.shape
+    kernel = functools.partial(z_combine_kernel, heads, head_dim, groups)
+    return pl.pallas_call(
+        kernel,
+        out_shape=jax.ShapeDtypeStruct((rows_per, tokens), jnp.bfloat16),
+        in_specs=[
+            pl.BlockSpec(memory_space=pl.ANY),
+            pl.BlockSpec(memory_space=pltpu.VMEM),
+        ],
+        out_specs=pl.BlockSpec(memory_space=pltpu.VMEM),
+        scratch_shapes=[
+            pltpu.VMEM((groups, rows_per, lanes_all), merged.dtype),
+            pltpu.VMEM((rows_per, width), jnp.float32),
+            pltpu.VMEM((rows_per, 128), jnp.float32),
+            pltpu.SemaphoreType.DMA(()),
+            pltpu.SemaphoreType.DMA((groups - 1,)),
+            pltpu.SemaphoreType.DMA((groups - 1,)),
+        ],
+        compiler_params=pltpu.CompilerParams(
+            collective_id=3, has_side_effects=True, vmem_limit_bytes=48 * 1024 * 1024
+        ),
+        cost_estimate=pl.CostEstimate(
+            flops=2 * rows_per * tokens * width + 4 * merged.size,
+            transcendentals=groups * rows_per * 128,
+            bytes_accessed=2 * merged.size * 2 + tokens * width * 2 + rows_per * tokens * 2,
+        ),
+    )(merged, w_all)
+
+
 def per_device(
     queries,
     keys,
@@ -573,8 +635,7 @@
     y_n = lax.axis_size("y")
     by_y = paired.reshape(z_n, y_n, tok_dev, paired.shape[-1])
     merged = y_exchange(by_y, head_count, head_dim)
-    received = lax.all_to_all(merged, "z", 0, 0, tiled=True)
-    projected = combine_project(received, w_all, head_count, head_dim)
+    projected = z_combine(merged, w_all, head_count, head_dim)
     head_groups = lax.axis_size("heads")
     summed = heads_sum(projected, head_groups)
     summed = summed.reshape(tok_dev, page_devices // head_groups, tok_dev)[:, :, :w_cols].reshape(

time: 261 us -> 265 us (1.015)
  Pallas kernels: 108 us -> 128 us
  waiting for transfers between devices: 109 us -> 96.4 us
  starting transfers between devices: 3.64 us -> 0.08 us
    pallas_call x1, Pallas kernels: 3.04 us -> 23.5 us  [z_combine(): pl.pallas_call(kernel, out_shape=jax.ShapeDtypeStruct((rows_per, tokens),...]
    all_to_all x1 -> x0, waiting for transfers between devices: 19.4 us -> none  [per_device(): received = lax.all_to_all(merged, 'z', 0, 0, tiled=True)]
    all_gather x1, waiting for transfers between devices: 0.46 us -> 6.75 us  [per_device(): w_all = lax.all_gather(w_plane[None], PAGES, axis=1, tiled=True)]
    all_to_all x1 -> x0, starting transfers between devices: 3.56 us -> none  [per_device(): received = lax.all_to_all(merged, 'z', 0, 0, tiled=True)]
  transfers between devices with their start and end apart: 3 -> 2, of which waited for: 3 -> 2; matrix products, arithmetic and copies ran while one was open for 3% -> 3% of each run, Pallas kernels for 36% -> 35%
where the time goes in v12:
time: 265 us; the launch traced here: 264 us
  Pallas kernels  128 us (48%)
  waiting for transfers between devices  96.4 us (36%)
  local copies, waits for them, and re-layouts  18.2 us (7%)
  between operations  14.3 us (5%)
  other arithmetic  6.78 us (3%)
    all_gather x1, waiting for transfers between devices, per_device(): gathered = lax.all_gather(stacked, PAGES, axis=1, tiled=True)  89.6 us
    pallas_call x1, Pallas kernels, y_exchange(): pl.pallas_call(kernel, out_shape=jax.ShapeDtypeStruct((chunks, rows_per,...  49.9 us
    pallas_call x1, Pallas kernels, local_attention(): pl.pallas_call(kernel, out_shape=(jax.ShapeDtypeStruct((chunks, rows_per,...  24.7 us
    pallas_call x1, Pallas kernels, z_combine(): pl.pallas_call(kernel, out_shape=jax.ShapeDtypeStruct((rows_per, tokens),...  23.5 us
    pallas_call x1, Pallas kernels, pair_merge(): pl.pallas_call(kernel, out_shape=jax.ShapeDtypeStruct((chips, rows_per, l...  18.1 us
    pallas_call x1, Pallas kernels, heads_sum(): pl.pallas_call(kernel, out_shape=jax.ShapeDtypeStruct((rows, block), jnp....  11.7 us
    all_gather x1, waiting for transfers between devices, per_device(): w_all = lax.all_gather(w_plane[None], PAGES, axis=1, tiled=True)  6.75 us
    unnamed x30, local copies, waits for them, and re-layouts  5.91 us
  transfers between devices with their start and end apart: 2, of which 2 were waited for; matrix products, arithmetic and copies ran while one was open for 3% of the time, Pallas kernels for 35%

profile of v12, /device:TPU:4, one launch (start us, length us, event | category | flops | bytes accessed | tf_op | source)
XLA Modules:
  0.0 263.7 jit_solution(11625904573901774233)
XLA Ops:
  7.2 0.0 copy-start.7
  7.2 0.0 all-gather.4.cloned.1.call-start
  7.2 0.9 convert_element_type.40
  8.1 1.0 slice.25
  9.1 0.0 copy-start.8
  9.2 0.9 convert_element_type.43
  10.1 0.0 copy-start.10
  10.1 0.0 copy-start.11
  10.1 0.0 copy-start.3
  10.1 1.1 slice.28
  11.3 0.7 select_reduce_fusion
  12.0 0.2 multiply_cosine_fusion
  12.2 0.3 subtract_convert_fusion.1
  12.6 0.3 pad_maximum_fusion.1
  13.0 0.0 copy-done.7
  13.0 0.7 pad_maximum_fusion
  13.7 0.0 all-gather.4.cloned.1.call-update
  13.8 0.0 all-gather.6.cloned.1.call-start
  13.8 0.0 copy-done.8
  13.8 0.6 pad.4
  14.5 0.0 all-gather.6.cloned.1.call-update
  14.5 0.0 copy-done.10
  14.5 0.1 eq.61
  14.6 0.0 copy-done.11
  14.6 0.1 eq.65
  14.7 0.0 copy-done.3
  14.7 0.0 copy-start.4
  14.7 2.0 reshape.157.kc_ref
  16.7 0.0 copy-done.4
  16.7 0.0 copy-start.14
  16.7 2.0 reshape.158.vc_ref
  18.7 0.2 fusion.1.sfresh_ref
  18.9 0.0 copy-start.12
  18.9 0.2 compare_reduce_fusion.1
  19.1 0.2 fusion
  19.2 0.6 broadcast_select_fusion
  19.8 0.0 copy-start.13
  19.8 0.0 copy-done.14
  19.8 0.1 select_reduce_fusion.1
  19.9 0.2 compare_reduce_fusion
  20.1 0.5 fusion.5.skind_ref
  20.6 89.6 %all-gather.4.cloned.1.call-done.q_ref.kf_ref.vf_ref = bf16[3,4608,512]{2,1,0:T(8,128)(2,1)} async-done(((bf16[3,72,512]{2,1,0:T(8,128)(2,1)}), bf16[3,4608,512]{2,1,0:T(8,128)(2,1)}) %all-gather.4.cloned.1.call-update) | async-done | bytes 14155792 | tf_op jit(solution)/shard_map/all_gather | solution.py:599
  110.2 0.0 copy-done.12
  110.2 0.0 copy-done.13
  110.2 24.7 %shard_map.121 = (bf16[64,72,640]{2,1,0:T(8,128)(2,1)}, bf16[12,128,512]{2,1,0:T(8,128)(2,1)}, bf16[12,128,512]{2,1,0:T(8,128)(2,1)}) custom-call(s32[12]{0:T(128)} %copy-done.13, s32[12]{0:T(128)} %fusion.5.skind_ref, s32[12]{0:T(128)} %get-tuple-element.9.slim_ref, s32[12]{0:T(128)} %copy-done.12, ...), custom_call_target="tpu_custom_call" | custom-call | flops 2415919104 | bytes 16908288 | tf_op jit(solution)/shard_map/pallas_call | solution.py:144
  134.9 0.0 copy-start
  134.9 2.7 %copy-done = bf16[64,72,640]{2,1,0:T(8,128)(2,1)S(1)} copy-done((bf16[64,72,640]{2,1,0:T(8,128)(2,1)S(1)}, bf16[64,72,640]{2,1,0:T(8,128)(2,1)}, u32[]{:S(2)}) %copy-start) | copy-done | bytes 5898264
  137.6 18.1 %shard_map.122 = bf16[32,72,640]{2,1,0:T(8,128)(2,1)S(1)} custom-call(bf16[32,2,72,640]{3,2,1,0:T(8,128)(2,1)S(1)} %bitcast.6), custom_call_target="tpu_custom_call" | custom-call | flops 8847360 | bytes 8847360 | tf_op jit(solution)/shard_map/pallas_call | solution.py:313
  155.7 49.9 %shard_map.123.src_hbm = bf16[8,72,640]{2,1,0:T(8,128)(2,1)S(1)} custom-call(bf16[8,4,72,640]{3,2,1,0:T(8,128)(2,1)S(1)} %bitcast.5), custom_call_target="tpu_custom_call" | custom-call | flops 5898240 | bytes 5898240 | tf_op jit(solution)/shard_map/pallas_call | solution.py:475
  205.6 6.8 %all-gather.6.cloned.1.call-done = bf16[4608,512]{1,0:T(8,128)(2,1)} async-done(((bf16[72,512]{1,0:T(8,128)(2,1)}), bf16[4608,512]{1,0:T(8,128)(2,1)}) %all-gather.6.cloned.1.call-update) | async-done | bytes 4718608 | tf_op jit(solution)/shard_map/all_gather | solution.py:598
  212.4 2.3 copy-done.1
  214.7 23.5 %shard_map.124.proj_hbm = bf16[72,4608]{1,0:T(8,128)(2,1)S(1)} custom-call(bf16[8,72,640]{2,1,0:T(8,128)(2,1)S(1)} %shard_map.123.src_hbm, bf16[1,4608,512]{2,1,0:T(8,128)(2,1)S(1)} %bitcast.7), custom_call_target="tpu_custom_call" | custom-call | flops 341213184 | bytes 6856704 | tf_op jit(solution)/shard_map/pallas_call | solution.py:532
  238.3 0.0 copy-start.2
  238.3 0.8 copy-done.2
  239.1 11.7 %shard_map.125 = f32[72,1152]{1,0:T(8,128)} custom-call(bf16[72,4608]{1,0:T(8,128)(2,1)} %copy-done.2), custom_call_target="tpu_custom_call" | custom-call | flops 331776 | bytes 995328 | tf_op jit(solution)/shard_map/pallas_call | solution.py:375
  250.8 1.5 reshape.161
  252.3 0.2 reshape.162
  252.5 0.0 copy-done.6
  252.5 0.0 copy-start.5
  252.5 1.9 reshape.163
  254.4 0.0 copy-done.5
  254.4 1.8 reshape.164
  256.2 0.0 copy-done.9
  256.2 0.7 add_convert_fusion
  (10 shorter events, 0.2 us)
Async XLA Ops:
  7.2 5.8 %copy-start.7 = (bf16[72,4,128]{2,1,0:T(4,128)(2,1)S(1)}, bf16[72,4,128]{2,1,0:T(4,128)(2,1)}, u32[]{:S(2)}) copy-start(bf16[72,4,128]{2,1,0:T(4,128)(2,1)} %param.12) | copy-start | bytes 221188
  7.2 103.0 %all-gather.4.cloned.1.call-start = ((), (), s32[]{:S(2)}) async-start(), calls=%async_computation | async-start | bytes 14376960 | tf_op jit(solution)/shard_map/all_gather | solution.py:599
  9.1 4.7 %copy-start.8 = (bf16[512,64]{0,1:T(8,128)(2,1)S(1)}, bf16[512,64]{0,1:T(8,128)(2,1)}, u32[]{:S(2)}) copy-start(bf16[512,64]{0,1:T(8,128)(2,1)} %param.18) | copy-start | bytes 196612
  10.1 4.4 %copy-start.10 = (s32[6,6]{1,0:T(8,128)S(1)}, s32[6,6]{1,0:T(8,128)}, u32[]{:S(2)}) copy-start(s32[6,6]{1,0:T(8,128)} %param.17) | copy-start | bytes 436
  10.1 4.5 %copy-start.11 = (s32[6,122]{1,0:T(8,128)S(1)}, s32[6,122]{1,0:T(8,128)}, u32[]{:S(2)}) copy-start(s32[6,122]{1,0:T(8,128)} %param.16) | copy-start | bytes 8788
  10.1 4.6 %copy-start.3 = (bf16[12,128,4,128]{3,2,1,0:T(4,128)(2,1)S(1)}, bf16[12,128,4,128]{3,2,1,0:T(4,128)(2,1)}, u32[]{:S(2)}) copy-start(bf16[12,128,4,128]{3,2,1,0:T(4,128)(2,1)} %param.13) | copy-start | bytes 4718596
  13.8 198.6 %all-gather.6.cloned.1.call-start = ((), (), s32[]{:S(2)}) async-start(), calls=%async_computation.1 | async-start | bytes 4792320 | tf_op jit(solution)/shard_map/all_gather | solution.py:598
  14.7 2.0 copy-start.4
  16.7 3.1 %copy-start.14 = (s32[6]{0:T(128)S(1)}, s32[6]{0:T(128)}, u32[]{:S(2)}) copy-start(s32[6]{0:T(128)} %param.15) | copy-start | bytes 76
  18.9 91.3 %copy-start.12 = (s32[12]{0:T(128)}, s32[12]{0:T(128)S(1)}, u32[]{:S(2)}) copy-start(s32[12]{0:T(128)S(1)} %fusion.1.sfresh_ref) | copy-start | bytes 148
  19.8 90.4 %copy-start.13 = (s32[12]{0:T(128)}, s32[12]{0:T(128)S(1)}, u32[]{:S(2)}) copy-start(s32[12]{0:T(128)S(1)} %get-tuple-element.17.sreq_ref) | copy-start | bytes 148
  134.9 2.7 %copy-start = (bf16[64,72,640]{2,1,0:T(8,128)(2,1)S(1)}, bf16[64,72,640]{2,1,0:T(8,128)(2,1)}, u32[]{:S(2)}) copy-start(bf16[64,72,640]{2,1,0:T(8,128)(2,1)} %get-tuple-element.6) | copy-start | bytes 17694724
  212.4 2.3 copy-start.1
  238.3 0.8 copy-start.2
  239.1 13.4 %copy-start.6 = (bf16[12,128,512]{2,1,0:T(8,128)(2,1)S(1)}, bf16[12,128,512]{2,1,0:T(8,128)(2,1)}, u32[]{:S(2)}) copy-start(bf16[12,128,512]{2,1,0:T(8,128)(2,1)} %get-tuple-element.7) | copy-start | bytes 4718596
  252.5 1.9 copy-start.5
  254.4 1.8 copy-start.9
Sparse Core Ops, SparseCore 0:
  13.9 96.2 all-gather.3
  113.5 98.8 all-gather.5

commit v13 on v12

--- a/solution.py
+++ b/solution.py
@@ -494,8 +494,7 @@
     )(by_y)
 
 
-def z_combine_kernel(heads, head_dim, groups, src_hbm, w_ref, out_ref, parts, o_acc, l_acc,
-                     own_sem, send_sems, recv_sems):
+def z_exchange_kernel(groups, src_hbm, out_ref, parts, own_sem, send_sems, recv_sems):
     me = lax.axis_index("z")
     barrier = pltpu.get_barrier_semaphore()
     for k in range(1, groups):
@@ -522,39 +521,28 @@
     local.wait()
     for copy in copies:
         copy.wait()
-    combine_kernel(heads, head_dim, parts, w_ref, out_ref, o_acc, l_acc)
-
-
-def z_combine(merged, w_all, heads, head_dim):
+    out_ref[...] = parts[...]
+
+
+def z_exchange(merged):
     groups, rows_per, lanes_all = merged.shape
-    _, tokens, width = w_all.shape
-    kernel = functools.partial(z_combine_kernel, heads, head_dim, groups)
+    kernel = functools.partial(z_exchange_kernel, groups)
     return pl.pallas_call(
         kernel,
-        out_shape=jax.ShapeDtypeStruct((rows_per, tokens), jnp.bfloat16),
-        in_specs=[
-            pl.BlockSpec(memory_space=pl.ANY),
-            pl.BlockSpec(memory_space=pltpu.VMEM),
-        ],
+        out_shape=jax.ShapeDtypeStruct(merged.shape, merged.dtype),
+        in_specs=[pl.BlockSpec(memory_space=pl.ANY)],
         out_specs=pl.BlockSpec(memory_space=pltpu.VMEM),
         scratch_shapes=[
-            pltpu.VMEM((groups, rows_per, lanes_all), merged.dtype),
-            pltpu.VMEM((rows_per, width), jnp.float32),
-            pltpu.VMEM((rows_per, 128), jnp.float32),
+            pltpu.VMEM(merged.shape, merged.dtype),
             pltpu.SemaphoreType.DMA(()),
             pltpu.SemaphoreType.DMA((groups - 1,)),
             pltpu.SemaphoreType.DMA((groups - 1,)),
         ],
-        compiler_params=pltpu.CompilerParams(
-            collective_id=3, has_side_effects=True, vmem_limit_bytes=48 * 1024 * 1024
-        ),
+        compiler_params=pltpu.CompilerParams(collective_id=3, has_side_effects=True),
         cost_estimate=pl.CostEstimate(
-            flops=2 * rows_per * tokens * width + 4 * merged.size,
-            transcendentals=groups * rows_per * 128,
-            bytes_accessed=2 * merged.size * 2 + tokens * width * 2 + rows_per * tokens * 2,
-        ),
-    )(merged, w_all)
-
+            flops=0, transcendentals=0, bytes_accessed=3 * merged.size * 2
+        ),
+    )(merged)
 
 def per_device(
     queries,
@@ -635,7 +623,8 @@
     y_n = lax.axis_size("y")
     by_y = paired.reshape(z_n, y_n, tok_dev, paired.shape[-1])
     merged = y_exchange(by_y, head_count, head_dim)
-    projected = z_combine(merged, w_all, head_count, head_dim)
+    received = z_exchange(merged)
+    projected = combine_project(received, w_all, head_count, head_dim)
     head_groups = lax.axis_size("heads")
     summed = heads_sum(projected, head_groups)
     summed = summed.reshape(tok_dev, page_devices // head_groups, tok_dev)[:, :, :w_cols].reshape(

time: 265 us -> 259 us (0.977)
  waiting for transfers between devices: 96.4 us -> 89.6 us
    all_gather x1, waiting for transfers between devices: 6.75 us -> 0.02 us  [per_device(): w_all = lax.all_gather(w_plane[None], PAGES, axis=1, tiled=True)]
    pallas_call x1 -> x2, Pallas kernels: 23.5 us -> 27.8 us  [the longest x1 24.8 us: z_exchange(): pl.pallas_call(kernel, out_shape=jax.ShapeDtypeStruct(merged.shape, merge...]
    pallas_call x1, Pallas kernels: 24.7 us -> 21.7 us  [local_attention(): pl.pallas_call(kernel, out_shape=(jax.ShapeDtypeStruct((chunks, rows_per,...]
    unnamed x30 -> x34, local copies, waits for them, and re-layouts: 5.91 us -> 7.88 us
  transfers between devices with their start and end apart: 2 -> 2, of which waited for: 2 -> 1; matrix products, arithmetic and copies ran while one was open for 3% -> 3% of each run, Pallas kernels for 35% -> 44%
where the time goes in v13:
time: 259 us
  Pallas kernels  128 us (49%)
  waiting for transfers between devices  89.6 us (35%)
  local copies, waits for them, and re-layouts  20.2 us (8%)
  between operations  14.3 us (6%)
  other arithmetic  6.8 us (3%)
    all_gather x1, waiting for transfers between devices, per_device(): gathered = lax.all_gather(stacked, PAGES, axis=1, tiled=True)  89.6 us
    pallas_call x1, Pallas kernels, y_exchange(): pl.pallas_call(kernel, out_shape=jax.ShapeDtypeStruct((chunks, rows_per,...  50.7 us
    pallas_call x1, Pallas kernels, z_exchange(): pl.pallas_call(kernel, out_shape=jax.ShapeDtypeStruct(merged.shape, merge...  24.8 us
    pallas_call x1, Pallas kernels, local_attention(): pl.pallas_call(kernel, out_shape=(jax.ShapeDtypeStruct((chunks, rows_per,...  21.7 us
    pallas_call x1, Pallas kernels, pair_merge(): pl.pallas_call(kernel, out_shape=jax.ShapeDtypeStruct((chips, rows_per, l...  16.3 us
    pallas_call x1, Pallas kernels, heads_sum(): pl.pallas_call(kernel, out_shape=jax.ShapeDtypeStruct((rows, block), jnp....  11 us
    unnamed x34, local copies, waits for them, and re-layouts  7.88 us
  transfers between devices with their start and end apart: 2, of which 1 were waited for; matrix products, arithmetic and copies ran while one was open for 3% of the time, Pallas kernels for 44%

profile of v13, /device:TPU:4, one launch (start us, length us, event | category | flops | bytes accessed | tf_op | source)
XLA Modules:
  0.0 258.5 jit_solution(13749936325767892520)
XLA Ops:
  7.2 0.0 copy-start.9
  7.2 0.0 all-gather.4.cloned.1.call-start
  7.2 0.9 convert_element_type.40
  8.1 1.0 slice.25
  9.1 0.0 copy-start.10
  9.2 0.9 convert_element_type.43
  10.1 0.0 copy-start.12
  10.1 0.0 copy-start.13
  10.1 0.0 copy-start.5
  10.1 1.1 slice.28
  11.3 0.7 select_reduce_fusion
  12.0 0.2 multiply_cosine_fusion
  12.2 0.3 subtract_convert_fusion.1
  12.6 0.3 pad_maximum_fusion.1
  13.0 0.0 copy-done.9
  13.0 0.7 pad_maximum_fusion
  13.7 0.0 all-gather.4.cloned.1.call-update
  13.8 0.0 all-gather.6.cloned.1.call-start
  13.8 0.0 copy-done.10
  13.8 0.6 pad.4
  14.5 0.0 all-gather.6.cloned.1.call-update
  14.5 0.0 copy-done.12
  14.5 0.1 eq.61
  14.6 0.0 copy-done.13
  14.6 0.1 eq.65
  14.7 0.0 copy-done.5
  14.7 0.0 copy-start.6
  14.7 2.0 reshape.157.kc_ref
  16.7 0.0 copy-done.6
  16.7 2.0 reshape.158.vc_ref
  18.7 0.2 fusion.1.sfresh_ref
  18.9 0.2 compare_reduce_fusion.1
  19.0 0.2 fusion
  19.2 0.5 broadcast_select_fusion
  19.8 0.0 copy-done.16
  19.8 0.1 select_reduce_fusion.1
  19.9 0.2 compare_reduce_fusion
  20.1 0.6 fusion.5.skind_ref
  20.6 89.6 %all-gather.4.cloned.1.call-done.q_ref.kf_ref.vf_ref = bf16[3,4608,512]{2,1,0:T(8,128)(2,1)} async-done(((bf16[3,72,512]{2,1,0:T(8,128)(2,1)}), bf16[3,4608,512]{2,1,0:T(8,128)(2,1)}) %all-gather.4.cloned.1.call-update) | async-done | bytes 14155792 | tf_op jit(solution)/shard_map/all_gather | solution.py:587
  110.2 0.0 copy-done.14
  110.2 0.0 copy-done.15
  110.2 21.7 %shard_map.121 = (bf16[64,72,640]{2,1,0:T(8,128)(2,1)}, bf16[12,128,512]{2,1,0:T(8,128)(2,1)}, bf16[12,128,512]{2,1,0:T(8,128)(2,1)}) custom-call(s32[12]{0:T(128)} %copy-done.15, s32[12]{0:T(128)} %fusion.5.skind_ref, s32[12]{0:T(128)} %get-tuple-element.9.slim_ref, s32[12]{0:T(128)} %copy-done.14, ...), custom_call_target="tpu_custom_call" | custom-call | flops 2415919104 | bytes 16908288 | tf_op jit(solution)/shard_map/pallas_call | solution.py:144
  131.9 2.7 %copy-done = bf16[64,72,640]{2,1,0:T(8,128)(2,1)S(1)} copy-done((bf16[64,72,640]{2,1,0:T(8,128)(2,1)S(1)}, bf16[64,72,640]{2,1,0:T(8,128)(2,1)}, u32[]{:S(2)}) %copy-start) | copy-done | bytes 5898264
  134.6 16.3 %shard_map.122 = bf16[32,72,640]{2,1,0:T(8,128)(2,1)S(1)} custom-call(bf16[32,2,72,640]{3,2,1,0:T(8,128)(2,1)S(1)} %bitcast.6), custom_call_target="tpu_custom_call" | custom-call | flops 8847360 | bytes 8847360 | tf_op jit(solution)/shard_map/pallas_call | solution.py:313
  150.9 50.7 %shard_map.123.src_hbm = bf16[8,72,640]{2,1,0:T(8,128)(2,1)S(1)} custom-call(bf16[8,4,72,640]{3,2,1,0:T(8,128)(2,1)S(1)} %bitcast.5), custom_call_target="tpu_custom_call" | custom-call | flops 5898240 | bytes 5898240 | tf_op jit(solution)/shard_map/pallas_call | solution.py:475
  201.6 0.0 copy-start.3
  201.6 0.9 copy-done.3
  202.5 24.8 %shard_map.124.recv_ref = bf16[8,72,640]{2,1,0:T(8,128)(2,1)} custom-call(bf16[8,72,640]{2,1,0:T(8,128)(2,1)} %copy-done.3), custom_call_target="tpu_custom_call" | custom-call | bytes 2211840 | tf_op jit(solution)/shard_map/pallas_call | solution.py:530
  227.2 0.0 all-gather.6.cloned.1.call-done
  227.3 0.0 copy-start.1
  227.3 2.3 copy-done.1
  229.6 1.1 copy-done.2
  230.7 3.0 %shard_map.125.proj_hbm = bf16[72,4608]{1,0:T(8,128)(2,1)S(1)} custom-call(bf16[8,72,640]{2,1,0:T(8,128)(2,1)S(1)} %copy-done.2, bf16[1,4608,512]{2,1,0:T(8,128)(2,1)S(1)} %bitcast.7), custom_call_target="tpu_custom_call" | custom-call | flops 341213184 | bytes 6119424 | tf_op jit(solution)/shard_map/pallas_call | solution.py:225
  233.8 0.0 copy-start.4
  233.8 0.8 copy-done.4
  234.6 11.0 %shard_map.126 = f32[72,1152]{1,0:T(8,128)} custom-call(bf16[72,4608]{1,0:T(8,128)(2,1)} %copy-done.4), custom_call_target="tpu_custom_call" | custom-call | flops 331776 | bytes 995328 | tf_op jit(solution)/shard_map/pallas_call | solution.py:375
  245.6 1.5 reshape.161
  247.1 0.2 reshape.162
  247.3 0.0 copy-done.8
  247.3 1.9 reshape.163
  249.2 0.0 copy-done.7
  249.2 1.8 reshape.164
  251.0 0.0 copy-done.11
  251.0 0.7 add_convert_fusion
  (15 shorter events, 0.2 us)
Async XLA Ops:
  7.2 5.8 %copy-start.9 = (bf16[72,4,128]{2,1,0:T(4,128)(2,1)S(1)}, bf16[72,4,128]{2,1,0:T(4,128)(2,1)}, u32[]{:S(2)}) copy-start(bf16[72,4,128]{2,1,0:T(4,128)(2,1)} %param.12) | copy-start | bytes 221188
  7.2 103.0 %all-gather.4.cloned.1.call-start = ((), (), s32[]{:S(2)}) async-start(), calls=%async_computation | async-start | bytes 14376960 | tf_op jit(solution)/shard_map/all_gather | solution.py:587
  9.1 4.7 %copy-start.10 = (bf16[512,64]{0,1:T(8,128)(2,1)S(1)}, bf16[512,64]{0,1:T(8,128)(2,1)}, u32[]{:S(2)}) copy-start(bf16[512,64]{0,1:T(8,128)(2,1)} %param.18) | copy-start | bytes 196612
  10.1 4.4 %copy-start.12 = (s32[6,6]{1,0:T(8,128)S(1)}, s32[6,6]{1,0:T(8,128)}, u32[]{:S(2)}) copy-start(s32[6,6]{1,0:T(8,128)} %param.17) | copy-start | bytes 436
  10.1 4.5 %copy-start.13 = (s32[6,122]{1,0:T(8,128)S(1)}, s32[6,122]{1,0:T(8,128)}, u32[]{:S(2)}) copy-start(s32[6,122]{1,0:T(8,128)} %param.16) | copy-start | bytes 8788
  10.1 4.6 %copy-start.5 = (bf16[12,128,4,128]{3,2,1,0:T(4,128)(2,1)S(1)}, bf16[12,128,4,128]{3,2,1,0:T(4,128)(2,1)}, u32[]{:S(2)}) copy-start(bf16[12,128,4,128]{3,2,1,0:T(4,128)(2,1)} %param.13) | copy-start | bytes 4718596
  13.8 213.5 %all-gather.6.cloned.1.call-start = ((), (), s32[]{:S(2)}) async-start(), calls=%async_computation.1 | async-start | bytes 4792320 | tf_op jit(solution)/shard_map/all_gather | solution.py:586
  14.7 2.0 copy-start.6
  16.7 3.1 %copy-start.16 = (s32[6]{0:T(128)S(1)}, s32[6]{0:T(128)}, u32[]{:S(2)}) copy-start(s32[6]{0:T(128)} %param.15) | copy-start | bytes 76
  18.9 91.3 %copy-start.14 = (s32[12]{0:T(128)}, s32[12]{0:T(128)S(1)}, u32[]{:S(2)}) copy-start(s32[12]{0:T(128)S(1)} %fusion.1.sfresh_ref) | copy-start | bytes 148
  19.8 90.4 %copy-start.15 = (s32[12]{0:T(128)}, s32[12]{0:T(128)S(1)}, u32[]{:S(2)}) copy-start(s32[12]{0:T(128)S(1)} %get-tuple-element.17.sreq_ref) | copy-start | bytes 148
  131.9 2.7 %copy-start = (bf16[64,72,640]{2,1,0:T(8,128)(2,1)S(1)}, bf16[64,72,640]{2,1,0:T(8,128)(2,1)}, u32[]{:S(2)}) copy-start(bf16[64,72,640]{2,1,0:T(8,128)(2,1)} %get-tuple-element.6) | copy-start | bytes 17694724
  201.6 0.9 copy-start.3
  227.3 2.3 copy-start.1
  229.6 1.1 copy-start.2
  233.8 0.8 copy-start.4
  234.6 12.7 %copy-start.8 = (bf16[12,128,512]{2,1,0:T(8,128)(2,1)S(1)}, bf16[12,128,512]{2,1,0:T(8,128)(2,1)}, u32[]{:S(2)}) copy-start(bf16[12,128,512]{2,1,0:T(8,128)(2,1)} %get-tuple-element.7) | copy-start | bytes 4718596
  247.3 1.9 copy-start.7
  249.2 1.8 copy-start.11
Sparse Core Ops, SparseCore 0:
  13.9 96.2 all-gather.3
  113.5 96.0 all-gather.5

commit v14 on v13

--- a/solution.py
+++ b/solution.py
@@ -255,19 +255,25 @@
     pl.semaphore_signal(barrier, inc=1, device_id={"core": partner}, device_id_type=pl.DeviceIdType.MESH)
     pl.semaphore_wait(barrier, 1)
 
-    local = pltpu.make_async_copy(packed_hbm.at[:, core], mine, local_sem)
-    local.start()
-    remote = pltpu.make_async_remote_copy(
-        src_ref=packed_hbm.at[:, partner],
-        dst_ref=theirs,
-        send_sem=send_sem,
-        recv_sem=recv_sem,
-        device_id={"core": partner},
-        device_id_type=pl.DeviceIdType.MESH,
-    )
-    remote.start()
-    local.wait()
-    remote.wait()
+    pieces = 2
+    size = chunks // pieces
+    pending = []
+    for p in range(pieces):
+        rows = pl.ds(p * size, size)
+        local = pltpu.make_async_copy(
+            packed_hbm.at[rows, core], mine.at[rows], local_sem.at[p]
+        )
+        local.start()
+        remote = pltpu.make_async_remote_copy(
+            src_ref=packed_hbm.at[rows, partner],
+            dst_ref=theirs.at[rows],
+            send_sem=send_sem.at[p],
+            recv_sem=recv_sem.at[p],
+            device_id={"core": partner},
+            device_id_type=pl.DeviceIdType.MESH,
+        )
+        remote.start()
+        pending.append((local, remote))
 
     lane = lax.broadcasted_iota(jnp.int32, (rows_per, lanes), 1)
 
@@ -302,7 +308,11 @@
         out_ref[c, :, width:] = merged.astype(out_ref.dtype)
         return carry
 
-    lax.fori_loop(0, chunks, merge_step, 0)
+    for p in range(pieces):
+        local, remote = pending[p]
+        local.wait()
+        remote.wait()
+        lax.fori_loop(p * size, (p + 1) * size, merge_step, 0)
 
 
 def pair_merge(packed, heads, head_dim):
@@ -318,9 +328,9 @@
         scratch_shapes=[
             pltpu.VMEM((chips, rows_per, lanes_all), packed.dtype),
             pltpu.VMEM((chips, rows_per, lanes_all), packed.dtype),
-            pltpu.SemaphoreType.DMA(()),
-            pltpu.SemaphoreType.DMA(()),
-            pltpu.SemaphoreType.DMA(()),
+            pltpu.SemaphoreType.DMA((2,)),
+            pltpu.SemaphoreType.DMA((2,)),
+            pltpu.SemaphoreType.DMA((2,)),
         ],
         compiler_params=pltpu.CompilerParams(
             collective_id=0, has_side_effects=True, vmem_limit_bytes=40 * 1024 * 1024

time: 259 us -> 256 us (0.988)
  Pallas kernels: 128 us -> 124 us
    pallas_call x1, Pallas kernels: 21.7 us -> 18.8 us  [local_attention(): pl.pallas_call(kernel, out_shape=(jax.ShapeDtypeStruct((chunks, rows_per,...]
  transfers between devices with their start and end apart: 2 -> 2, of which waited for: 1 -> 1; matrix products, arithmetic and copies ran while one was open for 3% -> 3% of each run, Pallas kernels for 44% -> 43%
where the time goes in v14:
time: 256 us; the launch traced here: 255 us
  Pallas kernels  124 us (48%)
  waiting for transfers between devices  89.6 us (35%)
  local copies, waits for them, and re-layouts  20.2 us (8%)
  between operations  14.3 us (6%)
  other arithmetic  6.8 us (3%)
    all_gather x1, waiting for transfers between devices, per_device(): gathered = lax.all_gather(stacked, PAGES, axis=1, tiled=True)  89.6 us
    pallas_call x1, Pallas kernels, y_exchange(): pl.pallas_call(kernel, out_shape=jax.ShapeDtypeStruct((chunks, rows_per,...  52.5 us
    pallas_call x1, Pallas kernels, z_exchange(): pl.pallas_call(kernel, out_shape=jax.ShapeDtypeStruct(merged.shape, merge...  23.1 us
    pallas_call x1, Pallas kernels, local_attention(): pl.pallas_call(kernel, out_shape=(jax.ShapeDtypeStruct((chunks, rows_per,...  18.8 us
    pallas_call x1, Pallas kernels, pair_merge(): pl.pallas_call(kernel, out_shape=jax.ShapeDtypeStruct((chips, rows_per, l...  15.6 us
    pallas_call x1, Pallas kernels, heads_sum(): pl.pallas_call(kernel, out_shape=jax.ShapeDtypeStruct((rows, block), jnp....  11 us
    unnamed x34, local copies, waits for them, and re-layouts  7.87 us
  transfers between devices with their start and end apart: 2, of which 1 were waited for; matrix products, arithmetic and copies ran while one was open for 3% of the time, Pallas kernels for 43%

profile of v14, /device:TPU:4, one launch (start us, length us, event | category | flops | bytes accessed | tf_op | source)
XLA Modules:
  0.0 255.0 jit_solution(558443633968478826)
XLA Ops:
  7.2 0.0 copy-start.9
  7.2 0.0 all-gather.4.cloned.1.call-start
  7.2 0.9 convert_element_type.40
  8.1 1.0 slice.25
  9.1 0.0 copy-start.10
  9.2 0.9 convert_element_type.43
  10.1 0.0 copy-start.12
  10.1 0.0 copy-start.13
  10.1 0.0 copy-start.5
  10.1 1.1 slice.28
  11.3 0.7 select_reduce_fusion
  12.0 0.2 multiply_cosine_fusion
  12.2 0.3 subtract_convert_fusion.1
  12.6 0.3 pad_maximum_fusion.1
  13.0 0.0 copy-done.9
  13.0 0.7 pad_maximum_fusion
  13.7 0.0 all-gather.4.cloned.1.call-update
  13.8 0.0 all-gather.6.cloned.1.call-start
  13.8 0.0 copy-done.10
  13.8 0.6 pad.4
  14.5 0.0 all-gather.6.cloned.1.call-update
  14.5 0.0 copy-done.12
  14.5 0.1 eq.61
  14.6 0.0 copy-done.13
  14.6 0.1 eq.65
  14.7 0.0 copy-done.5
  14.7 0.0 copy-start.6
  14.7 2.0 reshape.157.kc_ref
  16.7 0.0 copy-done.6
  16.7 2.0 reshape.158.vc_ref
  18.7 0.2 fusion.1.sfresh_ref
  18.9 0.2 compare_reduce_fusion.1
  19.0 0.2 fusion
  19.2 0.5 broadcast_select_fusion
  19.8 0.0 copy-done.16
  19.8 0.1 select_reduce_fusion.1
  19.9 0.2 compare_reduce_fusion
  20.1 0.6 fusion.5.skind_ref
  20.6 89.6 %all-gather.4.cloned.1.call-done.q_ref.kf_ref.vf_ref = bf16[3,4608,512]{2,1,0:T(8,128)(2,1)} async-done(((bf16[3,72,512]{2,1,0:T(8,128)(2,1)}), bf16[3,4608,512]{2,1,0:T(8,128)(2,1)}) %all-gather.4.cloned.1.call-update) | async-done | bytes 14155792 | tf_op jit(solution)/shard_map/all_gather | solution.py:597
  110.2 0.0 copy-done.14
  110.2 0.0 copy-done.15
  110.2 18.8 %shard_map.121 = (bf16[64,72,640]{2,1,0:T(8,128)(2,1)}, bf16[12,128,512]{2,1,0:T(8,128)(2,1)}, bf16[12,128,512]{2,1,0:T(8,128)(2,1)}) custom-call(s32[12]{0:T(128)} %copy-done.15, s32[12]{0:T(128)} %fusion.5.skind_ref, s32[12]{0:T(128)} %get-tuple-element.9.slim_ref, s32[12]{0:T(128)} %copy-done.14, ...), custom_call_target="tpu_custom_call" | custom-call | flops 2415919104 | bytes 16908288 | tf_op jit(solution)/shard_map/pallas_call | solution.py:144
  129.0 2.7 %copy-done = bf16[64,72,640]{2,1,0:T(8,128)(2,1)S(1)} copy-done((bf16[64,72,640]{2,1,0:T(8,128)(2,1)S(1)}, bf16[64,72,640]{2,1,0:T(8,128)(2,1)}, u32[]{:S(2)}) %copy-start) | copy-done | bytes 5898264
  131.6 15.6 %shard_map.122 = bf16[32,72,640]{2,1,0:T(8,128)(2,1)S(1)} custom-call(bf16[32,2,72,640]{3,2,1,0:T(8,128)(2,1)S(1)} %bitcast.6), custom_call_target="tpu_custom_call" | custom-call | flops 8847360 | bytes 8847360 | tf_op jit(solution)/shard_map/pallas_call | solution.py:323
  147.3 52.5 %shard_map.123.src_hbm = bf16[8,72,640]{2,1,0:T(8,128)(2,1)S(1)} custom-call(bf16[8,4,72,640]{3,2,1,0:T(8,128)(2,1)S(1)} %bitcast.5), custom_call_target="tpu_custom_call" | custom-call | flops 5898240 | bytes 5898240 | tf_op jit(solution)/shard_map/pallas_call | solution.py:485
  199.7 0.0 copy-start.3
  199.7 0.9 copy-done.3
  200.6 23.1 %shard_map.124.recv_ref = bf16[8,72,640]{2,1,0:T(8,128)(2,1)} custom-call(bf16[8,72,640]{2,1,0:T(8,128)(2,1)} %copy-done.3), custom_call_target="tpu_custom_call" | custom-call | bytes 2211840 | tf_op jit(solution)/shard_map/pallas_call | solution.py:540
  223.7 0.0 all-gather.6.cloned.1.call-done
  223.7 0.0 copy-start.1
  223.8 2.3 copy-done.1
  226.1 1.1 copy-done.2
  227.2 3.0 %shard_map.125.proj_hbm = bf16[72,4608]{1,0:T(8,128)(2,1)S(1)} custom-call(bf16[8,72,640]{2,1,0:T(8,128)(2,1)S(1)} %copy-done.2, bf16[1,4608,512]{2,1,0:T(8,128)(2,1)S(1)} %bitcast.7), custom_call_target="tpu_custom_call" | custom-call | flops 341213184 | bytes 6119424 | tf_op jit(solution)/shard_map/pallas_call | solution.py:225
  230.2 0.0 copy-start.4
  230.2 0.8 copy-done.4
  231.1 11.0 %shard_map.126 = f32[72,1152]{1,0:T(8,128)} custom-call(bf16[72,4608]{1,0:T(8,128)(2,1)} %copy-done.4), custom_call_target="tpu_custom_call" | custom-call | flops 331776 | bytes 995328 | tf_op jit(solution)/shard_map/pallas_call | solution.py:385
  242.1 1.5 reshape.161
  243.6 0.2 reshape.162
  243.8 0.0 copy-done.8
  243.8 1.9 reshape.163
  245.7 0.0 copy-done.7
  245.7 1.8 reshape.164
  247.5 0.0 copy-done.11
  247.5 0.7 add_convert_fusion
  (15 shorter events, 0.2 us)
Async XLA Ops:
  7.2 5.8 %copy-start.9 = (bf16[72,4,128]{2,1,0:T(4,128)(2,1)S(1)}, bf16[72,4,128]{2,1,0:T(4,128)(2,1)}, u32[]{:S(2)}) copy-start(bf16[72,4,128]{2,1,0:T(4,128)(2,1)} %param.12) | copy-start | bytes 221188
  7.2 103.0 %all-gather.4.cloned.1.call-start = ((), (), s32[]{:S(2)}) async-start(), calls=%async_computation | async-start | bytes 14376960 | tf_op jit(solution)/shard_map/all_gather | solution.py:597
  9.1 4.7 %copy-start.10 = (bf16[512,64]{0,1:T(8,128)(2,1)S(1)}, bf16[512,64]{0,1:T(8,128)(2,1)}, u32[]{:S(2)}) copy-start(bf16[512,64]{0,1:T(8,128)(2,1)} %param.18) | copy-start | bytes 196612
  10.1 4.4 %copy-start.12 = (s32[6,6]{1,0:T(8,128)S(1)}, s32[6,6]{1,0:T(8,128)}, u32[]{:S(2)}) copy-start(s32[6,6]{1,0:T(8,128)} %param.17) | copy-start | bytes 436
  10.1 4.5 %copy-start.13 = (s32[6,122]{1,0:T(8,128)S(1)}, s32[6,122]{1,0:T(8,128)}, u32[]{:S(2)}) copy-start(s32[6,122]{1,0:T(8,128)} %param.16) | copy-start | bytes 8788
  10.1 4.6 %copy-start.5 = (bf16[12,128,4,128]{3,2,1,0:T(4,128)(2,1)S(1)}, bf16[12,128,4,128]{3,2,1,0:T(4,128)(2,1)}, u32[]{:S(2)}) copy-start(bf16[12,128,4,128]{3,2,1,0:T(4,128)(2,1)} %param.13) | copy-start | bytes 4718596
  13.8 210.0 %all-gather.6.cloned.1.call-start = ((), (), s32[]{:S(2)}) async-start(), calls=%async_computation.1 | async-start | bytes 4792320 | tf_op jit(solution)/shard_map/all_gather | solution.py:596
  14.7 2.0 copy-start.6
  16.7 3.1 %copy-start.16 = (s32[6]{0:T(128)S(1)}, s32[6]{0:T(128)}, u32[]{:S(2)}) copy-start(s32[6]{0:T(128)} %param.15) | copy-start | bytes 76
  18.9 91.3 %copy-start.14 = (s32[12]{0:T(128)}, s32[12]{0:T(128)S(1)}, u32[]{:S(2)}) copy-start(s32[12]{0:T(128)S(1)} %fusion.1.sfresh_ref) | copy-start | bytes 148
  19.8 90.4 %copy-start.15 = (s32[12]{0:T(128)}, s32[12]{0:T(128)S(1)}, u32[]{:S(2)}) copy-start(s32[12]{0:T(128)S(1)} %get-tuple-element.17.sreq_ref) | copy-start | bytes 148
  129.0 2.7 %copy-start = (bf16[64,72,640]{2,1,0:T(8,128)(2,1)S(1)}, bf16[64,72,640]{2,1,0:T(8,128)(2,1)}, u32[]{:S(2)}) copy-start(bf16[64,72,640]{2,1,0:T(8,128)(2,1)} %get-tuple-element.6) | copy-start | bytes 17694724
  199.7 0.9 copy-start.3
  223.7 2.3 copy-start.1
  226.1 1.1 copy-start.2
  230.2 0.8 copy-start.4
  231.1 12.7 %copy-start.8 = (bf16[12,128,512]{2,1,0:T(8,128)(2,1)S(1)}, bf16[12,128,512]{2,1,0:T(8,128)(2,1)}, u32[]{:S(2)}) copy-start(bf16[12,128,512]{2,1,0:T(8,128)(2,1)} %get-tuple-element.7) | copy-start | bytes 4718596
  243.8 1.9 copy-start.7
  245.7 1.8 copy-start.11
Sparse Core Ops, SparseCore 0:
  13.9 96.2 all-gather.3
  113.5 93.8 all-gather.5

commit v15 on v14

--- a/solution.py
+++ b/solution.py
@@ -450,24 +450,27 @@
             device_id_type=pl.DeviceIdType.MESH,
         )
     pl.semaphore_wait(barrier, groups - 1)
-    local = pltpu.make_async_copy(src_hbm.at[:, me], parts.at[0], own_sem)
-    local.start()
-    copies = []
-    for k in range(1, groups):
-        dest = lax.rem(me + k, groups)
-        copy = pltpu.make_async_remote_copy(
-            src_ref=src_hbm.at[:, dest],
-            dst_ref=parts.at[k],
-            send_sem=send_sems.at[k - 1],
-            recv_sem=recv_sems.at[k - 1],
-            device_id={"y": dest},
-            device_id_type=pl.DeviceIdType.MESH,
-        )
-        copy.start()
-        copies.append(copy)
-    local.wait()
-    for copy in copies:
-        copy.wait()
+    pieces = 2
+    size = chunks // pieces
+    pending = []
+    for p in range(pieces):
+        rows = pl.ds(p * size, size)
+        local = pltpu.make_async_copy(src_hbm.at[rows, me], parts.at[0, rows], own_sem.at[p])
+        local.start()
+        copies = [local]
+        for k in range(1, groups):
+            dest = lax.rem(me + k, groups)
+            copy = pltpu.make_async_remote_copy(
+                src_ref=src_hbm.at[rows, dest],
+                dst_ref=parts.at[k, rows],
+                send_sem=send_sems.at[p, k - 1],
+                recv_sem=recv_sems.at[p, k - 1],
+                device_id={"y": dest},
+                device_id_type=pl.DeviceIdType.MESH,
+            )
+            copy.start()
+            copies.append(copy)
+        pending.append(copies)
 
     def get_part(j, c, cut):
         return parts[j, c, :, cut]
@@ -476,7 +479,10 @@
         merge_chunk(heads, head_dim, groups, get_part, out_ref, c)
         return carry
 
-    lax.fori_loop(0, chunks, step, 0)
+    for p in range(pieces):
+        for copy in pending[p]:
+            copy.wait()
+        lax.fori_loop(p * size, (p + 1) * size, step, 0)
 
 
 def y_exchange(by_y, heads, head_dim):
@@ -489,9 +495,9 @@
         out_specs=pl.BlockSpec(memory_space=pltpu.VMEM),
         scratch_shapes=[
             pltpu.VMEM((groups, chunks, rows_per, lanes_all), by_y.dtype),
-            pltpu.SemaphoreType.DMA(()),
-            pltpu.SemaphoreType.DMA((groups - 1,)),
-            pltpu.SemaphoreType.DMA((groups - 1,)),
+            pltpu.SemaphoreType.DMA((2,)),
+            pltpu.SemaphoreType.DMA((2, groups - 1)),
+            pltpu.SemaphoreType.DMA((2, groups - 1)),
         ],
         compiler_params=pltpu.CompilerParams(
             collective_id=2, has_side_effects=True, vmem_limit_bytes=32 * 1024 * 1024

time: 256 us -> 253 us (0.988)
  Pallas kernels: 124 us -> 121 us
    pallas_call x1, Pallas kernels: 52.5 us -> 48.2 us  [y_exchange(): pl.pallas_call(kernel, out_shape=jax.ShapeDtypeStruct((chunks, rows_per,...]
    pallas_call x1, Pallas kernels: 18.8 us -> 21.8 us  [local_attention(): pl.pallas_call(kernel, out_shape=(jax.ShapeDtypeStruct((chunks, rows_per,...]
where the time goes in v15:
time: 253 us; the launch traced here: 252 us
  Pallas kernels  121 us (48%)
  waiting for transfers between devices  89.6 us (35%)
  local copies, waits for them, and re-layouts  20.2 us (8%)
  between operations  14.3 us (6%)
  other arithmetic  6.8 us (3%)
    all_gather x1, waiting for transfers between devices, per_device(): gathered = lax.all_gather(stacked, PAGES, axis=1, tiled=True)  89.6 us
    pallas_call x1, Pallas kernels, y_exchange(): pl.pallas_call(kernel, out_shape=jax.ShapeDtypeStruct((chunks, rows_per,...  48.2 us
    pallas_call x1, Pallas kernels, z_exchange(): pl.pallas_call(kernel, out_shape=jax.ShapeDtypeStruct(merged.shape, merge...  24.1 us
    pallas_call x1, Pallas kernels, local_attention(): pl.pallas_call(kernel, out_shape=(jax.ShapeDtypeStruct((chunks, rows_per,...  21.8 us
    pallas_call x1, Pallas kernels, pair_merge(): pl.pallas_call(kernel, out_shape=jax.ShapeDtypeStruct((chips, rows_per, l...  14.4 us
    pallas_call x1, Pallas kernels, heads_sum(): pl.pallas_call(kernel, out_shape=jax.ShapeDtypeStruct((rows, block), jnp....  9.7 us
    unnamed x34, local copies, waits for them, and re-layouts  7.88 us
  transfers between devices with their start and end apart: 2, of which 1 were waited for; matrix products, arithmetic and copies ran while one was open for 3% of the time, Pallas kernels for 43%

profile of v15, /device:TPU:4, one launch (start us, length us, event | category | flops | bytes accessed | tf_op | source)
XLA Modules:
  0.0 252.2 jit_solution(9737182728982836227)
XLA Ops:
  7.2 0.0 copy-start.9
  7.2 0.0 all-gather.4.cloned.1.call-start
  7.2 0.9 convert_element_type.40
  8.1 1.0 slice.25
  9.1 0.0 copy-start.10
  9.2 0.9 convert_element_type.43
  10.1 0.0 copy-start.12
  10.1 0.0 copy-start.13
  10.1 0.0 copy-start.5
  10.1 1.1 slice.28
  11.3 0.7 select_reduce_fusion
  12.0 0.2 multiply_cosine_fusion
  12.2 0.3 subtract_convert_fusion.1
  12.6 0.3 pad_maximum_fusion.1
  13.0 0.0 copy-done.9
  13.0 0.7 pad_maximum_fusion
  13.7 0.0 all-gather.4.cloned.1.call-update
  13.8 0.0 all-gather.6.cloned.1.call-start
  13.8 0.0 copy-done.10
  13.8 0.6 pad.4
  14.5 0.0 all-gather.6.cloned.1.call-update
  14.5 0.0 copy-done.12
  14.5 0.1 eq.61
  14.6 0.0 copy-done.13
  14.6 0.1 eq.65
  14.7 0.0 copy-done.5
  14.7 0.0 copy-start.6
  14.7 2.0 reshape.157.kc_ref
  16.7 0.0 copy-done.6
  16.7 2.0 reshape.158.vc_ref
  18.7 0.2 fusion.1.sfresh_ref
  18.9 0.2 compare_reduce_fusion.1
  19.0 0.2 fusion
  19.2 0.5 broadcast_select_fusion
  19.8 0.0 copy-done.16
  19.8 0.1 select_reduce_fusion.1
  19.9 0.2 compare_reduce_fusion
  20.1 0.6 fusion.5.skind_ref
  20.6 89.6 %all-gather.4.cloned.1.call-done.q_ref.kf_ref.vf_ref = bf16[3,4608,512]{2,1,0:T(8,128)(2,1)} async-done(((bf16[3,72,512]{2,1,0:T(8,128)(2,1)}), bf16[3,4608,512]{2,1,0:T(8,128)(2,1)}) %all-gather.4.cloned.1.call-update) | async-done | bytes 14155792 | tf_op jit(solution)/shard_map/all_gather | solution.py:603
  110.2 0.0 copy-done.14
  110.2 0.0 copy-done.15
  110.2 21.8 %shard_map.121 = (bf16[64,72,640]{2,1,0:T(8,128)(2,1)}, bf16[12,128,512]{2,1,0:T(8,128)(2,1)}, bf16[12,128,512]{2,1,0:T(8,128)(2,1)}) custom-call(s32[12]{0:T(128)} %copy-done.15, s32[12]{0:T(128)} %fusion.5.skind_ref, s32[12]{0:T(128)} %get-tuple-element.9.slim_ref, s32[12]{0:T(128)} %copy-done.14, ...), custom_call_target="tpu_custom_call" | custom-call | flops 2415919104 | bytes 16908288 | tf_op jit(solution)/shard_map/pallas_call | solution.py:144
  132.0 2.7 %copy-done = bf16[64,72,640]{2,1,0:T(8,128)(2,1)S(1)} copy-done((bf16[64,72,640]{2,1,0:T(8,128)(2,1)S(1)}, bf16[64,72,640]{2,1,0:T(8,128)(2,1)}, u32[]{:S(2)}) %copy-start) | copy-done | bytes 5898264
  134.7 14.4 %shard_map.122 = bf16[32,72,640]{2,1,0:T(8,128)(2,1)S(1)} custom-call(bf16[32,2,72,640]{3,2,1,0:T(8,128)(2,1)S(1)} %bitcast.6), custom_call_target="tpu_custom_call" | custom-call | flops 8847360 | bytes 8847360 | tf_op jit(solution)/shard_map/pallas_call | solution.py:323
  149.1 48.2 %shard_map.123.src_hbm = bf16[8,72,640]{2,1,0:T(8,128)(2,1)S(1)} custom-call(bf16[8,4,72,640]{3,2,1,0:T(8,128)(2,1)S(1)} %bitcast.5), custom_call_target="tpu_custom_call" | custom-call | flops 5898240 | bytes 5898240 | tf_op jit(solution)/shard_map/pallas_call | solution.py:491
  197.3 0.0 copy-start.3
  197.3 0.9 copy-done.3
  198.2 24.1 %shard_map.124.recv_ref = bf16[8,72,640]{2,1,0:T(8,128)(2,1)} custom-call(bf16[8,72,640]{2,1,0:T(8,128)(2,1)} %copy-done.3), custom_call_target="tpu_custom_call" | custom-call | bytes 2211840 | tf_op jit(solution)/shard_map/pallas_call | solution.py:546
  222.3 0.0 all-gather.6.cloned.1.call-done
  222.3 0.0 copy-start.1
  222.3 2.3 copy-done.1
  224.6 1.1 copy-done.2
  225.7 3.0 %shard_map.125.proj_hbm = bf16[72,4608]{1,0:T(8,128)(2,1)S(1)} custom-call(bf16[8,72,640]{2,1,0:T(8,128)(2,1)S(1)} %copy-done.2, bf16[1,4608,512]{2,1,0:T(8,128)(2,1)S(1)} %bitcast.7), custom_call_target="tpu_custom_call" | custom-call | flops 341213184 | bytes 6119424 | tf_op jit(solution)/shard_map/pallas_call | solution.py:225
  228.8 0.0 copy-start.4
  228.8 0.8 copy-done.4
  229.6 9.7 %shard_map.126 = f32[72,1152]{1,0:T(8,128)} custom-call(bf16[72,4608]{1,0:T(8,128)(2,1)} %copy-done.4), custom_call_target="tpu_custom_call" | custom-call | flops 331776 | bytes 995328 | tf_op jit(solution)/shard_map/pallas_call | solution.py:385
  239.3 1.5 reshape.161
  240.8 0.2 reshape.162
  241.0 0.0 copy-done.8
  241.0 0.0 copy-start.7
  241.0 1.9 reshape.163
  242.9 0.0 copy-done.7
  242.9 1.8 reshape.164
  244.7 0.7 add_convert_fusion
  (15 shorter events, 0.2 us)
Async XLA Ops:
  7.2 5.8 %copy-start.9 = (bf16[72,4,128]{2,1,0:T(4,128)(2,1)S(1)}, bf16[72,4,128]{2,1,0:T(4,128)(2,1)}, u32[]{:S(2)}) copy-start(bf16[72,4,128]{2,1,0:T(4,128)(2,1)} %param.12) | copy-start | bytes 221188
  7.2 103.0 %all-gather.4.cloned.1.call-start = ((), (), s32[]{:S(2)}) async-start(), calls=%async_computation | async-start | bytes 14376960 | tf_op jit(solution)/shard_map/all_gather | solution.py:603
  9.1 4.7 %copy-start.10 = (bf16[512,64]{0,1:T(8,128)(2,1)S(1)}, bf16[512,64]{0,1:T(8,128)(2,1)}, u32[]{:S(2)}) copy-start(bf16[512,64]{0,1:T(8,128)(2,1)} %param.18) | copy-start | bytes 196612
  10.1 4.4 %copy-start.12 = (s32[6,6]{1,0:T(8,128)S(1)}, s32[6,6]{1,0:T(8,128)}, u32[]{:S(2)}) copy-start(s32[6,6]{1,0:T(8,128)} %param.17) | copy-start | bytes 436
  10.1 4.5 %copy-start.13 = (s32[6,122]{1,0:T(8,128)S(1)}, s32[6,122]{1,0:T(8,128)}, u32[]{:S(2)}) copy-start(s32[6,122]{1,0:T(8,128)} %param.16) | copy-start | bytes 8788
  10.1 4.6 %copy-start.5 = (bf16[12,128,4,128]{3,2,1,0:T(4,128)(2,1)S(1)}, bf16[12,128,4,128]{3,2,1,0:T(4,128)(2,1)}, u32[]{:S(2)}) copy-start(bf16[12,128,4,128]{3,2,1,0:T(4,128)(2,1)} %param.13) | copy-start | bytes 4718596
  13.8 208.5 %all-gather.6.cloned.1.call-start = ((), (), s32[]{:S(2)}) async-start(), calls=%async_computation.1 | async-start | bytes 4792320 | tf_op jit(solution)/shard_map/all_gather | solution.py:602
  14.7 2.0 copy-start.6
  16.7 3.1 %copy-start.16 = (s32[6]{0:T(128)S(1)}, s32[6]{0:T(128)}, u32[]{:S(2)}) copy-start(s32[6]{0:T(128)} %param.15) | copy-start | bytes 76
  18.9 91.3 %copy-start.14 = (s32[12]{0:T(128)}, s32[12]{0:T(128)S(1)}, u32[]{:S(2)}) copy-start(s32[12]{0:T(128)S(1)} %fusion.1.sfresh_ref) | copy-start | bytes 148
  19.8 90.4 %copy-start.15 = (s32[12]{0:T(128)}, s32[12]{0:T(128)S(1)}, u32[]{:S(2)}) copy-start(s32[12]{0:T(128)S(1)} %get-tuple-element.17.sreq_ref) | copy-start | bytes 148
  132.0 2.7 %copy-start = (bf16[64,72,640]{2,1,0:T(8,128)(2,1)S(1)}, bf16[64,72,640]{2,1,0:T(8,128)(2,1)}, u32[]{:S(2)}) copy-start(bf16[64,72,640]{2,1,0:T(8,128)(2,1)} %get-tuple-element.6) | copy-start | bytes 17694724
  197.3 0.9 copy-start.3
  222.3 2.3 copy-start.1
  224.6 1.1 copy-start.2
  228.8 0.8 copy-start.4
  229.6 11.4 %copy-start.8 = (bf16[12,128,512]{2,1,0:T(8,128)(2,1)S(1)}, bf16[12,128,512]{2,1,0:T(8,128)(2,1)}, u32[]{:S(2)}) copy-start(bf16[12,128,512]{2,1,0:T(8,128)(2,1)} %get-tuple-element.7) | copy-start | bytes 4718596
  241.0 1.9 copy-start.7
  242.9 1.8 copy-start.11
Sparse Core Ops, SparseCore 0:
  13.9 96.2 all-gather.3
  113.5 89.3 all-gather.5

commit v16 on v15

--- a/solution.py
+++ b/solution.py
@@ -255,7 +255,7 @@
     pl.semaphore_signal(barrier, inc=1, device_id={"core": partner}, device_id_type=pl.DeviceIdType.MESH)
     pl.semaphore_wait(barrier, 1)
 
-    pieces = 2
+    pieces = 4
     size = chunks // pieces
     pending = []
     for p in range(pieces):
@@ -328,9 +328,9 @@
         scratch_shapes=[
             pltpu.VMEM((chips, rows_per, lanes_all), packed.dtype),
             pltpu.VMEM((chips, rows_per, lanes_all), packed.dtype),
-            pltpu.SemaphoreType.DMA((2,)),
-            pltpu.SemaphoreType.DMA((2,)),
-            pltpu.SemaphoreType.DMA((2,)),
+            pltpu.SemaphoreType.DMA((4,)),
+            pltpu.SemaphoreType.DMA((4,)),
+            pltpu.SemaphoreType.DMA((4,)),
         ],
         compiler_params=pltpu.CompilerParams(
             collective_id=0, has_side_effects=True, vmem_limit_bytes=40 * 1024 * 1024
@@ -450,7 +450,7 @@
             device_id_type=pl.DeviceIdType.MESH,
         )
     pl.semaphore_wait(barrier, groups - 1)
-    pieces = 2
+    pieces = 4
     size = chunks // pieces
     pending = []
     for p in range(pieces):
@@ -495,9 +495,9 @@
         out_specs=pl.BlockSpec(memory_space=pltpu.VMEM),
         scratch_shapes=[
             pltpu.VMEM((groups, chunks, rows_per, lanes_all), by_y.dtype),
-            pltpu.SemaphoreType.DMA((2,)),
-            pltpu.SemaphoreType.DMA((2, groups - 1)),
-            pltpu.SemaphoreType.DMA((2, groups - 1)),
+            pltpu.SemaphoreType.DMA((4,)),
+            pltpu.SemaphoreType.DMA((4, groups - 1)),
+            pltpu.SemaphoreType.DMA((4, groups - 1)),
         ],
         compiler_params=pltpu.CompilerParams(
             collective_id=2, has_side_effects=True, vmem_limit_bytes=32 * 1024 * 1024

time: 253 us -> 251 us (level)
    pallas_call x1, Pallas kernels: 21.8 us -> 18.8 us  [local_attention(): pl.pallas_call(kernel, out_shape=(jax.ShapeDtypeStruct((chunks, rows_per,...]
  transfers between devices with their start and end apart: 2 -> 2, of which waited for: 1 -> 1; matrix products, arithmetic and copies ran while one was open for 3% -> 3% of each run, Pallas kernels for 43% -> 42%
where the time goes in v16:
time: 251 us; the launch traced here: 250 us
  Pallas kernels  119 us (47%)
  waiting for transfers between devices  89.6 us (36%)
  local copies, waits for them, and re-layouts  20.2 us (8%)
  between operations  14.3 us (6%)
  other arithmetic  6.8 us (3%)
    all_gather x1, waiting for transfers between devices, per_device(): gathered = lax.all_gather(stacked, PAGES, axis=1, tiled=True)  89.6 us
    pallas_call x1, Pallas kernels, y_exchange(): pl.pallas_call(kernel, out_shape=jax.ShapeDtypeStruct((chunks, rows_per,...  47.3 us
    pallas_call x1, Pallas kernels, z_exchange(): pl.pallas_call(kernel, out_shape=jax.ShapeDtypeStruct(merged.shape, merge...  22.1 us
    pallas_call x1, Pallas kernels, local_attention(): pl.pallas_call(kernel, out_shape=(jax.ShapeDtypeStruct((chunks, rows_per,...  18.8 us
    pallas_call x1, Pallas kernels, pair_merge(): pl.pallas_call(kernel, out_shape=jax.ShapeDtypeStruct((chips, rows_per, l...  16.7 us
    pallas_call x1, Pallas kernels, heads_sum(): pl.pallas_call(kernel, out_shape=jax.ShapeDtypeStruct((rows, block), jnp....  11.2 us
    unnamed x34, local copies, waits for them, and re-layouts  7.87 us
  transfers between devices with their start and end apart: 2, of which 1 were waited for; matrix products, arithmetic and copies ran while one was open for 3% of the time, Pallas kernels for 42%

profile of v16, /device:TPU:4, one launch (start us, length us, event | category | flops | bytes accessed | tf_op | source)
XLA Modules:
  0.0 250.2 jit_solution(3327180210588674854)
XLA Ops:
  7.2 0.0 copy-start.9
  7.2 0.0 all-gather.4.cloned.1.call-start
  7.2 0.9 convert_element_type.40
  8.1 1.0 slice.25
  9.1 0.0 copy-start.10
  9.2 0.9 convert_element_type.43
  10.1 0.0 copy-start.12
  10.1 0.0 copy-start.13
  10.1 0.0 copy-start.5
  10.1 1.1 slice.28
  11.3 0.7 select_reduce_fusion
  12.0 0.2 multiply_cosine_fusion
  12.2 0.3 subtract_convert_fusion.1
  12.6 0.3 pad_maximum_fusion.1
  13.0 0.0 copy-done.9
  13.0 0.7 pad_maximum_fusion
  13.7 0.0 all-gather.4.cloned.1.call-update
  13.8 0.0 all-gather.6.cloned.1.call-start
  13.8 0.0 copy-done.10
  13.8 0.6 pad.4
  14.5 0.0 all-gather.6.cloned.1.call-update
  14.5 0.0 copy-done.12
  14.5 0.1 eq.61
  14.6 0.0 copy-done.13
  14.6 0.1 eq.65
  14.7 0.0 copy-done.5
  14.7 0.0 copy-start.6
  14.7 2.0 reshape.157.kc_ref
  16.7 0.0 copy-done.6
  16.7 2.0 reshape.158.vc_ref
  18.7 0.2 fusion.1.sfresh_ref
  18.9 0.2 compare_reduce_fusion.1
  19.0 0.2 fusion
  19.2 0.5 broadcast_select_fusion
  19.8 0.0 copy-done.16
  19.8 0.1 select_reduce_fusion.1
  19.9 0.2 compare_reduce_fusion
  20.1 0.6 fusion.5.skind_ref
  20.6 89.6 %all-gather.4.cloned.1.call-done.q_ref.kf_ref.vf_ref = bf16[3,4608,512]{2,1,0:T(8,128)(2,1)} async-done(((bf16[3,72,512]{2,1,0:T(8,128)(2,1)}), bf16[3,4608,512]{2,1,0:T(8,128)(2,1)}) %all-gather.4.cloned.1.call-update) | async-done | bytes 14155792 | tf_op jit(solution)/shard_map/all_gather | solution.py:603
  110.2 0.0 copy-done.14
  110.2 0.0 copy-done.15
  110.2 18.8 %shard_map.121 = (bf16[64,72,640]{2,1,0:T(8,128)(2,1)}, bf16[12,128,512]{2,1,0:T(8,128)(2,1)}, bf16[12,128,512]{2,1,0:T(8,128)(2,1)}) custom-call(s32[12]{0:T(128)} %copy-done.15, s32[12]{0:T(128)} %fusion.5.skind_ref, s32[12]{0:T(128)} %get-tuple-element.9.slim_ref, s32[12]{0:T(128)} %copy-done.14, ...), custom_call_target="tpu_custom_call" | custom-call | flops 2415919104 | bytes 16908288 | tf_op jit(solution)/shard_map/pallas_call | solution.py:144
  128.9 2.7 %copy-done = bf16[64,72,640]{2,1,0:T(8,128)(2,1)S(1)} copy-done((bf16[64,72,640]{2,1,0:T(8,128)(2,1)S(1)}, bf16[64,72,640]{2,1,0:T(8,128)(2,1)}, u32[]{:S(2)}) %copy-start) | copy-done | bytes 5898264
  131.6 16.7 %shard_map.122 = bf16[32,72,640]{2,1,0:T(8,128)(2,1)S(1)} custom-call(bf16[32,2,72,640]{3,2,1,0:T(8,128)(2,1)S(1)} %bitcast.6), custom_call_target="tpu_custom_call" | custom-call | flops 8847360 | bytes 8847360 | tf_op jit(solution)/shard_map/pallas_call | solution.py:323
  148.3 47.3 %shard_map.123.src_hbm = bf16[8,72,640]{2,1,0:T(8,128)(2,1)S(1)} custom-call(bf16[8,4,72,640]{3,2,1,0:T(8,128)(2,1)S(1)} %bitcast.5), custom_call_target="tpu_custom_call" | custom-call | flops 5898240 | bytes 5898240 | tf_op jit(solution)/shard_map/pallas_call | solution.py:491
  195.7 0.0 copy-start.3
  195.7 0.9 copy-done.3
  196.5 22.1 %shard_map.124.recv_ref = bf16[8,72,640]{2,1,0:T(8,128)(2,1)} custom-call(bf16[8,72,640]{2,1,0:T(8,128)(2,1)} %copy-done.3), custom_call_target="tpu_custom_call" | custom-call | bytes 2211840 | tf_op jit(solution)/shard_map/pallas_call | solution.py:546
  218.7 0.0 all-gather.6.cloned.1.call-done
  218.7 0.0 copy-start.1
  218.7 2.3 copy-done.1
  221.0 1.1 copy-done.2
  222.2 3.0 %shard_map.125.proj_hbm = bf16[72,4608]{1,0:T(8,128)(2,1)S(1)} custom-call(bf16[8,72,640]{2,1,0:T(8,128)(2,1)S(1)} %copy-done.2, bf16[1,4608,512]{2,1,0:T(8,128)(2,1)S(1)} %bitcast.7), custom_call_target="tpu_custom_call" | custom-call | flops 341213184 | bytes 6119424 | tf_op jit(solution)/shard_map/pallas_call | solution.py:225
  225.2 0.0 copy-start.4
  225.2 0.8 copy-done.4
  226.0 11.2 %shard_map.126 = f32[72,1152]{1,0:T(8,128)} custom-call(bf16[72,4608]{1,0:T(8,128)(2,1)} %copy-done.4), custom_call_target="tpu_custom_call" | custom-call | flops 331776 | bytes 995328 | tf_op jit(solution)/shard_map/pallas_call | solution.py:385
  237.3 1.5 reshape.161
  238.7 0.2 reshape.162
  238.9 0.0 copy-done.8
  238.9 0.0 copy-start.7
  238.9 1.9 reshape.163
  240.8 0.0 copy-done.7
  240.8 1.8 reshape.164
  242.6 0.7 add_convert_fusion
  (15 shorter events, 0.2 us)
Async XLA Ops:
  7.2 5.8 %copy-start.9 = (bf16[72,4,128]{2,1,0:T(4,128)(2,1)S(1)}, bf16[72,4,128]{2,1,0:T(4,128)(2,1)}, u32[]{:S(2)}) copy-start(bf16[72,4,128]{2,1,0:T(4,128)(2,1)} %param.12) | copy-start | bytes 221188
  7.2 103.0 %all-gather.4.cloned.1.call-start = ((), (), s32[]{:S(2)}) async-start(), calls=%async_computation | async-start | bytes 14376960 | tf_op jit(solution)/shard_map/all_gather | solution.py:603
  9.1 4.7 %copy-start.10 = (bf16[512,64]{0,1:T(8,128)(2,1)S(1)}, bf16[512,64]{0,1:T(8,128)(2,1)}, u32[]{:S(2)}) copy-start(bf16[512,64]{0,1:T(8,128)(2,1)} %param.18) | copy-start | bytes 196612
  10.1 4.4 %copy-start.12 = (s32[6,6]{1,0:T(8,128)S(1)}, s32[6,6]{1,0:T(8,128)}, u32[]{:S(2)}) copy-start(s32[6,6]{1,0:T(8,128)} %param.17) | copy-start | bytes 436
  10.1 4.5 %copy-start.13 = (s32[6,122]{1,0:T(8,128)S(1)}, s32[6,122]{1,0:T(8,128)}, u32[]{:S(2)}) copy-start(s32[6,122]{1,0:T(8,128)} %param.16) | copy-start | bytes 8788
  10.1 4.6 %copy-start.5 = (bf16[12,128,4,128]{3,2,1,0:T(4,128)(2,1)S(1)}, bf16[12,128,4,128]{3,2,1,0:T(4,128)(2,1)}, u32[]{:S(2)}) copy-start(bf16[12,128,4,128]{3,2,1,0:T(4,128)(2,1)} %param.13) | copy-start | bytes 4718596
  13.8 204.9 %all-gather.6.cloned.1.call-start = ((), (), s32[]{:S(2)}) async-start(), calls=%async_computation.1 | async-start | bytes 4792320 | tf_op jit(solution)/shard_map/all_gather | solution.py:602
  14.7 2.0 copy-start.6
  16.7 3.1 %copy-start.16 = (s32[6]{0:T(128)S(1)}, s32[6]{0:T(128)}, u32[]{:S(2)}) copy-start(s32[6]{0:T(128)} %param.15) | copy-start | bytes 76
  18.9 91.3 %copy-start.14 = (s32[12]{0:T(128)}, s32[12]{0:T(128)S(1)}, u32[]{:S(2)}) copy-start(s32[12]{0:T(128)S(1)} %fusion.1.sfresh_ref) | copy-start | bytes 148
  19.8 90.4 %copy-start.15 = (s32[12]{0:T(128)}, s32[12]{0:T(128)S(1)}, u32[]{:S(2)}) copy-start(s32[12]{0:T(128)S(1)} %get-tuple-element.17.sreq_ref) | copy-start | bytes 148
  128.9 2.7 %copy-start = (bf16[64,72,640]{2,1,0:T(8,128)(2,1)S(1)}, bf16[64,72,640]{2,1,0:T(8,128)(2,1)}, u32[]{:S(2)}) copy-start(bf16[64,72,640]{2,1,0:T(8,128)(2,1)} %get-tuple-element.6) | copy-start | bytes 17694724
  195.7 0.9 copy-start.3
  218.7 2.3 copy-start.1
  221.0 1.1 copy-start.2
  225.2 0.8 copy-start.4
  226.0 12.9 %copy-start.8 = (bf16[12,128,512]{2,1,0:T(8,128)(2,1)S(1)}, bf16[12,128,512]{2,1,0:T(8,128)(2,1)}, u32[]{:S(2)}) copy-start(bf16[12,128,512]{2,1,0:T(8,128)(2,1)} %get-tuple-element.7) | copy-start | bytes 4718596
  238.9 1.9 copy-start.7
  240.8 1.8 copy-start.11
Sparse Core Ops, SparseCore 0:
  13.9 96.2 all-gather.3
  113.5 85.3 all-gather.5

commit v17 on v16

--- a/solution.py
+++ b/solution.py
@@ -255,7 +255,7 @@
     pl.semaphore_signal(barrier, inc=1, device_id={"core": partner}, device_id_type=pl.DeviceIdType.MESH)
     pl.semaphore_wait(barrier, 1)
 
-    pieces = 4
+    pieces = 8
     size = chunks // pieces
     pending = []
     for p in range(pieces):
@@ -328,9 +328,9 @@
         scratch_shapes=[
             pltpu.VMEM((chips, rows_per, lanes_all), packed.dtype),
             pltpu.VMEM((chips, rows_per, lanes_all), packed.dtype),
-            pltpu.SemaphoreType.DMA((4,)),
-            pltpu.SemaphoreType.DMA((4,)),
-            pltpu.SemaphoreType.DMA((4,)),
+            pltpu.SemaphoreType.DMA((8,)),
+            pltpu.SemaphoreType.DMA((8,)),
+            pltpu.SemaphoreType.DMA((8,)),
         ],
         compiler_params=pltpu.CompilerParams(
             collective_id=0, has_side_effects=True, vmem_limit_bytes=40 * 1024 * 1024
@@ -450,7 +450,7 @@
             device_id_type=pl.DeviceIdType.MESH,
         )
     pl.semaphore_wait(barrier, groups - 1)
-    pieces = 4
+    pieces = 8
     size = chunks // pieces
     pending = []
     for p in range(pieces):
@@ -495,9 +495,9 @@
         out_specs=pl.BlockSpec(memory_space=pltpu.VMEM),
         scratch_shapes=[
             pltpu.VMEM((groups, chunks, rows_per, lanes_all), by_y.dtype),
-            pltpu.SemaphoreType.DMA((4,)),
-            pltpu.SemaphoreType.DMA((4, groups - 1)),
-            pltpu.SemaphoreType.DMA((4, groups - 1)),
+            pltpu.SemaphoreType.DMA((8,)),
+            pltpu.SemaphoreType.DMA((8, groups - 1)),
+            pltpu.SemaphoreType.DMA((8, groups - 1)),
         ],
         compiler_params=pltpu.CompilerParams(
             collective_id=2, has_side_effects=True, vmem_limit_bytes=32 * 1024 * 1024

time: 251 us -> 253 us (level)
  Pallas kernels: 119 us -> 122 us
    pallas_call x1, Pallas kernels: 18.8 us -> 24.2 us  [local_attention(): pl.pallas_call(kernel, out_shape=(jax.ShapeDtypeStruct((chunks, rows_per,...]
    pallas_call x1, Pallas kernels: 16.7 us -> 12.3 us  [pair_merge(): pl.pallas_call(kernel, out_shape=jax.ShapeDtypeStruct((chips, rows_per, l...]
  transfers between devices with their start and end apart: 2 -> 2, of which waited for: 1 -> 1; matrix products, arithmetic and copies ran while one was open for 3% -> 3% of each run, Pallas kernels for 42% -> 43%
where the time goes in v17:
time: 253 us
  Pallas kernels  122 us (48%)
  waiting for transfers between devices  89.6 us (35%)
  local copies, waits for them, and re-layouts  20.2 us (8%)
  between operations  14.3 us (6%)
  other arithmetic  6.8 us (3%)
    all_gather x1, waiting for transfers between devices, per_device(): gathered = lax.all_gather(stacked, PAGES, axis=1, tiled=True)  89.6 us
    pallas_call x1, Pallas kernels, y_exchange(): pl.pallas_call(kernel, out_shape=jax.ShapeDtypeStruct((chunks, rows_per,...  47.5 us
    pallas_call x1, Pallas kernels, local_attention(): pl.pallas_call(kernel, out_shape=(jax.ShapeDtypeStruct((chunks, rows_per,...  24.2 us
    pallas_call x1, Pallas kernels, z_exchange(): pl.pallas_call(kernel, out_shape=jax.ShapeDtypeStruct(merged.shape, merge...  23.9 us
    pallas_call x1, Pallas kernels, pair_merge(): pl.pallas_call(kernel, out_shape=jax.ShapeDtypeStruct((chips, rows_per, l...  12.3 us
    pallas_call x1, Pallas kernels, heads_sum(): pl.pallas_call(kernel, out_shape=jax.ShapeDtypeStruct((rows, block), jnp....  10.8 us
    unnamed x34, local copies, waits for them, and re-layouts  7.87 us
  transfers between devices with their start and end apart: 2, of which 1 were waited for; matrix products, arithmetic and copies ran while one was open for 3% of the time, Pallas kernels for 43%

profile of v17, /device:TPU:4, one launch (start us, length us, event | category | flops | bytes accessed | tf_op | source)
XLA Modules:
  0.0 252.8 jit_solution(14324551329673926511)
XLA Ops:
  7.2 0.0 copy-start.9
  7.2 0.0 all-gather.4.cloned.1.call-start
  7.2 0.9 convert_element_type.40
  8.1 1.0 slice.25
  9.1 0.0 copy-start.10
  9.2 0.9 convert_element_type.43
  10.1 0.0 copy-start.12
  10.1 0.0 copy-start.13
  10.1 0.0 copy-start.5
  10.1 1.1 slice.28
  11.3 0.7 select_reduce_fusion
  12.0 0.2 multiply_cosine_fusion
  12.2 0.3 subtract_convert_fusion.1
  12.6 0.3 pad_maximum_fusion.1
  13.0 0.0 copy-done.9
  13.0 0.7 pad_maximum_fusion
  13.7 0.0 all-gather.4.cloned.1.call-update
  13.8 0.0 all-gather.6.cloned.1.call-start
  13.8 0.0 copy-done.10
  13.8 0.6 pad.4
  14.5 0.0 all-gather.6.cloned.1.call-update
  14.5 0.0 copy-done.12
  14.5 0.1 eq.61
  14.6 0.0 copy-done.13
  14.6 0.1 eq.65
  14.7 0.0 copy-done.5
  14.7 0.0 copy-start.6
  14.7 2.0 reshape.157.kc_ref
  16.7 0.0 copy-done.6
  16.7 2.0 reshape.158.vc_ref
  18.7 0.2 fusion.1.sfresh_ref
  18.9 0.2 compare_reduce_fusion.1
  19.0 0.2 fusion
  19.2 0.5 broadcast_select_fusion
  19.8 0.0 copy-done.16
  19.8 0.1 select_reduce_fusion.1
  19.9 0.2 compare_reduce_fusion
  20.1 0.6 fusion.5.skind_ref
  20.6 89.6 %all-gather.4.cloned.1.call-done.q_ref.kf_ref.vf_ref = bf16[3,4608,512]{2,1,0:T(8,128)(2,1)} async-done(((bf16[3,72,512]{2,1,0:T(8,128)(2,1)}), bf16[3,4608,512]{2,1,0:T(8,128)(2,1)}) %all-gather.4.cloned.1.call-update) | async-done | bytes 14155792 | tf_op jit(solution)/shard_map/all_gather | solution.py:603
  110.2 0.0 copy-done.14
  110.2 0.0 copy-done.15
  110.2 24.2 %shard_map.121 = (bf16[64,72,640]{2,1,0:T(8,128)(2,1)}, bf16[12,128,512]{2,1,0:T(8,128)(2,1)}, bf16[12,128,512]{2,1,0:T(8,128)(2,1)}) custom-call(s32[12]{0:T(128)} %copy-done.15, s32[12]{0:T(128)} %fusion.5.skind_ref, s32[12]{0:T(128)} %get-tuple-element.9.slim_ref, s32[12]{0:T(128)} %copy-done.14, ...), custom_call_target="tpu_custom_call" | custom-call | flops 2415919104 | bytes 16908288 | tf_op jit(solution)/shard_map/pallas_call | solution.py:144
  134.4 2.7 %copy-done = bf16[64,72,640]{2,1,0:T(8,128)(2,1)S(1)} copy-done((bf16[64,72,640]{2,1,0:T(8,128)(2,1)S(1)}, bf16[64,72,640]{2,1,0:T(8,128)(2,1)}, u32[]{:S(2)}) %copy-start) | copy-done | bytes 5898264
  137.1 12.3 %shard_map.122 = bf16[32,72,640]{2,1,0:T(8,128)(2,1)S(1)} custom-call(bf16[32,2,72,640]{3,2,1,0:T(8,128)(2,1)S(1)} %bitcast.6), custom_call_target="tpu_custom_call" | custom-call | flops 8847360 | bytes 8847360 | tf_op jit(solution)/shard_map/pallas_call | solution.py:323
  149.4 47.5 %shard_map.123.src_hbm = bf16[8,72,640]{2,1,0:T(8,128)(2,1)S(1)} custom-call(bf16[8,4,72,640]{3,2,1,0:T(8,128)(2,1)S(1)} %bitcast.5), custom_call_target="tpu_custom_call" | custom-call | flops 5898240 | bytes 5898240 | tf_op jit(solution)/shard_map/pallas_call | solution.py:491
  197.0 0.0 copy-start.3
  197.0 0.9 copy-done.3
  197.8 23.9 %shard_map.124.recv_ref = bf16[8,72,640]{2,1,0:T(8,128)(2,1)} custom-call(bf16[8,72,640]{2,1,0:T(8,128)(2,1)} %copy-done.3), custom_call_target="tpu_custom_call" | custom-call | bytes 2211840 | tf_op jit(solution)/shard_map/pallas_call | solution.py:546
  221.8 0.0 all-gather.6.cloned.1.call-done
  221.8 0.0 copy-start.1
  221.8 2.3 copy-done.1
  224.1 1.1 copy-done.2
  225.2 3.0 %shard_map.125.proj_hbm = bf16[72,4608]{1,0:T(8,128)(2,1)S(1)} custom-call(bf16[8,72,640]{2,1,0:T(8,128)(2,1)S(1)} %copy-done.2, bf16[1,4608,512]{2,1,0:T(8,128)(2,1)S(1)} %bitcast.7), custom_call_target="tpu_custom_call" | custom-call | flops 341213184 | bytes 6119424 | tf_op jit(solution)/shard_map/pallas_call | solution.py:225
  228.3 0.0 copy-start.4
  228.3 0.8 copy-done.4
  229.1 10.8 %shard_map.126 = f32[72,1152]{1,0:T(8,128)} custom-call(bf16[72,4608]{1,0:T(8,128)(2,1)} %copy-done.4), custom_call_target="tpu_custom_call" | custom-call | flops 331776 | bytes 995328 | tf_op jit(solution)/shard_map/pallas_call | solution.py:385
  239.9 1.5 reshape.161
  241.4 0.2 reshape.162
  241.6 0.0 copy-done.8
  241.6 0.0 copy-start.7
  241.6 1.9 reshape.163
  243.5 0.0 copy-done.7
  243.5 1.8 reshape.164
  245.3 0.7 add_convert_fusion
  (15 shorter events, 0.2 us)
Async XLA Ops:
  7.2 5.8 %copy-start.9 = (bf16[72,4,128]{2,1,0:T(4,128)(2,1)S(1)}, bf16[72,4,128]{2,1,0:T(4,128)(2,1)}, u32[]{:S(2)}) copy-start(bf16[72,4,128]{2,1,0:T(4,128)(2,1)} %param.12) | copy-start | bytes 221188
  7.2 103.0 %all-gather.4.cloned.1.call-start = ((), (), s32[]{:S(2)}) async-start(), calls=%async_computation | async-start | bytes 14376960 | tf_op jit(solution)/shard_map/all_gather | solution.py:603
  9.1 4.7 %copy-start.10 = (bf16[512,64]{0,1:T(8,128)(2,1)S(1)}, bf16[512,64]{0,1:T(8,128)(2,1)}, u32[]{:S(2)}) copy-start(bf16[512,64]{0,1:T(8,128)(2,1)} %param.18) | copy-start | bytes 196612
  10.1 4.4 %copy-start.12 = (s32[6,6]{1,0:T(8,128)S(1)}, s32[6,6]{1,0:T(8,128)}, u32[]{:S(2)}) copy-start(s32[6,6]{1,0:T(8,128)} %param.17) | copy-start | bytes 436
  10.1 4.5 %copy-start.13 = (s32[6,122]{1,0:T(8,128)S(1)}, s32[6,122]{1,0:T(8,128)}, u32[]{:S(2)}) copy-start(s32[6,122]{1,0:T(8,128)} %param.16) | copy-start | bytes 8788
  10.1 4.6 %copy-start.5 = (bf16[12,128,4,128]{3,2,1,0:T(4,128)(2,1)S(1)}, bf16[12,128,4,128]{3,2,1,0:T(4,128)(2,1)}, u32[]{:S(2)}) copy-start(bf16[12,128,4,128]{3,2,1,0:T(4,128)(2,1)} %param.13) | copy-start | bytes 4718596
  13.8 208.0 %all-gather.6.cloned.1.call-start = ((), (), s32[]{:S(2)}) async-start(), calls=%async_computation.1 | async-start | bytes 4792320 | tf_op jit(solution)/shard_map/all_gather | solution.py:602
  14.7 2.0 copy-start.6
  16.7 3.1 %copy-start.16 = (s32[6]{0:T(128)S(1)}, s32[6]{0:T(128)}, u32[]{:S(2)}) copy-start(s32[6]{0:T(128)} %param.15) | copy-start | bytes 76
  18.9 91.3 %copy-start.14 = (s32[12]{0:T(128)}, s32[12]{0:T(128)S(1)}, u32[]{:S(2)}) copy-start(s32[12]{0:T(128)S(1)} %fusion.1.sfresh_ref) | copy-start | bytes 148
  19.8 90.4 %copy-start.15 = (s32[12]{0:T(128)}, s32[12]{0:T(128)S(1)}, u32[]{:S(2)}) copy-start(s32[12]{0:T(128)S(1)} %get-tuple-element.17.sreq_ref) | copy-start | bytes 148
  134.4 2.7 %copy-start = (bf16[64,72,640]{2,1,0:T(8,128)(2,1)S(1)}, bf16[64,72,640]{2,1,0:T(8,128)(2,1)}, u32[]{:S(2)}) copy-start(bf16[64,72,640]{2,1,0:T(8,128)(2,1)} %get-tuple-element.6) | copy-start | bytes 17694724
  197.0 0.9 copy-start.3
  221.8 2.3 copy-start.1
  224.1 1.1 copy-start.2
  228.3 0.8 copy-start.4
  229.1 12.5 %copy-start.8 = (bf16[12,128,512]{2,1,0:T(8,128)(2,1)S(1)}, bf16[12,128,512]{2,1,0:T(8,128)(2,1)}, u32[]{:S(2)}) copy-start(bf16[12,128,512]{2,1,0:T(8,128)(2,1)} %get-tuple-element.7) | copy-start | bytes 4718596
  241.6 1.9 copy-start.7
  243.5 1.8 copy-start.11
Sparse Core Ops, SparseCore 0:
  13.9 96.2 all-gather.3
  113.5 85.9 all-gather.5
